TPU v7x, 32 devices: a whole 2x2x4 slice. The times are simulated.
32 devices in a mesh: clips: 2 (over y), frame: 4 (over z), rows: 2 (over x), view: 2 (over core).
Axes of the slice: x: 2, y: 2, z: 4, core: 2. Of those that a mesh axis runs over, the one named last changes fastest.
Arguments:
- feats: bfloat16 [4, 4, 8, 480, 256], P(('clips', 'view'), 'frame', 'rows'), parts along dimension 0, may hold values from -8 to 8
- norm_gains: float32 [3, 256], replicated, may hold values from 0.6 to 10
- cross_qkv: bfloat16 [256, 768], replicated, may hold values from -0.45 to 0.45
- cross_out: bfloat16 [256, 256], replicated, may hold values from -0.375 to 0.375
- time_qkv: bfloat16 [256, 768], replicated, may hold values from -0.45 to 0.45
- time_out: bfloat16 [256, 256], replicated, may hold values from -0.375 to 0.375
- mlp_in: bfloat16 [256, 1024], replicated, may hold values from -0.375 to 0.375
- mlp_out: bfloat16 [1024, 256], replicated, may hold values from -0.1875 to 0.1875
Outputs:
- result: bfloat16 [4, 4, 8, 480, 256], P(('clips', 'view'), 'frame', 'rows'), parts along dimension 0
There are 2 independent parts, one for each index of `clips`. A program takes and returns all parts, laid end to end along the dimension named above; an argument that names none is the same for every part. Nothing has to cross between parts.
All inputs are finite; a program needn't handle non-finite values.
Results may differ from a plain program's by a relative error of at most 0.012.
Values may be sent and summed in bfloat16 or wider, within the bound.
No kernel may reach another device: no remote copies, remote signals or barrier semaphores. Data moves between devices by JAX's collectives and lax.ppermute only.
A program may use at most 64 MiB of HBM per device.

v0:
```python
import jax
import jax.numpy as jnp
from jax import lax
from jax.sharding import PartitionSpec as P

HEADS = 8


EPSILON = 1e-05


def swapped(value, axis, bit):
    return lax.ppermute(value, axis, [(i, i ^ 1 << bit) for i in range(lax.axis_size(axis))])


def layer_norm(values, norm_gain):
    wide = values.astype(jnp.float32)
    centre = jnp.mean(wide, axis=-1, keepdims=True)
    spread = jnp.mean((wide - centre) ** 2, axis=-1, keepdims=True)
    return ((wide - centre) * lax.rsqrt(spread + EPSILON) * norm_gain).astype(jnp.bfloat16)


def row_attend(queries, key_rows, value_rows):
    length, channels = queries.shape
    head_dim = channels // HEADS
    q_heads = queries.reshape(length, HEADS, head_dim)
    k_heads = key_rows.reshape(length, HEADS, head_dim)
    v_heads = value_rows.reshape(length, HEADS, head_dim)
    scores = jnp.einsum(
        "qhd,khd->hqk", q_heads, k_heads, preferred_element_type=jnp.float32
    ) * head_dim ** (-0.5)
    top_score = jnp.max(scores, axis=-1, keepdims=True)
    expo = jnp.exp(scores - top_score)
    shares = (expo / jnp.sum(expo, axis=-1, keepdims=True)).astype(jnp.bfloat16)
    mixed = jnp.einsum("hqk,khd->qhd", shares, v_heads, preferred_element_type=jnp.float32)
    return mixed.reshape(length, channels).astype(jnp.bfloat16)


def time_attend(queries, key_rows, value_rows):
    frames, pixels, channels = queries.shape
    head_dim = channels // HEADS
    q_heads = queries.reshape(frames, pixels, HEADS, head_dim)
    k_heads = key_rows.reshape(frames, pixels, HEADS, head_dim)
    v_heads = value_rows.reshape(frames, pixels, HEADS, head_dim)
    scores = jnp.einsum(
        "fnhd,gnhd->hfgn", q_heads, k_heads, preferred_element_type=jnp.float32
    ) * head_dim ** (-0.5)
    top_score = jnp.max(scores, axis=2, keepdims=True)
    expo = jnp.exp(scores - top_score)
    shares = (expo / jnp.sum(expo, axis=2, keepdims=True)).astype(jnp.bfloat16)
    mixed = jnp.einsum("hfgn,gnhd->fnhd", shares, v_heads, preferred_element_type=jnp.float32)
    return mixed.reshape(frames, pixels, channels).astype(jnp.bfloat16)


def local(feats, norm_gains, cross_qkv, cross_out, time_qkv, time_out, mlp_in, mlp_out):
    rows_here, row_width, channels = (feats.shape[2], feats.shape[3], feats.shape[4])
    frame_count = lax.axis_size("frame")
    tokens_flat = feats[0, 0].reshape(-1, channels)
    pixel_count = tokens_flat.shape[0]
    block_pixels = pixel_count // frame_count
    normed_a = layer_norm(tokens_flat, norm_gains[0])
    projected = jnp.dot(normed_a, cross_qkv, preferred_element_type=jnp.float32).astype(
        jnp.bfloat16
    )
    queries = projected[:, :channels]
    partner = swapped(projected[:, channels:], "view", 0)

    def cross_row(pieces):
        return row_attend(pieces[0], pieces[1][:, :channels], pieces[1][:, channels:])

    cross_mix = lax.map(
        cross_row,
        (
            queries.reshape(rows_here, row_width, channels),
            partner.reshape(rows_here, row_width, 2 * channels),
        ),
    )
    cross_mix = cross_mix.reshape(-1, channels)
    stream_b = (
        tokens_flat.astype(jnp.float32)
        + jnp.dot(cross_mix, cross_out, preferred_element_type=jnp.float32)
    ).astype(jnp.bfloat16)
    normed_b = layer_norm(stream_b, norm_gains[1])
    outgoing = normed_b.reshape(1, frame_count, block_pixels, channels)
    gathered = lax.all_to_all(outgoing, "frame", split_axis=1, concat_axis=0, tiled=True)[:, 0]
    frames, pixels, _ = gathered.shape
    projected_b = jnp.dot(
        gathered.reshape(-1, channels), time_qkv, preferred_element_type=jnp.float32
    ).astype(jnp.bfloat16)
    projected_b = projected_b.reshape(frames, pixels, 3 * channels)
    mixed = time_attend(
        projected_b[..., :channels],
        projected_b[..., channels : 2 * channels],
        projected_b[..., 2 * channels :],
    )
    time_mix = mixed[:, None]
    returned = lax.all_to_all(time_mix, "frame", split_axis=0, concat_axis=1, tiled=True).reshape(
        pixel_count, channels
    )
    stream_c = (
        stream_b.astype(jnp.float32)
        + jnp.dot(returned, time_out, preferred_element_type=jnp.float32)
    ).astype(jnp.bfloat16)
    normed_c = layer_norm(stream_c, norm_gains[2])
    inner_act = jax.nn.gelu(
        jnp.dot(normed_c, mlp_in, preferred_element_type=jnp.float32), approximate=True
    ).astype(jnp.bfloat16)
    result = (
        stream_c.astype(jnp.float32)
        + jnp.dot(inner_act, mlp_out, preferred_element_type=jnp.float32)
    ).astype(jnp.bfloat16)
    return result.reshape(1, 1, rows_here, row_width, channels)


def solution(mesh):
    placed = (P(("clips", "view"), "frame", "rows", None, None), P(), P(), P(), P(), P(), P(), P())
    return jax.shard_map(
        local,
        mesh=mesh,
        in_specs=placed,
        out_specs=P(("clips", "view"), "frame", "rows", None, None),
        check_vma=False,
    )
```

profile of v0, /device:TPU:0, one launch (start us, length us, event | category | flops | bytes accessed | tf_op | source)
XLA Modules:
  0.0 185.9 jit_solution(15738146926986763434)
XLA Ops:
  0.0 1.6 convert_reduce_fusion.2
  1.7 1.8 multiply_reduce_fusion.1
  3.6 0.8 fusion.60
  4.5 1.8 fusion.42
  6.3 0.9 convolution_convert_fusion.2
  7.2 1.4 slice.40
  8.6 0.5 collective-permute-start
  9.1 1.0 slice.41
  10.2 2.8 %collective-permute-done = bf16[1920,512]{1,0:T(8,128)(2,1)S(1)} collective-permute-done((bf16[1920,512]{1,0:T(8,128)(2,1)}, bf16[1920,512]{1,0:T(8,128)(2,1)S(1)}, u32[]{:S(2)}, u32[]{:S(2)}) %collective-permute-start) | collective-permute-done | bytes 1966112 | tf_op jit(solution)/shard_map/ppermute | solution.py:13
  12.9 1.4 copy-done.2
  14.3 48.6 %while.10 = (s32[]{:T(128)}, bf16[4,480,256]{2,1,0:T(8,128)(2,1)}, bf16[4,480,512]{2,1,0:T(8,128)(2,1)}, bf16[4,480,256]{2,1,0:T(8,128)(2,1)}, s32[]{:T(128)}) while((s32[]{:T(128)}, bf16[4,480,256]{2,1,0:T(8,128)(2,1)}, bf16[4,480,512]{2,1,0:T(8,128)(2,1)}, bf16[4,480,256]{2,1,0:T(8,128)(2,1)}, s32[]{:T(128)}) %tuple.39), condition=%wide.region_5.6_spmd, body=%wide.region_2.5_spmd.sunk | while | flops 245268960 | bytes 20675140 | solution.py:71
  14.3 1.2 constant_dynamic-slice_fusion.4
  15.5 0.2 copy.78
  15.7 1.0 constant_dynamic-slice_fusion.5
  16.7 0.1 copy.79
  16.8 4.8 %fusion.91 = (f32[8,480]{1,0:T(8,128)S(1)}, f32[8,480,480]{1,2,0:T(8,128)}) fusion(bf16[480,8,32]{0,2,1:T(8,128)(2,1)S(1)} %bitcast.83, bf16[480,8,32]{0,2,1:T(8,128)(2,1)S(1)} %bitcast.86), kind=kOutput, calls=%fused_computation.73.clone.1 | convolution fusion | flops 123494880 | bytes 7879680 | tf_op jit(solution)/shard_map/while/body/eval_jaxpr/sub | solution.py:33
  21.6 4.0 %fusion.92 = bf16[8,32,480]{2,1,0:T(8,128)(2,1)S(1)} fusion(bf16[480,8,32]{0,2,1:T(8,128)(2,1)S(1)} %bitcast.85, f32[8,480,480]{1,2,0:T(8,128)} %get-tuple-element.101, f32[8,480]{1,0:T(8,128)S(1)} %get-tuple-element.102), kind=kOutput, calls=%fused_computation.7.clone.1 | convolution fusion | flops 121774080 | bytes 7879680 | tf_op jit(solution)/shard_map/while/body/eval_jaxpr/hqk,khd->qhd/dot_general | solution.py:35
  25.6 0.1 copy.80
  25.8 0.7 constant_dynamic-update-slice_fusion.2
  26.5 1.1 constant_dynamic-slice_fusion.4
  27.6 0.2 copy.78
  27.8 1.0 constant_dynamic-slice_fusion.5
  28.8 0.1 copy.79
  28.9 4.8 %fusion.91 = (f32[8,480]{1,0:T(8,128)S(1)}, f32[8,480,480]{1,2,0:T(8,128)}) fusion(bf16[480,8,32]{0,2,1:T(8,128)(2,1)S(1)} %bitcast.83, bf16[480,8,32]{0,2,1:T(8,128)(2,1)S(1)} %bitcast.86), kind=kOutput, calls=%fused_computation.73.clone.1 | convolution fusion | flops 123494880 | bytes 7879680 | tf_op jit(solution)/shard_map/while/body/eval_jaxpr/sub | solution.py:33
  33.7 4.0 %fusion.92 = bf16[8,32,480]{2,1,0:T(8,128)(2,1)S(1)} fusion(bf16[480,8,32]{0,2,1:T(8,128)(2,1)S(1)} %bitcast.85, f32[8,480,480]{1,2,0:T(8,128)} %get-tuple-element.101, f32[8,480]{1,0:T(8,128)S(1)} %get-tuple-element.102), kind=kOutput, calls=%fused_computation.7.clone.1 | convolution fusion | flops 121774080 | bytes 7879680 | tf_op jit(solution)/shard_map/while/body/eval_jaxpr/hqk,khd->qhd/dot_general | solution.py:35
  37.8 0.1 copy.80
  37.9 0.7 constant_dynamic-update-slice_fusion.2
  38.6 1.1 constant_dynamic-slice_fusion.4
  39.7 0.2 copy.78
  39.9 1.0 constant_dynamic-slice_fusion.5
  40.9 0.1 copy.79
  41.1 4.8 %fusion.91 = (f32[8,480]{1,0:T(8,128)S(1)}, f32[8,480,480]{1,2,0:T(8,128)}) fusion(bf16[480,8,32]{0,2,1:T(8,128)(2,1)S(1)} %bitcast.83, bf16[480,8,32]{0,2,1:T(8,128)(2,1)S(1)} %bitcast.86), kind=kOutput, calls=%fused_computation.73.clone.1 | convolution fusion | flops 123494880 | bytes 7879680 | tf_op jit(solution)/shard_map/while/body/eval_jaxpr/sub | solution.py:33
  45.9 4.0 %fusion.92 = bf16[8,32,480]{2,1,0:T(8,128)(2,1)S(1)} fusion(bf16[480,8,32]{0,2,1:T(8,128)(2,1)S(1)} %bitcast.85, f32[8,480,480]{1,2,0:T(8,128)} %get-tuple-element.101, f32[8,480]{1,0:T(8,128)S(1)} %get-tuple-element.102), kind=kOutput, calls=%fused_computation.7.clone.1 | convolution fusion | flops 121774080 | bytes 7879680 | tf_op jit(solution)/shard_map/while/body/eval_jaxpr/hqk,khd->qhd/dot_general | solution.py:35
  49.9 0.1 copy.80
  50.0 0.7 constant_dynamic-update-slice_fusion.2
  50.7 1.1 constant_dynamic-slice_fusion.4
  51.8 0.2 copy.78
  52.1 1.0 constant_dynamic-slice_fusion.5
  53.2 4.8 %fusion.91 = (f32[8,480]{1,0:T(8,128)S(1)}, f32[8,480,480]{1,2,0:T(8,128)}) fusion(bf16[480,8,32]{0,2,1:T(8,128)(2,1)S(1)} %bitcast.83, bf16[480,8,32]{0,2,1:T(8,128)(2,1)S(1)} %bitcast.86), kind=kOutput, calls=%fused_computation.73.clone.1 | convolution fusion | flops 123494880 | bytes 7879680 | tf_op jit(solution)/shard_map/while/body/eval_jaxpr/sub | solution.py:33
  58.0 4.0 %fusion.92 = bf16[8,32,480]{2,1,0:T(8,128)(2,1)S(1)} fusion(bf16[480,8,32]{0,2,1:T(8,128)(2,1)S(1)} %bitcast.85, f32[8,480,480]{1,2,0:T(8,128)} %get-tuple-element.101, f32[8,480]{1,0:T(8,128)S(1)} %get-tuple-element.102), kind=kOutput, calls=%fused_computation.7.clone.1 | convolution fusion | flops 121774080 | bytes 7879680 | tf_op jit(solution)/shard_map/while/body/eval_jaxpr/hqk,khd->qhd/dot_general | solution.py:35
  62.0 0.1 copy.80
  62.1 0.7 constant_dynamic-update-slice_fusion.2
  62.9 1.8 convert_reduce_fusion.1
  64.7 0.6 fusion.37
  65.3 0.6 fusion.39
  65.9 30.7 %all_to_all.8 = bf16[1,4,480,256]{3,2,0,1:T(8,128)(2,1)S(1)} all-to-all(bf16[1,4,480,256]{3,2,0,1:T(8,128)(2,1)S(1)} %bitcast.92), channel_id=1, replica_groups=mesh['clips'=2,'frame'=4,'rows'=2,'view'=2] {'frame'}, dimensions={1} | all-to-all | bytes 1966080 | tf_op jit(solution)/shard_map/all_to_all | solution.py:85
  96.6 0.9 convolution_convert_fusion.1
  97.5 1.5 fusion.59
  99.0 1.5 copy.73
  100.5 4.6 %copy.60 = bf16[4,480,8,32]{3,0,1,2:T(4,128)(2,1)} copy(bf16[4,480,8,32]{1,3,2,0:T(8,128)(2,1)S(1)} %bitcast.88) | data formatting | bytes 1966080 | tf_op jit(solution)/shard_map/reshape | solution.py:43
  105.0 1.5 copy.74
  106.5 4.5 %copy.61 = bf16[4,480,8,32]{3,0,1,2:T(4,128)(2,1)} copy(bf16[4,480,8,32]{1,3,2,0:T(8,128)(2,1)S(1)} %bitcast.89) | data formatting | bytes 1966080 | tf_op jit(solution)/shard_map/reshape | solution.py:42
  111.0 8.4 %fusion.61 = f32[8,480,4,4]{3,2,1,0:T(4,128)} fusion(bf16[4,480,8,32]{3,0,1,2:T(4,128)(2,1)} %copy.60, bf16[4,480,8,32]{3,0,1,2:T(4,128)(2,1)} %copy.61), kind=kOutput, calls=%fused_computation.76 | convolution fusion | flops 3932160 | bytes 2211840 | tf_op jit(solution)/shard_map/fnhd,gnhd->hfgn/dot_general | solution.py:45
  119.5 5.1 %copy.62 = f32[8,480,4,4]{1,0,2,3:T(8,128)S(1)} copy(f32[8,480,4,4]{3,2,1,0:T(4,128)} %fusion.61) | data formatting | bytes 491520 | tf_op jit(solution)/shard_map/fnhd,gnhd->hfgn/dot_general | solution.py:45
  124.7 7.4 %copy.64 = bf16[8,4,4,480]{2,1,0,3:T(4,128)(2,1)} copy(bf16[8,4,4,480]{3,0,2,1:T(8,128)(2,1)S(1)} %divide_convert_fusion.4) | data formatting | bytes 245760 | tf_op jit(solution)/shard_map/convert_element_type | solution.py:50
  132.1 0.5 copy.72
  132.7 4.7 %copy.63 = bf16[4,480,8,32]{3,0,2,1:T(4,128)(2,1)} copy(bf16[4,480,8,32]{1,3,2,0:T(8,128)(2,1)S(1)} %bitcast.90) | data formatting | bytes 1966080 | tf_op jit(solution)/shard_map/reshape | solution.py:44
  137.4 9.5 %fusion.20 = bf16[4,480,8,32]{3,0,2,1:T(4,128)(2,1)} fusion(bf16[4,480,8,32]{3,0,2,1:T(4,128)(2,1)} %copy.63, bf16[8,4,4,480]{2,1,0,3:T(4,128)(2,1)} %copy.64), kind=kOutput, calls=%fused_computation.24 | convolution fusion | flops 4423680 | bytes 2088960 | tf_op jit(solution)/shard_map/hfgn,gnhd->fnhd/dot_general | solution.py:51
  146.9 5.4 %copy.65 = bf16[4,480,8,32]{1,3,2,0:T(8,128)(2,1)S(1)} copy(bf16[4,480,8,32]{3,0,2,1:T(4,128)(2,1)} %fusion.20) | data formatting | bytes 1966080 | tf_op jit(solution)/shard_map/convert_element_type | solution.py:52
  152.3 0.5 copy.66
  152.9 26.7 %all_to_all.9 = bf16[4,1,480,256]{3,2,1,0:T(8,128)(2,1)S(1)} all-to-all(bf16[4,1,480,256]{3,2,1,0:T(8,128)(2,1)S(1)} %copy.66), channel_id=1, replica_groups=mesh['clips'=2,'frame'=4,'rows'=2,'view'=2] {'frame'}, dimensions={0} | all-to-all | bytes 1966080 | tf_op jit(solution)/shard_map/all_to_all | solution.py:97
  179.6 1.5 convert_reduce_fusion
  181.1 0.6 fusion.34
  181.7 4.2 %fusion.27 = bf16[1920,256]{1,0:T(8,128)(2,1)} fusion(bf16[1024,256]{1,0:T(8,128)(2,1)S(1)} %copy-done, bf16[256,1024]{1,0:T(8,128)(2,1)S(1)} %copy-done.6, bf16[1920,256]{1,0:T(8,128)(2,1)S(1)} %get-tuple-element.69, f32[256]{0:T(256)S(1)} %bitcast.98, f32[1920]{0:T(1024)S(1)} %add_rsqrt_fusion, f32[1920]{0:T(1024)S(1)} %broadcast_multiply_fusion), kind=kOutput, calls=%fused_computation.37 | convolution fusion | flops 2034892800 | bytes 3031040 | tf_op jit(solution)/shard_map/dot_general | solution.py:110
  (30 shorter events, 0.7 us)
Async XLA Ops:
  0.0 181.7 %copy-start = (bf16[1024,256]{1,0:T(8,128)(2,1)S(1)}, bf16[1024,256]{1,0:T(8,128)(2,1)}, u32[]{:S(2)}) copy-start(bf16[1024,256]{1,0:T(8,128)(2,1)} %param.17) | copy-start | bytes 1572868
  0.0 6.2 %copy-start.3 = (bf16[256,768]{1,0:T(8,128)(2,1)S(1)}, bf16[256,768]{1,0:T(8,128)(2,1)}, u32[]{:S(2)}) copy-start(bf16[256,768]{1,0:T(8,128)(2,1)} %param.12) | copy-start | bytes 1179652
  8.6 4.3 %collective-permute-start = (bf16[1920,512]{1,0:T(8,128)(2,1)}, bf16[1920,512]{1,0:T(8,128)(2,1)S(1)}, u32[]{:S(2)}, u32[]{:S(2)}) collective-permute-start(bf16[1920,512]{1,0:T(8,128)(2,1)} %slice.40), channel_id=1, source_target_pairs={{0,1},{1,0},{2,3},{3,2},{4,5},{5,4},{6,7},{7,6},{8,9},{9,8},{10,11... | collective-permute-start | bytes 5898248 | tf_op jit(solution)/shard_map/ppermute | solution.py:13
  12.9 1.4 copy-start.2
  14.3 48.6 %copy-start.1 = (bf16[1,1,4,480,256]{4,3,2,1,0:T(8,128)(2,1)S(1)}, bf16[1,1,4,480,256]{4,3,2,1,0:T(8,128)(2,1)}, u32[]{:S(2)}) copy-start(bf16[1,1,4,480,256]{4,3,2,1,0:T(8,128)(2,1)} %param.10) | copy-start | bytes 2949124
  14.3 48.6 %copy-start.5 = (bf16[256,256]{1,0:T(8,128)(2,1)S(1)}, bf16[256,256]{1,0:T(8,128)(2,1)}, u32[]{:S(2)}) copy-start(bf16[256,256]{1,0:T(8,128)(2,1)} %param.13) | copy-start | bytes 393220
  62.9 33.7 %copy-start.4 = (bf16[256,768]{1,0:T(8,128)(2,1)S(1)}, bf16[256,768]{1,0:T(8,128)(2,1)}, u32[]{:S(2)}) copy-start(bf16[256,768]{1,0:T(8,128)(2,1)} %param.14) | copy-start | bytes 1179652
  179.6 2.1 %copy-start.6 = (bf16[256,1024]{1,0:T(8,128)(2,1)S(1)}, bf16[256,1024]{1,0:T(8,128)(2,1)}, u32[]{:S(2)}) copy-start(bf16[256,1024]{1,0:T(8,128)(2,1)} %param.16) | copy-start | bytes 1572868
where the time goes:
time: 187 us; the launch traced here: 186 us
  matrix products  62.5 us (33%)
  blocking collectives  57.4 us (31%)
  local copies, waits for them, and re-layouts  55.2 us (30%)
  other arithmetic  7.24 us (4%)
  waiting for transfers between devices  2.78 us (1%)
    all_to_all x1, blocking collectives, local(): lax.all_to_all(outgoing, 'frame', split_axis=1, concat_axis=0, tiled=True)  30.7 us
    all_to_all x1, blocking collectives, local(): lax.all_to_all(time_mix, 'frame', split_axis=0, concat_axis=1, tiled=True)  26.7 us
    sub x4, matrix products, row_attend(): expo = jnp.exp(scores - top_score)  19.1 us
    dot_general x4, matrix products, row_attend(): jnp.einsum('hqk,khd->qhd', shares, v_heads, preferred_element_type=jnp.fl...  16.1 us
    dynamic_slice x16, local copies, waits for them, and re-layouts, local(): lax.map(cross_row, (queries.reshape(rows_here, row_width, channels), part...  9.61 us
    dot_general x1, matrix products, time_attend(): jnp.einsum('hfgn,gnhd->fnhd', shares, v_heads, preferred_element_type=jnp...  9.5 us
    dot_general x1, matrix products, time_attend(): jnp.einsum('fnhd,gnhd->hfgn', q_heads, k_heads, preferred_element_type=jn...  8.41 us
    convert_element_type x1, local copies, waits for them, and re-layouts, time_attend(): shares = (expo / jnp.sum(expo, axis=2, keepdims=True)).astype(jnp.bfloat16)  7.42 us
  transfers between devices with their start and end apart: 1, of which 1 were waited for; matrix products, arithmetic and copies ran while one was open for 1% of the time, Pallas kernels for 0%

commit v1 on v0

--- a/solution.py
+++ b/solution.py
@@ -1,7 +1,13 @@
+import functools
+
 import jax
 import jax.numpy as jnp
+import numpy as np
 from jax import lax
+from jax.experimental import pallas as pl
+from jax.experimental.pallas import tpu as pltpu
 from jax.sharding import PartitionSpec as P
+
 
 HEADS = 8
 
@@ -52,7 +58,7 @@
     return mixed.reshape(frames, pixels, channels).astype(jnp.bfloat16)
 
 
-def local(feats, norm_gains, cross_qkv, cross_out, time_qkv, time_out, mlp_in, mlp_out):
+def local_pixels(feats, norm_gains, cross_qkv, cross_out, time_qkv, time_out, mlp_in, mlp_out):
     rows_here, row_width, channels = (feats.shape[2], feats.shape[3], feats.shape[4])
     frame_count = lax.axis_size("frame")
     tokens_flat = feats[0, 0].reshape(-1, channels)
@@ -112,6 +118,207 @@
     return result.reshape(1, 1, rows_here, row_width, channels)
 
 
+LOG2E = 1.4426950408889634
+
+
+def dot(a, b):
+    return jnp.dot(a, b, preferred_element_type=jnp.float32)
+
+
+def dot_dims(a, b, left, right):
+    return lax.dot_general(
+        a, b, (((left,), (right,)), ((), ())), preferred_element_type=jnp.float32
+    )
+
+
+def row_kernel(own_ref, other_ref, gains_ref, qkv_ref, out_ref, time_ref, stream_ref, proj_ref, mix_ref):
+    channels = own_ref.shape[1]
+    length = own_ref.shape[0]
+    head_dim = channels // HEADS
+    normed = layer_norm(own_ref[...], gains_ref[0:1, :])
+    queries = (dot(normed, qkv_ref[:, :channels]) * (head_dim**-0.5 * LOG2E)).astype(jnp.bfloat16)
+    other = layer_norm(other_ref[...], gains_ref[0:1, :])
+    keys = dot(other, qkv_ref[:, channels : 2 * channels]).astype(jnp.bfloat16)
+    values = dot(other, qkv_ref[:, 2 * channels :]).T.astype(jnp.bfloat16)
+    lane = lax.broadcasted_iota(jnp.int32, (1, 128), 1)
+    ones = jnp.ones((16, length), jnp.bfloat16)
+    for head in range(HEADS):
+        tile = head * head_dim // 128
+        low = head * head_dim - tile * 128
+        held = (lane >= low) & (lane < low + head_dim)
+        columns = slice(tile * 128, (tile + 1) * 128)
+        here = slice(head * head_dim, (head + 1) * head_dim)
+        key_part = jnp.where(held, keys[:, columns], jnp.zeros((), jnp.bfloat16))
+        scores = dot_dims(key_part, queries[:, columns], 1, 1)
+        expo = jnp.exp2(scores - jnp.max(scores, axis=0, keepdims=True)).astype(jnp.bfloat16)
+        mixed = dot(jnp.concatenate([values[here, :], ones], axis=0), expo)
+        mix_ref[here, :] = (mixed[:head_dim] / mixed[head_dim : head_dim + 1]).astype(jnp.bfloat16)
+    stream = own_ref[...].astype(jnp.float32) + dot_dims(mix_ref[...], out_ref[...], 0, 0)
+    stream = stream.astype(jnp.bfloat16)
+    stream_ref[...] = stream
+    normed_b = layer_norm(stream, gains_ref[1:2, :])
+    proj_ref[...] = dot(normed_b, time_ref[...]).astype(jnp.bfloat16)
+
+
+def time_kernel(frames, *refs):
+    projs, streams = refs[:frames], refs[frames : 2 * frames]
+    gather_ref, spread_ref, out_ref = refs[2 * frames : 2 * frames + 3]
+    results = refs[2 * frames + 3 :]
+    channels = streams[0].shape[1]
+    head_dim = channels // HEADS
+    lanes = frames * HEADS
+    scores = None
+    for f in range(frames):
+        query = projs[f][:, :channels].astype(jnp.float32)
+        for g in range(frames):
+            product = query * projs[g][:, channels : 2 * channels].astype(jnp.float32)
+            high = product.astype(jnp.bfloat16)
+            low = (product - high.astype(jnp.float32)).astype(jnp.bfloat16)
+            part = dot(high, gather_ref[f * frames + g]) + dot(low, gather_ref[f * frames + g])
+            scores = part if scores is None else scores + part
+    scores = scores * (head_dim**-0.5 * LOG2E)
+
+    def over_frames(op, value):
+        step = 1
+        while step < frames:
+            value = op(value, pltpu.roll(value, step * lanes, 1))
+            step *= 2
+        return value
+
+    expo = jnp.exp2(scores - over_frames(jnp.maximum, scores))
+    shares = (expo / over_frames(jnp.add, expo)).astype(jnp.bfloat16)
+    for f in range(frames):
+        mixed = None
+        for g in range(frames):
+            part = dot(shares, spread_ref[f * frames + g]) * projs[g][:, 2 * channels :].astype(
+                jnp.float32
+            )
+            mixed = part if mixed is None else mixed + part
+        stream = streams[f][...].astype(jnp.float32) + dot(
+            mixed.astype(jnp.bfloat16), out_ref[...]
+        )
+        results[f][...] = stream.astype(jnp.bfloat16)
+
+
+def mlp_kernel(stream_ref, gains_ref, in_ref, out_ref, result_ref):
+    stream = stream_ref[...]
+    normed = layer_norm(stream, gains_ref[2:3, :])
+    inner = jax.nn.gelu(dot(normed, in_ref[...]), approximate=True).astype(jnp.bfloat16)
+    result_ref[...] = (stream.astype(jnp.float32) + dot(inner, out_ref[...])).astype(jnp.bfloat16)
+
+
+PARAMS = pltpu.CompilerParams(vmem_limit_bytes=20 * 1024 * 1024)
+
+
+def attend_row(own, other, norm_gains, cross_qkv, cross_out, time_qkv):
+    length, channels = own.shape
+    return pl.pallas_call(
+        row_kernel,
+        out_shape=(
+            jax.ShapeDtypeStruct((length, channels), jnp.bfloat16),
+            jax.ShapeDtypeStruct((length, 3 * channels), jnp.bfloat16),
+        ),
+        scratch_shapes=[pltpu.VMEM((channels, length), jnp.bfloat16)],
+        compiler_params=PARAMS,
+        cost_estimate=pl.CostEstimate(
+            flops=2 * length * channels * 7 * channels + 4 * length * length * channels * HEADS,
+            bytes_accessed=2 * (6 * length * channels + 7 * channels * channels),
+            transcendentals=HEADS * length * length,
+        ),
+        name="attend_row",
+    )(own, other, norm_gains, cross_qkv, cross_out, time_qkv)
+
+
+def attend_time(projs, streams, time_out):
+    frames = len(projs)
+    length, channels = streams[0].shape
+    head_dim = channels // HEADS
+    lanes = frames * frames * HEADS
+    gather = np.zeros((frames * frames, channels, lanes), np.float32)
+    for f in range(frames):
+        for g in range(frames):
+            for c in range(channels):
+                gather[f * frames + g, c, (g * frames + f) * HEADS + c // head_dim] = 1
+    spread = np.swapaxes(gather, 1, 2)
+    tile = length // 2
+    once = lambda shape: pl.BlockSpec(shape, lambda i: (0,) * len(shape))
+    return pl.pallas_call(
+        functools.partial(time_kernel, frames),
+        grid=(2,),
+        in_specs=[pl.BlockSpec((tile, 3 * channels), lambda i: (i, 0))] * frames
+        + [pl.BlockSpec((tile, channels), lambda i: (i, 0))] * frames
+        + [once(gather.shape), once(spread.shape), once(time_out.shape)],
+        out_specs=[pl.BlockSpec((tile, channels), lambda i: (i, 0))] * frames,
+        out_shape=[jax.ShapeDtypeStruct((length, channels), jnp.bfloat16)] * frames,
+        compiler_params=PARAMS,
+        cost_estimate=pl.CostEstimate(
+            flops=2 * frames * length * channels * channels,
+            bytes_accessed=2 * 5 * frames * length * channels,
+            transcendentals=frames * frames * length * HEADS,
+        ),
+        name="attend_time",
+    )(*projs, *streams, jnp.asarray(gather, jnp.bfloat16), jnp.asarray(spread, jnp.bfloat16), time_out)
+
+
+def mlp_row(stream, norm_gains, mlp_in, mlp_out):
+    length, channels = stream.shape
+    hidden = mlp_in.shape[1]
+    return pl.pallas_call(
+        mlp_kernel,
+        out_shape=jax.ShapeDtypeStruct((length, channels), jnp.bfloat16),
+        compiler_params=PARAMS,
+        cost_estimate=pl.CostEstimate(
+            flops=4 * length * channels * hidden,
+            bytes_accessed=4 * (length * channels + channels * hidden),
+            transcendentals=length * hidden,
+        ),
+        name="mlp_row",
+    )(stream, norm_gains, mlp_in, mlp_out)
+
+
+def frame_swapped(value, distance):
+    count = lax.axis_size("frame")
+    return lax.ppermute(value, "frame", [(i, i ^ distance) for i in range(count)])
+
+
+def local_rows(feats, norm_gains, cross_qkv, cross_out, time_qkv, time_out, mlp_in, mlp_out):
+    rows_here, _, _ = feats.shape[2:]
+    here = lax.axis_index("frame")
+    rows = feats[0, 0]
+    order = sorted(range(1, rows_here), key=lambda d: (d != 1, d))
+    own_rows = {0: lax.dynamic_index_in_dim(rows, here, 0, keepdims=False)}
+    for d in order:
+        piece = lax.dynamic_index_in_dim(rows, here ^ d, 0, keepdims=False)
+        own_rows[d] = frame_swapped(piece, d)
+    streams, projs = {}, {}
+    for d in [0] + order:
+        own = own_rows[d]
+        if d:
+            own, streams[last] = lax.optimization_barrier((own, streams[last]))
+        other = swapped(own, "view", 0)
+        streams[d], projs[d] = attend_row(own, other, norm_gains, cross_qkv, cross_out, time_qkv)
+        last = d
+    frames = list(range(rows_here))
+    mixed = attend_time([projs[d] for d in frames], [streams[d] for d in frames], time_out)
+    result = jnp.zeros(rows.shape, jnp.bfloat16)
+    arrived = []
+    for d in order[1:] + order[:1]:
+        done = mlp_row(mixed[d], norm_gains, mlp_in, mlp_out)
+        arrived.append((here ^ d, frame_swapped(done, d)))
+    result = lax.dynamic_update_index_in_dim(
+        result, mlp_row(mixed[0], norm_gains, mlp_in, mlp_out), here, 0
+    )
+    for row, value in arrived:
+        result = lax.dynamic_update_index_in_dim(result, value, row, 0)
+    return result[None, None]
+
+
+def local(feats, *rest):
+    rows_here = feats.shape[2]
+    whole = rows_here == lax.axis_size("frame") and rows_here & (rows_here - 1) == 0
+    return (local_rows if whole else local_pixels)(feats, *rest)
+
+
 def solution(mesh):
     placed = (P(("clips", "view"), "frame", "rows", None, None), P(), P(), P(), P(), P(), P(), P())
     return jax.shard_map(

time: 187 us -> 74.6 us (0.40)
  matrix products: 62.5 us -> 0 us
  blocking collectives: 57.4 us -> 0 us
  local copies, waits for them, and re-layouts: 55.2 us -> 3.44 us
  Pallas kernels: 0 us -> 28.3 us
  waiting for transfers between devices: 2.78 us -> 26 us
  starting transfers between devices: 0.49 us -> 16.2 us
  other arithmetic: 7.24 us -> 0 us
    all_to_all x2 -> x0, blocking collectives: 57.4 us -> none  [the longest x1 30.7 us: local(): lax.all_to_all(outgoing, 'frame', split_axis=1, concat_axis=0, tiled=True)]
    dot_general x11 -> x0, matrix products: 43.3 us -> none  [the longest x4 16.1 us: row_attend(): jnp.einsum('hqk,khd->qhd', shares, v_heads, preferred_element_type=jnp.fl...]
    pallas_call x0 -> x8, Pallas kernels: none -> 28.3 us  [the longest x4 19.6 us: attend_row(): pl.pallas_call(row_kernel, out_shape=(jax.ShapeDtypeStruct((length, chann...]
    ppermute x0 -> x6, waiting for transfers between devices: none -> 24.5 us  [frame_swapped(): lax.ppermute(value, 'frame', [(i, i ^ distance) for i in range(count)])]
    sub x4 -> x0, matrix products: 19.1 us -> none  [row_attend(): expo = jnp.exp(scores - top_score)]
    ppermute x0 -> x6, starting transfers between devices: none -> 15.7 us  [frame_swapped(): lax.ppermute(value, 'frame', [(i, i ^ distance) for i in range(count)])]
    reshape x3 -> x0, local copies, waits for them, and re-layouts: 13.8 us -> none  [the longest x1 4.71 us: time_attend(): v_heads = value_rows.reshape(frames, pixels, HEADS, head_dim)]
    convert_element_type x3 -> x0, local copies, waits for them, and re-layouts: 13.4 us -> none  [the longest x1 7.42 us: time_attend(): shares = (expo / jnp.sum(expo, axis=2, keepdims=True)).astype(jnp.bfloat16)]
  transfers between devices with their start and end apart: 1 -> 10, of which waited for: 1 -> 6; matrix products, arithmetic and copies ran while one was open for 1% -> 2% of each run, Pallas kernels for 0% -> 23%
where the time goes in v1:
time: 74.6 us; the launch traced here: 74.2 us
  Pallas kernels  28.3 us (38%)
  waiting for transfers between devices  26 us (35%)
  starting transfers between devices  16.2 us (22%)
  local copies, waits for them, and re-layouts  3.44 us (5%)
    ppermute x6, waiting for transfers between devices, frame_swapped(): lax.ppermute(value, 'frame', [(i, i ^ distance) for i in range(count)])  24.5 us
    pallas_call x4, Pallas kernels, attend_row(): pl.pallas_call(row_kernel, out_shape=(jax.ShapeDtypeStruct((length, chann...  19.6 us
    ppermute x6, starting transfers between devices, frame_swapped(): lax.ppermute(value, 'frame', [(i, i ^ distance) for i in range(count)])  15.7 us
    pallas_call x1, Pallas kernels, attend_time(): pl.pallas_call(functools.partial(time_kernel, frames), grid=(2,), in_spec...  5.33 us
    pallas_call x3, Pallas kernels, mlp_row(): pl.pallas_call(mlp_kernel, out_shape=jax.ShapeDtypeStruct((length, channe...  3.37 us
    ppermute x4, waiting for transfers between devices, swapped(): lax.ppermute(value, axis, [(i, i ^ 1 << bit) for i in range(lax.axis_size...  1.51 us
  transfers between devices with their start and end apart: 10, of which 6 were waited for; matrix products, arithmetic and copies ran while one was open for 2% of the time, Pallas kernels for 23%

profile of v1, /device:TPU:0, one launch (start us, length us, event | category | flops | bytes accessed | tf_op | source)
XLA Modules:
  0.0 74.2 jit_solution(7650960349042155488)
XLA Ops:
  0.0 0.0 copy-start.5
  0.0 0.0 copy-start.6
  0.0 0.0 copy-start.7
  0.0 0.0 copy-start.8
  0.0 1.4 %dynamic-slice_bitcast_fusion = (bf16[480,256]{1,0:T(8,128)(2,1)S(1)}, bf16[480,256]{1,0:T(8,128)(2,1)S(1)}, bf16[480,256]{1,0:T(8,128)(2,1)S(1)}, bf16[480,256]{1,0:T(8,128)(2,1)S(1)}) fusion(bf16[1,1,4,480,256]{4,3,2,1,0:T(8,128)(2,1)} %param.10, s32[]{:T(128)S(6)} %select_n.21, s32[]{:T(128)S(6)} %select_n.19, s32[]{:T(128)S(6)} %select_n.18, s32[]{:T(128)S(6)} %select_n.20), kind=kLoop, calls=%fused_computation.4 | loop fusion | bytes 1966096 | tf_op jit(solution)/shard_map/jit(dynamic_index_in_dim)/squeeze | solution.py:291
  1.5 0.6 collective-permute-start
  2.0 2.6 %collective-permute-start.1 = (bf16[480,256]{1,0:T(8,128)(2,1)S(1)}, bf16[480,256]{1,0:T(8,128)(2,1)S(1)}, u32[]{:S(2)}, u32[]{:S(2)}) collective-permute-start(bf16[480,256]{1,0:T(8,128)(2,1)S(1)} %get-tuple-element.42), channel_id=1, source_target_pairs={{0,4},{4,0},{8,12},{12,8},{1,5},{5,1},{9,13},{13,9},{2,6},{6,2},{1... | collective-permute-start | bytes 737288 | tf_op jit(solution)/shard_map/ppermute | solution.py:281
  4.7 0.0 collective-permute-done.other_ref
  4.7 0.0 copy-done.5
  4.7 0.0 copy-done.6
  4.7 0.0 copy-done.7
  4.7 0.0 copy-done.8
  4.7 4.8 %attend_row.4 = (bf16[480,256]{1,0:T(8,128)(2,1)S(1)}, bf16[480,768]{1,0:T(8,128)(2,1)S(1)}) custom-call(bf16[480,256]{1,0:T(8,128)(2,1)S(1)} %get-tuple-element.43.own_ref, bf16[480,256]{1,0:T(8,128)(2,1)S(1)} %collective-permute-done.other_ref, f32[3,256]{1,0:T(4,128)S(1)} %copy-done.8, bf16[256,768]{1,0:T(8,128)(2,1)S(1)} %copy-done.5, ...), custom_call_target="tpu_custom_call" | custom-call | flops 2327838720 | bytes 2392064 | tf_op jit(solution)/shard_map/attend_row/pallas_call | solution.py:215
  9.5 1.7 %collective-permute-done.1.own_ref = bf16[480,256]{1,0:T(8,128)(2,1)S(1)} collective-permute-done((bf16[480,256]{1,0:T(8,128)(2,1)S(1)}, bf16[480,256]{1,0:T(8,128)(2,1)S(1)}, u32[]{:S(2)}, u32[]{:S(2)}) %collective-permute-start.1) | collective-permute-done | bytes 245792 | tf_op jit(solution)/shard_map/ppermute | solution.py:281
  11.2 0.0 collective-permute-start.2
  11.2 2.8 %collective-permute-start.3 = (bf16[480,256]{1,0:T(8,128)(2,1)S(1)}, bf16[480,256]{1,0:T(8,128)(2,1)S(1)}, u32[]{:S(2)}, u32[]{:S(2)}) collective-permute-start(bf16[480,256]{1,0:T(8,128)(2,1)S(1)} %get-tuple-element.44), channel_id=1, source_target_pairs={{0,8},{4,12},{8,0},{12,4},{1,9},{5,13},{9,1},{13,5},{2,10},{6,14},... | collective-permute-start | bytes 737288 | tf_op jit(solution)/shard_map/ppermute | solution.py:281
  14.0 0.0 collective-permute-done.2.other_ref
  14.0 4.8 %attend_row.5 = (bf16[480,256]{1,0:T(8,128)(2,1)S(1)}, bf16[480,768]{1,0:T(8,128)(2,1)S(1)}) custom-call(bf16[480,256]{1,0:T(8,128)(2,1)S(1)} %collective-permute-done.1.own_ref, bf16[480,256]{1,0:T(8,128)(2,1)S(1)} %collective-permute-done.2.other_ref, f32[3,256]{1,0:T(4,128)S(1)} %copy-done.8, bf16[256,768]{1,0:T(8,128)(2,1)S(1)} %copy-done.5, ...), custom_call_target="tpu_custom_call" | custom-call | flops 2327838720 | bytes 2392064 | tf_op jit(solution)/shard_map/attend_row/pallas_call | solution.py:215
  18.8 7.0 %collective-permute-done.3.own_ref = bf16[480,256]{1,0:T(8,128)(2,1)S(1)} collective-permute-done((bf16[480,256]{1,0:T(8,128)(2,1)S(1)}, bf16[480,256]{1,0:T(8,128)(2,1)S(1)}, u32[]{:S(2)}, u32[]{:S(2)}) %collective-permute-start.3) | collective-permute-done | bytes 245792 | tf_op jit(solution)/shard_map/ppermute | solution.py:281
  25.9 0.0 collective-permute-start.4
  25.9 3.6 %collective-permute-start.5 = (bf16[480,256]{1,0:T(8,128)(2,1)S(1)}, bf16[480,256]{1,0:T(8,128)(2,1)S(1)}, u32[]{:S(2)}, u32[]{:S(2)}) collective-permute-start(bf16[480,256]{1,0:T(8,128)(2,1)S(1)} %get-tuple-element.41), channel_id=1, source_target_pairs={{0,12},{4,8},{8,4},{12,0},{1,13},{5,9},{9,5},{13,1},{2,14},{6,10},... | collective-permute-start | bytes 737288 | tf_op jit(solution)/shard_map/ppermute | solution.py:281
  29.5 0.0 collective-permute-done.4.other_ref
  29.5 5.0 %attend_row.6 = (bf16[480,256]{1,0:T(8,128)(2,1)S(1)}, bf16[480,768]{1,0:T(8,128)(2,1)S(1)}) custom-call(bf16[480,256]{1,0:T(8,128)(2,1)S(1)} %collective-permute-done.3.own_ref, bf16[480,256]{1,0:T(8,128)(2,1)S(1)} %collective-permute-done.4.other_ref, f32[3,256]{1,0:T(4,128)S(1)} %copy-done.8, bf16[256,768]{1,0:T(8,128)(2,1)S(1)} %copy-done.5, ...), custom_call_target="tpu_custom_call" | custom-call | flops 2327838720 | bytes 2392064 | tf_op jit(solution)/shard_map/attend_row/pallas_call | solution.py:215
  34.5 1.6 %collective-permute-done.5.own_ref = bf16[480,256]{1,0:T(8,128)(2,1)S(1)} collective-permute-done((bf16[480,256]{1,0:T(8,128)(2,1)S(1)}, bf16[480,256]{1,0:T(8,128)(2,1)S(1)}, u32[]{:S(2)}, u32[]{:S(2)}) %collective-permute-start.5) | collective-permute-done | bytes 245792 | tf_op jit(solution)/shard_map/ppermute | solution.py:281
  36.1 0.0 copy-start
  36.1 0.0 copy-start.1
  36.1 0.0 copy-start.2
  36.1 0.0 collective-permute-start.6
  36.2 1.5 %collective-permute-done.6.other_ref = bf16[480,256]{1,0:T(8,128)(2,1)S(1)} collective-permute-done((bf16[480,256]{1,0:T(8,128)(2,1)S(1)}, bf16[480,256]{1,0:T(8,128)(2,1)S(1)}, u32[]{:S(2)}, u32[]{:S(2)}) %collective-permute-start.6) | collective-permute-done | bytes 245792 | tf_op jit(solution)/shard_map/ppermute | solution.py:19
  37.7 4.9 %attend_row.7 = (bf16[480,256]{1,0:T(8,128)(2,1)S(1)}, bf16[480,768]{1,0:T(8,128)(2,1)S(1)}) custom-call(bf16[480,256]{1,0:T(8,128)(2,1)S(1)} %collective-permute-done.5.own_ref, bf16[480,256]{1,0:T(8,128)(2,1)S(1)} %collective-permute-done.6.other_ref, f32[3,256]{1,0:T(4,128)S(1)} %copy-done.8, bf16[256,768]{1,0:T(8,128)(2,1)S(1)} %copy-done.5, ...), custom_call_target="tpu_custom_call" | custom-call | flops 2327838720 | bytes 2392064 | tf_op jit(solution)/shard_map/attend_row/pallas_call | solution.py:215
  42.5 0.0 copy-done
  42.5 0.0 copy-done.1
  42.5 0.0 copy-done.2
  42.5 0.0 copy-start.3
  42.6 0.0 copy-start.4
  42.6 5.3 %attend_time.1 = (bf16[480,256]{1,0:T(8,128)(2,1)S(1)}, bf16[480,256]{1,0:T(8,128)(2,1)S(1)}, bf16[480,256]{1,0:T(8,128)(2,1)S(1)}, bf16[480,256]{1,0:T(8,128)(2,1)S(1)}) custom-call(bf16[480,768]{1,0:T(8,128)(2,1)S(1)} %get-tuple-element.23.refs_0_, bf16[480,768]{1,0:T(8,128)(2,1)S(1)} %get-tuple-element.26.refs_1_, ...), custom_call_target="tpu_custom_call" | custom-call | flops 251658240 | bytes 4915200 | tf_op jit(solution)/shard_map/attend_time/pallas_call | solution.py:245
  47.9 0.0 copy-done.3
  47.9 0.0 copy-done.4
  47.9 1.1 %mlp_row.4 = bf16[480,256]{1,0:T(8,128)(2,1)S(1)} custom-call(bf16[480,256]{1,0:T(8,128)(2,1)S(1)} %get-tuple-element.38.stream_ref, f32[3,256]{1,0:T(4,128)S(1)} %copy-done.8, bf16[256,1024]{1,0:T(8,128)(2,1)S(1)} %copy-done.3, bf16[1024,256]{1,0:T(8,128)(2,1)S(1)} %copy-done.4), custom_call_target="tpu_custom_call" | custom-call | flops 503316480 | bytes 1540096 | tf_op jit(solution)/shard_map/mlp_row/pallas_call | solution.py:266
  49.1 3.9 %collective-permute-start.7 = (bf16[480,256]{1,0:T(8,128)(2,1)S(1)}, bf16[480,256]{1,0:T(8,128)(2,1)S(1)}, u32[]{:S(2)}, u32[]{:S(2)}) collective-permute-start(bf16[480,256]{1,0:T(8,128)(2,1)S(1)} %mlp_row.4), channel_id=1, source_target_pairs={{0,8},{4,12},{8,0},{12,4},{1,9},{5,13},{9,1},{13,5},{2,10},{6,14},... | collective-permute-start | bytes 737288 | tf_op jit(solution)/shard_map/ppermute | solution.py:281
  53.0 1.1 %mlp_row.5 = bf16[480,256]{1,0:T(8,128)(2,1)S(1)} custom-call(bf16[480,256]{1,0:T(8,128)(2,1)S(1)} %get-tuple-element.39.stream_ref, f32[3,256]{1,0:T(4,128)S(1)} %copy-done.8, bf16[256,1024]{1,0:T(8,128)(2,1)S(1)} %copy-done.3, bf16[1024,256]{1,0:T(8,128)(2,1)S(1)} %copy-done.4), custom_call_target="tpu_custom_call" | custom-call | flops 503316480 | bytes 1540096 | tf_op jit(solution)/shard_map/mlp_row/pallas_call | solution.py:266
  54.1 2.7 %collective-permute-start.8 = (bf16[480,256]{1,0:T(8,128)(2,1)S(1)}, bf16[480,256]{1,0:T(8,128)(2,1)S(1)}, u32[]{:S(2)}, u32[]{:S(2)}) collective-permute-start(bf16[480,256]{1,0:T(8,128)(2,1)S(1)} %mlp_row.5), channel_id=1, source_target_pairs={{0,12},{4,8},{8,4},{12,0},{1,13},{5,9},{9,5},{13,1},{2,14},{6,10},... | collective-permute-start | bytes 737288 | tf_op jit(solution)/shard_map/ppermute | solution.py:281
  56.8 1.1 %mlp_row.6 = bf16[480,256]{1,0:T(8,128)(2,1)S(1)} custom-call(bf16[480,256]{1,0:T(8,128)(2,1)S(1)} %get-tuple-element.40.stream_ref, f32[3,256]{1,0:T(4,128)S(1)} %copy-done.8, bf16[256,1024]{1,0:T(8,128)(2,1)S(1)} %copy-done.3, bf16[1024,256]{1,0:T(8,128)(2,1)S(1)} %copy-done.4), custom_call_target="tpu_custom_call" | custom-call | flops 503316480 | bytes 1540096 | tf_op jit(solution)/shard_map/mlp_row/pallas_call | solution.py:266
  57.9 0.1 collective-permute-start.9
  58.0 0.1 broadcast_in_dim.17
  58.1 1.1 %mlp_row.7 = bf16[1,1,4,480,256]{4,3,2,1,0:T(8,128)(2,1)S(1)} fusion(bf16[1,1,4,480,256]{4,3,2,1,0:T(8,128)(2,1)S(1)} %broadcast_in_dim.17, s32[]{:T(128)S(6)} %select_n.18, bf16[480,256]{1,0:T(8,128)(2,1)S(1)} %get-tuple-element.37, f32[3,256]{1,0:T(4,128)S(1)} %copy-done.8, bf16[256,1024]{1,0:T(8,128)(2,1)S(1)} %copy-done.3, ...), kind=kCustom, calls=%fused_computation.3 | custom fusion | bytes 1544196 | tf_op jit(solution)/shard_map/mlp_row/pallas_call | solution.py:266
  59.2 11.1 %collective-permute-done.7 = bf16[480,256]{1,0:T(8,128)(2,1)S(1)} collective-permute-done((bf16[480,256]{1,0:T(8,128)(2,1)S(1)}, bf16[480,256]{1,0:T(8,128)(2,1)S(1)}, u32[]{:S(2)}, u32[]{:S(2)}) %collective-permute-start.7) | collective-permute-done | bytes 245792 | tf_op jit(solution)/shard_map/ppermute | solution.py:281
  70.4 0.0 collective-permute-done.8
  70.4 0.0 copy-start.9
  70.4 3.1 %collective-permute-done.9 = bf16[480,256]{1,0:T(8,128)(2,1)S(1)} collective-permute-done((bf16[480,256]{1,0:T(8,128)(2,1)S(1)}, bf16[480,256]{1,0:T(8,128)(2,1)S(1)}, u32[]{:S(2)}, u32[]{:S(2)}) %collective-permute-start.9) | collective-permute-done | bytes 245792 | tf_op jit(solution)/shard_map/ppermute | solution.py:281
  73.5 0.0 copy-done.9
  73.5 0.7 bitcast_dynamic-update-slice_fusion
  (2 shorter events, 0.0 us)
Async XLA Ops:
  0.0 4.7 %copy-start.5 = (bf16[256,768]{1,0:T(8,128)(2,1)S(1)}, bf16[256,768]{1,0:T(8,128)(2,1)}, u32[]{:S(2)}) copy-start(bf16[256,768]{1,0:T(8,128)(2,1)} %qkv_ref.7) | copy-start | bytes 1179652
  0.0 4.7 %copy-start.6 = (bf16[256,768]{1,0:T(8,128)(2,1)S(1)}, bf16[256,768]{1,0:T(8,128)(2,1)}, u32[]{:S(2)}) copy-start(bf16[256,768]{1,0:T(8,128)(2,1)} %time_ref.7) | copy-start | bytes 1179652
  0.0 4.7 %copy-start.7 = (bf16[256,256]{1,0:T(8,128)(2,1)S(1)}, bf16[256,256]{1,0:T(8,128)(2,1)}, u32[]{:S(2)}) copy-start(bf16[256,256]{1,0:T(8,128)(2,1)} %out_ref.11) | copy-start | bytes 393220
  0.0 4.7 %copy-start.8 = (f32[3,256]{1,0:T(4,128)S(1)}, f32[3,256]{1,0:T(4,128)}, u32[]{:S(2)}) copy-start(f32[3,256]{1,0:T(4,128)} %gains_ref.14) | copy-start | bytes 9220
  1.5 3.2 %collective-permute-start = (bf16[480,256]{1,0:T(8,128)(2,1)S(1)}, bf16[480,256]{1,0:T(8,128)(2,1)S(1)}, u32[]{:S(2)}, u32[]{:S(2)}) collective-permute-start(bf16[480,256]{1,0:T(8,128)(2,1)S(1)} %get-tuple-element.43.own_ref), channel_id=1, source_target_pairs={{0,1},{1,0},{2,3},{3,2},{4,5},{5,4},{6,7},{7,6},{8,9},{9,8},{10,11... | collective-permute-start | bytes 737288 | tf_op jit(solution)/shard_map/ppermute | solution.py:19
  2.0 9.2 %collective-permute-start.1 = (bf16[480,256]{1,0:T(8,128)(2,1)S(1)}, bf16[480,256]{1,0:T(8,128)(2,1)S(1)}, u32[]{:S(2)}, u32[]{:S(2)}) collective-permute-start(bf16[480,256]{1,0:T(8,128)(2,1)S(1)} %get-tuple-element.42), channel_id=1, source_target_pairs={{0,4},{4,0},{8,12},{12,8},{1,5},{5,1},{9,13},{13,9},{2,6},{6,2},{1... | collective-permute-start | bytes 737288 | tf_op jit(solution)/shard_map/ppermute | solution.py:281
  11.2 2.8 %collective-permute-start.2 = (bf16[480,256]{1,0:T(8,128)(2,1)S(1)}, bf16[480,256]{1,0:T(8,128)(2,1)S(1)}, u32[]{:S(2)}, u32[]{:S(2)}) collective-permute-start(bf16[480,256]{1,0:T(8,128)(2,1)S(1)} %collective-permute-done.1.own_ref), channel_id=1, source_target_pairs={{0,1},{1,0},{2,3},{3,2},{4,5},{5,4},{6,7},{7,6},{8,9},{9,8},{10,11... | collective-permute-start | bytes 737288 | tf_op jit(solution)/shard_map/ppermute | solution.py:19
  11.2 14.6 %collective-permute-start.3 = (bf16[480,256]{1,0:T(8,128)(2,1)S(1)}, bf16[480,256]{1,0:T(8,128)(2,1)S(1)}, u32[]{:S(2)}, u32[]{:S(2)}) collective-permute-start(bf16[480,256]{1,0:T(8,128)(2,1)S(1)} %get-tuple-element.44), channel_id=1, source_target_pairs={{0,8},{4,12},{8,0},{12,4},{1,9},{5,13},{9,1},{13,5},{2,10},{6,14},... | collective-permute-start | bytes 737288 | tf_op jit(solution)/shard_map/ppermute | solution.py:281
  25.9 3.6 %collective-permute-start.4 = (bf16[480,256]{1,0:T(8,128)(2,1)S(1)}, bf16[480,256]{1,0:T(8,128)(2,1)S(1)}, u32[]{:S(2)}, u32[]{:S(2)}) collective-permute-start(bf16[480,256]{1,0:T(8,128)(2,1)S(1)} %collective-permute-done.3.own_ref), channel_id=1, source_target_pairs={{0,1},{1,0},{2,3},{3,2},{4,5},{5,4},{6,7},{7,6},{8,9},{9,8},{10,11... | collective-permute-start | bytes 737288 | tf_op jit(solution)/shard_map/ppermute | solution.py:19
  25.9 10.3 %collective-permute-start.5 = (bf16[480,256]{1,0:T(8,128)(2,1)S(1)}, bf16[480,256]{1,0:T(8,128)(2,1)S(1)}, u32[]{:S(2)}, u32[]{:S(2)}) collective-permute-start(bf16[480,256]{1,0:T(8,128)(2,1)S(1)} %get-tuple-element.41), channel_id=1, source_target_pairs={{0,12},{4,8},{8,4},{12,0},{1,13},{5,9},{9,5},{13,1},{2,14},{6,10},... | collective-permute-start | bytes 737288 | tf_op jit(solution)/shard_map/ppermute | solution.py:281
  36.1 6.4 %copy-start = (bf16[16,256,128]{2,1,0:T(8,128)(2,1)S(1)}, bf16[16,256,128]{2,1,0:T(8,128)(2,1)}, u32[]{:S(2)}) copy-start(bf16[16,256,128]{2,1,0:T(8,128)(2,1)} %constant.47.clone.refs_8_) | copy-start | bytes 3145732
  36.1 6.4 %copy-start.1 = (bf16[16,128,256]{2,1,0:T(8,128)(2,1)S(1)}, bf16[16,128,256]{2,1,0:T(8,128)(2,1)}, u32[]{:S(2)}) copy-start(bf16[16,128,256]{2,1,0:T(8,128)(2,1)} %constant.48.clone.refs_9_) | copy-start | bytes 3145732
  36.1 6.4 %copy-start.2 = (bf16[256,256]{1,0:T(8,128)(2,1)S(1)}, bf16[256,256]{1,0:T(8,128)(2,1)}, u32[]{:S(2)}) copy-start(bf16[256,256]{1,0:T(8,128)(2,1)} %refs_10_.1) | copy-start | bytes 393220
  36.1 1.5 %collective-permute-start.6 = (bf16[480,256]{1,0:T(8,128)(2,1)S(1)}, bf16[480,256]{1,0:T(8,128)(2,1)S(1)}, u32[]{:S(2)}, u32[]{:S(2)}) collective-permute-start(bf16[480,256]{1,0:T(8,128)(2,1)S(1)} %collective-permute-done.5.own_ref), channel_id=1, source_target_pairs={{0,1},{1,0},{2,3},{3,2},{4,5},{5,4},{6,7},{7,6},{8,9},{9,8},{10,11... | collective-permute-start | bytes 737288 | tf_op jit(solution)/shard_map/ppermute | solution.py:19
  42.5 5.4 %copy-start.3 = (bf16[256,1024]{1,0:T(8,128)(2,1)S(1)}, bf16[256,1024]{1,0:T(8,128)(2,1)}, u32[]{:S(2)}) copy-start(bf16[256,1024]{1,0:T(8,128)(2,1)} %in_ref.6) | copy-start | bytes 1572868
  42.6 5.4 %copy-start.4 = (bf16[1024,256]{1,0:T(8,128)(2,1)S(1)}, bf16[1024,256]{1,0:T(8,128)(2,1)}, u32[]{:S(2)}) copy-start(bf16[1024,256]{1,0:T(8,128)(2,1)} %out_ref.14) | copy-start | bytes 1572868
  49.1 21.3 %collective-permute-start.7 = (bf16[480,256]{1,0:T(8,128)(2,1)S(1)}, bf16[480,256]{1,0:T(8,128)(2,1)S(1)}, u32[]{:S(2)}, u32[]{:S(2)}) collective-permute-start(bf16[480,256]{1,0:T(8,128)(2,1)S(1)} %mlp_row.4), channel_id=1, source_target_pairs={{0,8},{4,12},{8,0},{12,4},{1,9},{5,13},{9,1},{13,5},{2,10},{6,14},... | collective-permute-start | bytes 737288 | tf_op jit(solution)/shard_map/ppermute | solution.py:281
  54.1 16.3 %collective-permute-start.8 = (bf16[480,256]{1,0:T(8,128)(2,1)S(1)}, bf16[480,256]{1,0:T(8,128)(2,1)S(1)}, u32[]{:S(2)}, u32[]{:S(2)}) collective-permute-start(bf16[480,256]{1,0:T(8,128)(2,1)S(1)} %mlp_row.5), channel_id=1, source_target_pairs={{0,12},{4,8},{8,4},{12,0},{1,13},{5,9},{9,5},{13,1},{2,14},{6,10},... | collective-permute-start | bytes 737288 | tf_op jit(solution)/shard_map/ppermute | solution.py:281
  57.9 15.6 %collective-permute-start.9 = (bf16[480,256]{1,0:T(8,128)(2,1)S(1)}, bf16[480,256]{1,0:T(8,128)(2,1)S(1)}, u32[]{:S(2)}, u32[]{:S(2)}) collective-permute-start(bf16[480,256]{1,0:T(8,128)(2,1)S(1)} %mlp_row.6), channel_id=1, source_target_pairs={{0,4},{4,0},{8,12},{12,8},{1,5},{5,1},{9,13},{13,9},{2,6},{6,2},{1... | collective-permute-start | bytes 737288 | tf_op jit(solution)/shard_map/ppermute | solution.py:281
  70.4 3.1 %copy-start.9 = (bf16[1,1,4,480,256]{4,3,2,1,0:T(8,128)(2,1)}, bf16[1,1,4,480,256]{4,3,2,1,0:T(8,128)(2,1)S(1)}, u32[]{:S(2)}) copy-start(bf16[1,1,4,480,256]{4,3,2,1,0:T(8,128)(2,1)S(1)} %bitcast_dynamic-update-slice_fusion.1) | copy-start | bytes 2949124

commit v2 on v0

--- a/solution.py
+++ b/solution.py
@@ -1,7 +1,12 @@
+import functools
+
 import jax
 import jax.numpy as jnp
 from jax import lax
+from jax.experimental import pallas as pl
+from jax.experimental.pallas import tpu as pltpu
 from jax.sharding import PartitionSpec as P
+
 
 HEADS = 8
 
@@ -52,7 +57,7 @@
     return mixed.reshape(frames, pixels, channels).astype(jnp.bfloat16)
 
 
-def local(feats, norm_gains, cross_qkv, cross_out, time_qkv, time_out, mlp_in, mlp_out):
+def local_pixels(feats, norm_gains, cross_qkv, cross_out, time_qkv, time_out, mlp_in, mlp_out):
     rows_here, row_width, channels = (feats.shape[2], feats.shape[3], feats.shape[4])
     frame_count = lax.axis_size("frame")
     tokens_flat = feats[0, 0].reshape(-1, channels)
@@ -112,6 +117,295 @@
     return result.reshape(1, 1, rows_here, row_width, channels)
 
 
+LOG2E = 1.4426950408889634
+LANES = 128
+PARAMS = pltpu.CompilerParams(vmem_limit_bytes=20 * 1024 * 1024)
+
+
+def dot(a, b):
+    return jnp.dot(a, b, preferred_element_type=jnp.float32)
+
+
+def dot_dims(a, b, left, right):
+    return lax.dot_general(
+        a, b, (((left,), (right,)), ((), ())), preferred_element_type=jnp.float32
+    )
+
+
+def row_queries(own_ref, gains_ref, qkv_ref):
+    channels = own_ref.shape[1]
+    normed = layer_norm(own_ref[...], gains_ref[0:1, :])
+    return dot(normed, qkv_ref[:, :channels]).astype(jnp.bfloat16)
+
+
+def row_keys_values(other_ref, gains_ref, qkv_ref):
+    channels = other_ref.shape[1]
+    normed = layer_norm(other_ref[...], gains_ref[0:1, :])
+    keys = dot(normed, qkv_ref[:, channels : 2 * channels]).astype(jnp.bfloat16)
+    values = dot(normed, qkv_ref[:, 2 * channels :]).astype(jnp.bfloat16)
+    return keys, values.T
+
+
+def cross_heads(queries, keys, values, mix_ref):
+    length, channels = keys.shape
+    head_dim = channels // HEADS
+    lane = lax.broadcasted_iota(jnp.int32, (1, LANES), 1)
+    ones = jnp.ones((16, length), jnp.bfloat16)
+    for head in range(HEADS):
+        tile = head * head_dim // LANES
+        low = head * head_dim - tile * LANES
+        held = (lane >= low) & (lane < low + head_dim)
+        columns = slice(tile * LANES, (tile + 1) * LANES)
+        here = slice(head * head_dim, (head + 1) * head_dim)
+        key_part = jnp.where(held, keys[:, columns], jnp.zeros((), jnp.bfloat16))
+        scores = dot_dims(key_part, queries[:, columns], 1, 1)
+        top = jnp.max(scores, axis=0, keepdims=True)
+        expo = jnp.exp2((scores - top) * (head_dim**-0.5 * LOG2E)).astype(jnp.bfloat16)
+        mixed = dot(jnp.concatenate([values[here, :], ones], axis=0), expo)
+        mix_ref[here, :] = (mixed[:head_dim] / mixed[head_dim : head_dim + 1]).astype(jnp.bfloat16)
+
+
+def after_cross(own, mix_ref, gains_ref, out_ref, time_ref):
+    stream = own.astype(jnp.float32) + dot_dims(mix_ref[...], out_ref[...], 0, 0)
+    stream = stream.astype(jnp.bfloat16)
+    normed = layer_norm(stream, gains_ref[1:2, :])
+    return stream, dot_dims(time_ref[...], normed, 0, 1).astype(jnp.bfloat16)
+
+
+def row_kernel(own_ref, other_ref, gains_ref, qkv_ref, out_ref, time_ref, stream_ref, proj_ref, mix_ref):
+    queries = row_queries(own_ref, gains_ref, qkv_ref)
+    keys, values = row_keys_values(other_ref, gains_ref, qkv_ref)
+    cross_heads(queries, keys, values, mix_ref)
+    stream_ref[...], proj_ref[...] = after_cross(
+        own_ref[...], mix_ref, gains_ref, out_ref, time_ref
+    )
+
+
+def time_heads(projs, pixels, mixes):
+    frames = len(projs)
+    channels = mixes[0].shape[0]
+    head_dim = channels // HEADS
+
+    def one_head(head, _):
+        def rows(ref, part):
+            start = pl.multiple_of(part * channels + head * head_dim, head_dim)
+            return ref[pl.ds(start, head_dim), pixels].astype(jnp.float32)
+
+        keys = [rows(ref, 1) for ref in projs]
+        values = [rows(ref, 2) for ref in projs]
+        for f in range(frames):
+            query = rows(projs[f], 0)
+            scores = [jnp.sum(query * key, axis=0, keepdims=True) for key in keys]
+            top = functools.reduce(jnp.maximum, scores)
+            expo = [jnp.exp2((s - top) * (head_dim**-0.5 * LOG2E)) for s in scores]
+            over = 1.0 / functools.reduce(jnp.add, expo)
+            mixed = None
+            for g in range(frames):
+                share = (expo[g] * over).astype(jnp.bfloat16).astype(jnp.float32)
+                part = share * values[g]
+                mixed = part if mixed is None else mixed + part
+            start = pl.multiple_of(head * head_dim, head_dim)
+            mixes[f][pl.ds(start, head_dim), :] = mixed.astype(jnp.bfloat16)
+        return 0
+
+    lax.fori_loop(0, HEADS, one_head, 0)
+
+
+def finish_tail(
+    own, mix_ref, first, gains_ref, out_ref, time_ref, time_out_ref, projs, streams, proj_ref, mixes, results
+):
+    count = own.shape[0]
+    stream, proj_ref[...] = after_cross(own, mix_ref, gains_ref, out_ref, time_ref)
+    time_heads(
+        [ref.at[:, first : first + count] for ref in projs] + [proj_ref], slice(None), mixes
+    )
+    before = [ref[first : first + count, :] for ref in streams] + [stream]
+    for f, result in enumerate(results):
+        result[...] = (
+            before[f].astype(jnp.float32) + dot_dims(mixes[f][...], time_out_ref[...], 0, 0)
+        ).astype(jnp.bfloat16)
+
+
+def finish_head_kernel(frames, own_ref, other_ref, gains_ref, qkv_ref, out_ref, time_ref, time_out_ref, *refs):
+    projs, streams = refs[: frames - 1], refs[frames - 1 : 2 * frames - 2]
+    refs = refs[2 * frames - 2 :]
+    results, refs = refs[:frames], refs[frames:]
+    queries_ref, keys_ref, values_ref, mix_ref, proj_ref = refs[:5]
+    count = results[0].shape[0]
+    queries = row_queries(own_ref, gains_ref, qkv_ref)
+    keys, values = row_keys_values(other_ref, gains_ref, qkv_ref)
+    queries_ref[...] = queries[count:]
+    keys_ref[...] = keys
+    values_ref[...] = values
+    cross_heads(queries[:count], keys, values, mix_ref)
+    finish_tail(
+        own_ref[:count, :], mix_ref, 0, gains_ref, out_ref, time_ref, time_out_ref,
+        projs, streams, proj_ref, refs[5:], results,
+    )
+
+
+def finish_rest_kernel(
+    frames, own_ref, queries_ref, keys_ref, values_ref, gains_ref, out_ref, time_ref, time_out_ref, *refs
+):
+    projs, streams = refs[: frames - 1], refs[frames - 1 : 2 * frames - 2]
+    refs = refs[2 * frames - 2 :]
+    results, refs = refs[:frames], refs[frames:]
+    count = results[0].shape[0]
+    first = own_ref.shape[0] - count
+    cross_heads(queries_ref[...], keys_ref[...], values_ref[...], refs[0])
+    finish_tail(
+        own_ref[first:, :], refs[0], first, gains_ref, out_ref, time_ref, time_out_ref,
+        projs, streams, refs[1], refs[2:], results,
+    )
+
+
+def mlp_kernel(pieces, *refs):
+    gains_ref, in_ref, out_ref, result_ref = refs[pieces:]
+    first = 0
+    for ref in refs[:pieces]:
+        stream = ref[...]
+        normed = layer_norm(stream, gains_ref[2:3, :])
+        inner = jax.nn.gelu(dot(normed, in_ref[...]), approximate=True).astype(jnp.bfloat16)
+        result_ref[first : first + stream.shape[0], :] = (
+            stream.astype(jnp.float32) + dot(inner, out_ref[...])
+        ).astype(jnp.bfloat16)
+        first += stream.shape[0]
+
+
+def array(*shape):
+    return jax.ShapeDtypeStruct(shape, jnp.bfloat16)
+
+
+def attend_row(own, other, norm_gains, cross_qkv, cross_out, time_qkv):
+    length, channels = own.shape
+    return pl.pallas_call(
+        row_kernel,
+        out_shape=(array(length, channels), array(3 * channels, length)),
+        scratch_shapes=[pltpu.VMEM((channels, length), jnp.bfloat16)],
+        compiler_params=PARAMS,
+        cost_estimate=pl.CostEstimate(
+            flops=2 * length * channels * 7 * channels + 4 * length * length * channels * HEADS,
+            bytes_accessed=2 * (6 * length * channels + 7 * channels * channels),
+            transcendentals=HEADS * length * length,
+        ),
+        name="attend_row",
+    )(own, other, norm_gains, cross_qkv, cross_out, time_qkv)
+
+
+def finish_cost(length, count, channels, frames):
+    return pl.CostEstimate(
+        flops=2 * length * channels * 3 * channels + 4 * length * count * channels * HEADS,
+        bytes_accessed=2 * (8 * frames * count * channels + 8 * channels * channels),
+        transcendentals=HEADS * length * count,
+    )
+
+
+def finish_scratch(count, channels, frames):
+    return (
+        [pltpu.VMEM((channels, count), jnp.bfloat16)]
+        + [pltpu.VMEM((3 * channels, count), jnp.bfloat16)]
+        + [pltpu.VMEM((channels, count), jnp.bfloat16)] * frames
+    )
+
+
+def finish_head(count, own, other, weights, time_out, projs, streams):
+    norm_gains, cross_qkv, cross_out, time_qkv = weights
+    length, channels = own.shape
+    frames = len(projs) + 1
+    out = pl.pallas_call(
+        functools.partial(finish_head_kernel, frames),
+        out_shape=[array(count, channels)] * frames
+        + [array(length - count, channels), array(length, channels), array(channels, length)],
+        scratch_shapes=finish_scratch(count, channels, frames),
+        compiler_params=PARAMS,
+        cost_estimate=finish_cost(length, count, channels, frames),
+        name="finish_head",
+    )(own, other, norm_gains, cross_qkv, cross_out, time_qkv, time_out, *projs, *streams)
+    return out[:frames], out[frames:]
+
+
+def finish_rest(own, kept, weights, time_out, projs, streams):
+    norm_gains, _, cross_out, time_qkv = weights
+    length, channels = own.shape
+    frames = len(projs) + 1
+    count = kept[0].shape[0]
+    return pl.pallas_call(
+        functools.partial(finish_rest_kernel, frames),
+        out_shape=[array(count, channels)] * frames,
+        scratch_shapes=finish_scratch(count, channels, frames),
+        compiler_params=PARAMS,
+        cost_estimate=finish_cost(length, count, channels, frames),
+        name="finish_rest",
+    )(own, *kept, norm_gains, cross_out, time_qkv, time_out, *projs, *streams)
+
+
+def mlp(pieces, norm_gains, mlp_in, mlp_out):
+    channels, hidden = mlp_in.shape
+    length = sum(piece.shape[0] for piece in pieces)
+    return pl.pallas_call(
+        functools.partial(mlp_kernel, len(pieces)),
+        out_shape=array(length, channels),
+        compiler_params=PARAMS,
+        cost_estimate=pl.CostEstimate(
+            flops=4 * length * channels * hidden,
+            bytes_accessed=4 * (length * channels + channels * hidden),
+            transcendentals=length * hidden,
+        ),
+        name="mlp",
+    )(*pieces, norm_gains, mlp_in, mlp_out)
+
+
+def frame_swapped(value, distance):
+    count = lax.axis_size("frame")
+    return lax.ppermute(value, "frame", [(i, i ^ distance) for i in range(count)])
+
+
+def local_rows(feats, norm_gains, cross_qkv, cross_out, time_qkv, time_out, mlp_in, mlp_out):
+    rows_here, row_width, _ = feats.shape[2:]
+    here = lax.axis_index("frame")
+    rows = feats[0, 0]
+    weights = (norm_gains, cross_qkv, cross_out, time_qkv)
+    order = list(range(1, rows_here))
+    own_rows = {0: lax.dynamic_index_in_dim(rows, here, 0, keepdims=False)}
+    for d in order:
+        piece = lax.dynamic_index_in_dim(rows, here ^ d, 0, keepdims=False)
+        own_rows[d] = frame_swapped(piece, d)
+    streams, projs = [], []
+    for d in [0] + order:
+        own = own_rows[d]
+        if d:
+            own, streams[-1] = lax.optimization_barrier((own, streams[-1]))
+        other = swapped(own, "view", 0)
+        if d == order[-1]:
+            break
+        stream, proj = attend_row(own, other, *weights)
+        streams.append(stream)
+        projs.append(proj)
+    count = min(row_width, 2 * LANES)
+    early, kept = finish_head(count, own, other, weights, time_out, projs, streams)
+    late = finish_rest(own, kept, weights, time_out, projs, streams)
+    far = order[1:]
+    result = jnp.zeros(rows.shape, jnp.bfloat16)
+    arrived = []
+    for pieces, first in ((early, 0), (late, count)):
+        for d in far:
+            done = mlp([pieces[d]], norm_gains, mlp_in, mlp_out)
+            arrived.append((here ^ d, first, frame_swapped(done, d)))
+    near = mlp([early[1], late[1]], norm_gains, mlp_in, mlp_out)
+    arrived.append((here ^ 1, 0, frame_swapped(near, 1)))
+    own_result = mlp([early[0], late[0]], norm_gains, mlp_in, mlp_out)
+    arrived.insert(0, (here, 0, own_result))
+    for row, first, value in arrived:
+        result = lax.dynamic_update_slice(result, value[None], (row, first, 0))
+    return result[None, None]
+
+
+def local(feats, *rest):
+    rows_here = feats.shape[2]
+    whole = rows_here == lax.axis_size("frame") and rows_here & (rows_here - 1) == 0
+    return (local_rows if whole else local_pixels)(feats, *rest)
+
+
 def solution(mesh):
     placed = (P(("clips", "view"), "frame", "rows", None, None), P(), P(), P(), P(), P(), P(), P())
     return jax.shard_map(

time: 187 us -> 74.7 us (0.40)
  matrix products: 62.5 us -> 0 us
  blocking collectives: 57.4 us -> 0 us
  local copies, waits for them, and re-layouts: 55.2 us -> 4.41 us
  Pallas kernels: 0 us -> 30.1 us
  starting transfers between devices: 0.49 us -> 19.9 us
  waiting for transfers between devices: 2.78 us -> 20 us
  other arithmetic: 7.24 us -> 0 us
    all_to_all x2 -> x0, blocking collectives: 57.4 us -> none  [the longest x1 30.7 us: local(): lax.all_to_all(outgoing, 'frame', split_axis=1, concat_axis=0, tiled=True)]
    dot_general x11 -> x0, matrix products: 43.3 us -> none  [the longest x4 16.1 us: row_attend(): jnp.einsum('hqk,khd->qhd', shares, v_heads, preferred_element_type=jnp.fl...]
    pallas_call x0 -> x10, Pallas kernels: none -> 30.1 us  [the longest x3 15.2 us: attend_row(): pl.pallas_call(row_kernel, out_shape=(array(length, channels), array(3 *...]
    ppermute x0 -> x8, starting transfers between devices: none -> 19.3 us  [frame_swapped(): lax.ppermute(value, 'frame', [(i, i ^ distance) for i in range(count)])]
    sub x4 -> x0, matrix products: 19.1 us -> none  [row_attend(): expo = jnp.exp(scores - top_score)]
    ppermute x0 -> x8, waiting for transfers between devices: none -> 18.4 us  [frame_swapped(): lax.ppermute(value, 'frame', [(i, i ^ distance) for i in range(count)])]
    reshape x3 -> x0, local copies, waits for them, and re-layouts: 13.8 us -> none  [the longest x1 4.71 us: time_attend(): v_heads = value_rows.reshape(frames, pixels, HEADS, head_dim)]
    convert_element_type x3 -> x0, local copies, waits for them, and re-layouts: 13.4 us -> none  [the longest x1 7.42 us: time_attend(): shares = (expo / jnp.sum(expo, axis=2, keepdims=True)).astype(jnp.bfloat16)]
  transfers between devices with their start and end apart: 1 -> 12, of which waited for: 1 -> 6; matrix products, arithmetic and copies ran while one was open for 1% -> 2% of each run, Pallas kernels for 0% -> 32%
where the time goes in v2:
time: 74.7 us; the launch traced here: 74.6 us
  Pallas kernels  30.1 us (40%)
  waiting for transfers between devices  20 us (27%)
  starting transfers between devices  19.9 us (27%)
  local copies, waits for them, and re-layouts  4.41 us (6%)
    ppermute x8, starting transfers between devices, frame_swapped(): lax.ppermute(value, 'frame', [(i, i ^ distance) for i in range(count)])  19.3 us
    ppermute x8, waiting for transfers between devices, frame_swapped(): lax.ppermute(value, 'frame', [(i, i ^ distance) for i in range(count)])  18.4 us
    pallas_call x3, Pallas kernels, attend_row(): pl.pallas_call(row_kernel, out_shape=(array(length, channels), array(3 *...  15.2 us
    pallas_call x1, Pallas kernels, finish_head(): pl.pallas_call(functools.partial(finish_head_kernel, frames), out_shape=[...  5.62 us
    pallas_call x1, Pallas kernels, finish_rest(): pl.pallas_call(functools.partial(finish_rest_kernel, frames), out_shape=[...  5.16 us
    pallas_call x5, Pallas kernels, mlp(): pl.pallas_call(functools.partial(mlp_kernel, len(pieces)), out_shape=arra...  4.17 us
    ppermute x4, waiting for transfers between devices, swapped(): lax.ppermute(value, axis, [(i, i ^ 1 << bit) for i in range(lax.axis_size...  1.52 us
  transfers between devices with their start and end apart: 12, of which 6 were waited for; matrix products, arithmetic and copies ran while one was open for 2% of the time, Pallas kernels for 32%

profile of v2, /device:TPU:0, one launch (start us, length us, event | category | flops | bytes accessed | tf_op | source)
XLA Modules:
  0.0 74.6 jit_solution(12242775178930424461)
XLA Ops:
  0.0 0.0 copy-start.2
  0.0 0.0 copy-start.3
  0.0 0.0 copy-start.5
  0.0 0.0 copy-start.6
  0.0 1.4 %dynamic-slice_bitcast_fusion = (bf16[480,256]{1,0:T(8,128)(2,1)S(1)}, bf16[480,256]{1,0:T(8,128)(2,1)S(1)}, bf16[480,256]{1,0:T(8,128)(2,1)S(1)}, bf16[480,256]{1,0:T(8,128)(2,1)S(1)}) fusion(bf16[1,1,4,480,256]{4,3,2,1,0:T(8,128)(2,1)} %param.8, s32[]{:T(128)S(6)} %select_n.22, s32[]{:T(128)S(6)} %select_n.20, s32[]{:T(128)S(6)} %select_n.19, s32[]{:T(128)S(6)} %select_n.21), kind=kLoop, calls=%fused_computation.2 | loop fusion | bytes 1966096 | tf_op jit(solution)/shard_map/jit(dynamic_index_in_dim)/squeeze | solution.py:369
  1.5 0.6 collective-permute-start.3
  2.0 2.6 %collective-permute-start.2 = (bf16[480,256]{1,0:T(8,128)(2,1)S(1)}, bf16[480,256]{1,0:T(8,128)(2,1)S(1)}, u32[]{:S(2)}, u32[]{:S(2)}) collective-permute-start(bf16[480,256]{1,0:T(8,128)(2,1)S(1)} %get-tuple-element.54), channel_id=1, source_target_pairs={{0,4},{4,0},{8,12},{12,8},{1,5},{5,1},{9,13},{13,9},{2,6},{6,2},{1... | collective-permute-start | bytes 737288 | tf_op jit(solution)/shard_map/ppermute | solution.py:360
  4.7 0.0 collective-permute-done.3.other_ref
  4.7 0.0 copy-done.2
  4.7 0.0 copy-done.3
  4.7 0.0 copy-done.5
  4.7 0.0 copy-done.6
  4.7 5.0 %attend_row.3 = (bf16[480,256]{1,0:T(8,128)(2,1)S(1)}, bf16[768,480]{1,0:T(8,128)(2,1)S(1)}) custom-call(bf16[480,256]{1,0:T(8,128)(2,1)S(1)} %get-tuple-element.51.own_ref, bf16[480,256]{1,0:T(8,128)(2,1)S(1)} %collective-permute-done.3.other_ref, f32[3,256]{1,0:T(4,128)S(1)} %copy-done.6, bf16[256,768]{1,0:T(8,128)(2,1)S(1)} %copy-done.5, ...), custom_call_target="tpu_custom_call" | custom-call | flops 2327838720 | bytes 2392064 | tf_op jit(solution)/shard_map/attend_row/pallas_call | solution.py:281
  9.7 1.5 %collective-permute-done.2.own_ref = bf16[480,256]{1,0:T(8,128)(2,1)S(1)} collective-permute-done((bf16[480,256]{1,0:T(8,128)(2,1)S(1)}, bf16[480,256]{1,0:T(8,128)(2,1)S(1)}, u32[]{:S(2)}, u32[]{:S(2)}) %collective-permute-start.2) | collective-permute-done | bytes 245792 | tf_op jit(solution)/shard_map/ppermute | solution.py:360
  11.2 0.0 collective-permute-start.4
  11.2 2.8 %collective-permute-start.1 = (bf16[480,256]{1,0:T(8,128)(2,1)S(1)}, bf16[480,256]{1,0:T(8,128)(2,1)S(1)}, u32[]{:S(2)}, u32[]{:S(2)}) collective-permute-start(bf16[480,256]{1,0:T(8,128)(2,1)S(1)} %get-tuple-element.52), channel_id=1, source_target_pairs={{0,8},{4,12},{8,0},{12,4},{1,9},{5,13},{9,1},{13,5},{2,10},{6,14},... | collective-permute-start | bytes 737288 | tf_op jit(solution)/shard_map/ppermute | solution.py:360
  14.0 0.0 collective-permute-done.4.other_ref
  14.0 5.0 %attend_row.4 = (bf16[480,256]{1,0:T(8,128)(2,1)S(1)}, bf16[768,480]{1,0:T(8,128)(2,1)S(1)}) custom-call(bf16[480,256]{1,0:T(8,128)(2,1)S(1)} %collective-permute-done.2.own_ref, bf16[480,256]{1,0:T(8,128)(2,1)S(1)} %collective-permute-done.4.other_ref, f32[3,256]{1,0:T(4,128)S(1)} %copy-done.6, bf16[256,768]{1,0:T(8,128)(2,1)S(1)} %copy-done.5, ...), custom_call_target="tpu_custom_call" | custom-call | flops 2327838720 | bytes 2392064 | tf_op jit(solution)/shard_map/attend_row/pallas_call | solution.py:281
  19.0 6.9 %collective-permute-done.1.own_ref = bf16[480,256]{1,0:T(8,128)(2,1)S(1)} collective-permute-done((bf16[480,256]{1,0:T(8,128)(2,1)S(1)}, bf16[480,256]{1,0:T(8,128)(2,1)S(1)}, u32[]{:S(2)}, u32[]{:S(2)}) %collective-permute-start.1) | collective-permute-done | bytes 245792 | tf_op jit(solution)/shard_map/ppermute | solution.py:360
  25.9 0.0 collective-permute-start.5
  25.9 0.0 copy-start.4
  25.9 3.6 %collective-permute-start = (bf16[480,256]{1,0:T(8,128)(2,1)S(1)}, bf16[480,256]{1,0:T(8,128)(2,1)S(1)}, u32[]{:S(2)}, u32[]{:S(2)}) collective-permute-start(bf16[480,256]{1,0:T(8,128)(2,1)S(1)} %get-tuple-element.53), channel_id=1, source_target_pairs={{0,12},{4,8},{8,4},{12,0},{1,13},{5,9},{9,5},{13,1},{2,14},{6,10},... | collective-permute-start | bytes 737288 | tf_op jit(solution)/shard_map/ppermute | solution.py:360
  29.5 0.0 collective-permute-done.5.other_ref
  29.5 5.2 %attend_row.5 = (bf16[480,256]{1,0:T(8,128)(2,1)S(1)}, bf16[768,480]{1,0:T(8,128)(2,1)S(1)}) custom-call(bf16[480,256]{1,0:T(8,128)(2,1)S(1)} %collective-permute-done.1.own_ref, bf16[480,256]{1,0:T(8,128)(2,1)S(1)} %collective-permute-done.5.other_ref, f32[3,256]{1,0:T(4,128)S(1)} %copy-done.6, bf16[256,768]{1,0:T(8,128)(2,1)S(1)} %copy-done.5, ...), custom_call_target="tpu_custom_call" | custom-call | flops 2327838720 | bytes 2392064 | tf_op jit(solution)/shard_map/attend_row/pallas_call | solution.py:281
  34.7 1.5 %collective-permute-done.own_ref = bf16[480,256]{1,0:T(8,128)(2,1)S(1)} collective-permute-done((bf16[480,256]{1,0:T(8,128)(2,1)S(1)}, bf16[480,256]{1,0:T(8,128)(2,1)S(1)}, u32[]{:S(2)}, u32[]{:S(2)}) %collective-permute-start) | collective-permute-done | bytes 245792 | tf_op jit(solution)/shard_map/ppermute | solution.py:360
  36.1 0.0 collective-permute-start.6
  36.1 1.5 %collective-permute-done.6.other_ref = bf16[480,256]{1,0:T(8,128)(2,1)S(1)} collective-permute-done((bf16[480,256]{1,0:T(8,128)(2,1)S(1)}, bf16[480,256]{1,0:T(8,128)(2,1)S(1)}, u32[]{:S(2)}, u32[]{:S(2)}) %collective-permute-start.6) | collective-permute-done | bytes 245792 | tf_op jit(solution)/shard_map/ppermute | solution.py:18
  37.7 0.0 copy-done.4
  37.7 0.0 copy-start
  37.7 0.0 copy-start.1
  37.7 5.6 %finish_head.1 = (bf16[256,256]{1,0:T(8,128)(2,1)S(1)}, bf16[256,256]{1,0:T(8,128)(2,1)S(1)}, bf16[256,256]{1,0:T(8,128)(2,1)S(1)}, bf16[256,256]{1,0:T(8,128)(2...) custom-call(bf16[480,256]{1,0:T(8,128)(2,1)S(1)} %collective-permute-done.own_ref,, ...), custom_call_target="tpu_custom_call" | custom-call | flops 1195376640 | bytes 5242880 | tf_op jit(solution)/shard_map/finish_head/pallas_call | solution.py:315
  43.3 0.0 copy-done
  43.3 0.0 copy-done.1
  43.3 0.8 %mlp.6 = bf16[256,256]{1,0:T(8,128)(2,1)S(1)} custom-call(bf16[256,256]{1,0:T(8,128)(2,1)S(1)} %get-tuple-element.45.refs_0_, f32[3,256]{1,0:T(4,128)S(1)} %copy-done.6, bf16[256,1024]{1,0:T(8,128)(2,1)S(1)} %copy-done, bf16[1024,256]{1,0:T(8,128)(2,1)S(1)} %copy-done.1), custom_call_target="tpu_custom_call" | custom-call | flops 268435456 | bytes 1310720 | tf_op jit(solution)/shard_map/mlp/pallas_call | solution.py:345
  44.1 3.9 %collective-permute-start.7 = (bf16[256,256]{1,0:T(8,128)(2,1)S(1)}, bf16[256,256]{1,0:T(8,128)(2,1)S(1)}, u32[]{:S(2)}, u32[]{:S(2)}) collective-permute-start(bf16[256,256]{1,0:T(8,128)(2,1)S(1)} %mlp.6), channel_id=1, source_target_pairs={{0,8},{4,12},{8,0},{12,4},{1,9},{5,13},{9,1},{13,5},{2,10},{6,14},... | collective-permute-start | bytes 393224 | tf_op jit(solution)/shard_map/ppermute | solution.py:360
  48.0 5.2 %finish_rest.1 = (bf16[224,256]{1,0:T(8,128)(2,1)S(1)}, bf16[224,256]{1,0:T(8,128)(2,1)S(1)}, bf16[224,256]{1,0:T(8,128)(2,1)S(1)}, bf16[224,256]{1,0:T(8,128)(2,1)S(1)}) custom-call(bf16[480,256]{1,0:T(8,128)(2,1)S(1)} %collective-permute-done.own_ref, bf16[224,256]{1,0:T(8,128)(2,1)S(1)} %get-tuple-element.41.queries_ref, ...), custom_call_target="tpu_custom_call" | custom-call | flops 1069547520 | bytes 4718592 | tf_op jit(solution)/shard_map/finish_rest/pallas_call | solution.py:332
  53.2 1.2 %mlp.10 = bf16[480,256]{1,0:T(8,128)(2,1)S(1)} custom-call(bf16[256,256]{1,0:T(8,128)(2,1)S(1)} %get-tuple-element.49.refs_0_, bf16[224,256]{1,0:T(8,128)(2,1)S(1)} %get-tuple-element.50.refs_1_, f32[3,256]{1,0:T(4,128)S(1)} %copy-done.6, bf16[256,1024]{1,0:T(8,128)(2,1)S(1)} %copy-done, bf16[1024,256]{1,0:T(8,128)(2,1)S(1)} %copy-done.1), custom_call_target="tpu_custom_call" | custom-call | flops 503316480 | bytes 1540096 | tf_op jit(solution)/shard_map/mlp/pallas_call | solution.py:345
  54.3 0.4 collective-permute-start.11
  54.7 0.8 %mlp.7 = bf16[256,256]{1,0:T(8,128)(2,1)S(1)} custom-call(bf16[256,256]{1,0:T(8,128)(2,1)S(1)} %get-tuple-element.46.refs_0_, f32[3,256]{1,0:T(4,128)S(1)} %copy-done.6, bf16[256,1024]{1,0:T(8,128)(2,1)S(1)} %copy-done, bf16[1024,256]{1,0:T(8,128)(2,1)S(1)} %copy-done.1), custom_call_target="tpu_custom_call" | custom-call | flops 268435456 | bytes 1310720 | tf_op jit(solution)/shard_map/mlp/pallas_call | solution.py:345
  55.5 2.4 %collective-permute-start.8 = (bf16[256,256]{1,0:T(8,128)(2,1)S(1)}, bf16[256,256]{1,0:T(8,128)(2,1)S(1)}, u32[]{:S(2)}, u32[]{:S(2)}) collective-permute-start(bf16[256,256]{1,0:T(8,128)(2,1)S(1)} %mlp.7), channel_id=1, source_target_pairs={{0,12},{4,8},{8,4},{12,0},{1,13},{5,9},{9,5},{13,1},{2,14},{6,10},... | collective-permute-start | bytes 393224 | tf_op jit(solution)/shard_map/ppermute | solution.py:360
  57.9 0.7 mlp.8
  58.6 0.9 %collective-permute-start.9 = (bf16[224,256]{1,0:T(8,128)(2,1)S(1)}, bf16[224,256]{1,0:T(8,128)(2,1)S(1)}, u32[]{:S(2)}, u32[]{:S(2)}) collective-permute-start(bf16[224,256]{1,0:T(8,128)(2,1)S(1)} %mlp.8), channel_id=1, source_target_pairs={{0,8},{4,12},{8,0},{12,4},{1,9},{5,13},{9,1},{13,5},{2,10},{6,14},... | collective-permute-start | bytes 344072 | tf_op jit(solution)/shard_map/ppermute | solution.py:360
  59.5 0.7 mlp.9
  60.3 2.7 %collective-permute-start.10 = (bf16[224,256]{1,0:T(8,128)(2,1)S(1)}, bf16[224,256]{1,0:T(8,128)(2,1)S(1)}, u32[]{:S(2)}, u32[]{:S(2)}) collective-permute-start(bf16[224,256]{1,0:T(8,128)(2,1)S(1)} %mlp.9), channel_id=1, source_target_pairs={{0,12},{4,8},{8,4},{12,0},{1,13},{5,9},{9,5},{13,1},{2,14},{6,10},... | collective-permute-start | bytes 344072 | tf_op jit(solution)/shard_map/ppermute | solution.py:360
  63.0 0.1 broadcast_in_dim.22
  63.0 1.2 %mlp.11 = bf16[1,1,4,480,256]{4,3,2,1,0:T(8,128)(2,1)S(1)} fusion(bf16[1,1,4,480,256]{4,3,2,1,0:T(8,128)(2,1)S(1)} %broadcast_in_dim.22, s32[]{:T(128)S(6)} %select_n.22, bf16[256,256]{1,0:T(8,128)(2,1)S(1)} %get-tuple-element.40, bf16[224,256]{1,0:T(8,128)(2,1)S(1)} %get-tuple-element.44, f32[3,256]{1,0:T(4,128)S(1)} %copy-done.6, ...), kind=kCustom, calls=%fused_computation.1 | custom fusion | bytes 1544196 | tf_op jit(solution)/shard_map/mlp/pallas_call | solution.py:345
  64.2 0.0 collective-permute-done.7
  64.3 2.4 %collective-permute-done.8 = bf16[256,256]{1,0:T(8,128)(2,1)S(1)} collective-permute-done((bf16[256,256]{1,0:T(8,128)(2,1)S(1)}, bf16[256,256]{1,0:T(8,128)(2,1)S(1)}, u32[]{:S(2)}, u32[]{:S(2)}) %collective-permute-start.8) | collective-permute-done | bytes 131104 | tf_op jit(solution)/shard_map/ppermute | solution.py:360
  66.7 6.2 %collective-permute-done.9 = bf16[224,256]{1,0:T(8,128)(2,1)S(1)} collective-permute-done((bf16[224,256]{1,0:T(8,128)(2,1)S(1)}, bf16[224,256]{1,0:T(8,128)(2,1)S(1)}, u32[]{:S(2)}, u32[]{:S(2)}) %collective-permute-start.9) | collective-permute-done | bytes 114720 | tf_op jit(solution)/shard_map/ppermute | solution.py:360
  72.9 0.0 collective-permute-done.10
  72.9 0.0 copy-start.7
  72.9 0.0 collective-permute-done.11
  72.9 0.9 %copy-done.7 = bf16[1,1,4,480,256]{4,3,2,1,0:T(8,128)(2,1)} copy-done((bf16[1,1,4,480,256]{4,3,2,1,0:T(8,128)(2,1)}, bf16[1,1,4,480,256]{4,3,2,1,0:T(8,128)(2,1)S(1)}, u32[]{:S(2)}) %copy-start.7) | copy-done | bytes 983064
  73.8 0.7 bitcast_dynamic-update-slice_fusion
  (4 shorter events, 0.1 us)
Async XLA Ops:
  0.0 4.7 %copy-start.2 = (bf16[256,768]{1,0:T(8,128)(2,1)S(1)}, bf16[256,768]{1,0:T(8,128)(2,1)}, u32[]{:S(2)}) copy-start(bf16[256,768]{1,0:T(8,128)(2,1)} %time_ref.9) | copy-start | bytes 1179652
  0.0 4.7 %copy-start.3 = (bf16[256,256]{1,0:T(8,128)(2,1)S(1)}, bf16[256,256]{1,0:T(8,128)(2,1)}, u32[]{:S(2)}) copy-start(bf16[256,256]{1,0:T(8,128)(2,1)} %out_ref.9) | copy-start | bytes 393220
  0.0 4.7 %copy-start.5 = (bf16[256,768]{1,0:T(8,128)(2,1)S(1)}, bf16[256,768]{1,0:T(8,128)(2,1)}, u32[]{:S(2)}) copy-start(bf16[256,768]{1,0:T(8,128)(2,1)} %qkv_ref.7) | copy-start | bytes 1179652
  0.0 4.7 %copy-start.6 = (f32[3,256]{1,0:T(4,128)S(1)}, f32[3,256]{1,0:T(4,128)}, u32[]{:S(2)}) copy-start(f32[3,256]{1,0:T(4,128)} %refs_2_.10) | copy-start | bytes 9220
  1.5 3.2 %collective-permute-start.3 = (bf16[480,256]{1,0:T(8,128)(2,1)S(1)}, bf16[480,256]{1,0:T(8,128)(2,1)S(1)}, u32[]{:S(2)}, u32[]{:S(2)}) collective-permute-start(bf16[480,256]{1,0:T(8,128)(2,1)S(1)} %get-tuple-element.51.own_ref), channel_id=1, source_target_pairs={{0,1},{1,0},{2,3},{3,2},{4,5},{5,4},{6,7},{7,6},{8,9},{9,8},{10,11... | collective-permute-start | bytes 737288 | tf_op jit(solution)/shard_map/ppermute | solution.py:18
  2.0 9.2 %collective-permute-start.2 = (bf16[480,256]{1,0:T(8,128)(2,1)S(1)}, bf16[480,256]{1,0:T(8,128)(2,1)S(1)}, u32[]{:S(2)}, u32[]{:S(2)}) collective-permute-start(bf16[480,256]{1,0:T(8,128)(2,1)S(1)} %get-tuple-element.54), channel_id=1, source_target_pairs={{0,4},{4,0},{8,12},{12,8},{1,5},{5,1},{9,13},{13,9},{2,6},{6,2},{1... | collective-permute-start | bytes 737288 | tf_op jit(solution)/shard_map/ppermute | solution.py:360
  11.2 2.8 %collective-permute-start.4 = (bf16[480,256]{1,0:T(8,128)(2,1)S(1)}, bf16[480,256]{1,0:T(8,128)(2,1)S(1)}, u32[]{:S(2)}, u32[]{:S(2)}) collective-permute-start(bf16[480,256]{1,0:T(8,128)(2,1)S(1)} %collective-permute-done.2.own_ref), channel_id=1, source_target_pairs={{0,1},{1,0},{2,3},{3,2},{4,5},{5,4},{6,7},{7,6},{8,9},{9,8},{10,11... | collective-permute-start | bytes 737288 | tf_op jit(solution)/shard_map/ppermute | solution.py:18
  11.2 14.6 %collective-permute-start.1 = (bf16[480,256]{1,0:T(8,128)(2,1)S(1)}, bf16[480,256]{1,0:T(8,128)(2,1)S(1)}, u32[]{:S(2)}, u32[]{:S(2)}) collective-permute-start(bf16[480,256]{1,0:T(8,128)(2,1)S(1)} %get-tuple-element.52), channel_id=1, source_target_pairs={{0,8},{4,12},{8,0},{12,4},{1,9},{5,13},{9,1},{13,5},{2,10},{6,14},... | collective-permute-start | bytes 737288 | tf_op jit(solution)/shard_map/ppermute | solution.py:360
  25.9 3.6 %collective-permute-start.5 = (bf16[480,256]{1,0:T(8,128)(2,1)S(1)}, bf16[480,256]{1,0:T(8,128)(2,1)S(1)}, u32[]{:S(2)}, u32[]{:S(2)}) collective-permute-start(bf16[480,256]{1,0:T(8,128)(2,1)S(1)} %collective-permute-done.1.own_ref), channel_id=1, source_target_pairs={{0,1},{1,0},{2,3},{3,2},{4,5},{5,4},{6,7},{7,6},{8,9},{9,8},{10,11... | collective-permute-start | bytes 737288 | tf_op jit(solution)/shard_map/ppermute | solution.py:18
  25.9 11.8 %copy-start.4 = (bf16[256,256]{1,0:T(8,128)(2,1)S(1)}, bf16[256,256]{1,0:T(8,128)(2,1)}, u32[]{:S(2)}) copy-start(bf16[256,256]{1,0:T(8,128)(2,1)} %time_out_ref.3) | copy-start | bytes 393220
  25.9 10.3 %collective-permute-start = (bf16[480,256]{1,0:T(8,128)(2,1)S(1)}, bf16[480,256]{1,0:T(8,128)(2,1)S(1)}, u32[]{:S(2)}, u32[]{:S(2)}) collective-permute-start(bf16[480,256]{1,0:T(8,128)(2,1)S(1)} %get-tuple-element.53), channel_id=1, source_target_pairs={{0,12},{4,8},{8,4},{12,0},{1,13},{5,9},{9,5},{13,1},{2,14},{6,10},... | collective-permute-start | bytes 737288 | tf_op jit(solution)/shard_map/ppermute | solution.py:360
  36.1 1.5 %collective-permute-start.6 = (bf16[480,256]{1,0:T(8,128)(2,1)S(1)}, bf16[480,256]{1,0:T(8,128)(2,1)S(1)}, u32[]{:S(2)}, u32[]{:S(2)}) collective-permute-start(bf16[480,256]{1,0:T(8,128)(2,1)S(1)} %collective-permute-done.own_ref), channel_id=1, source_target_pairs={{0,1},{1,0},{2,3},{3,2},{4,5},{5,4},{6,7},{7,6},{8,9},{9,8},{10,11... | collective-permute-start | bytes 737288 | tf_op jit(solution)/shard_map/ppermute | solution.py:18
  37.7 5.6 %copy-start = (bf16[256,1024]{1,0:T(8,128)(2,1)S(1)}, bf16[256,1024]{1,0:T(8,128)(2,1)}, u32[]{:S(2)}) copy-start(bf16[256,1024]{1,0:T(8,128)(2,1)} %refs_3_.10) | copy-start | bytes 1572868
  37.7 5.6 %copy-start.1 = (bf16[1024,256]{1,0:T(8,128)(2,1)S(1)}, bf16[1024,256]{1,0:T(8,128)(2,1)}, u32[]{:S(2)}) copy-start(bf16[1024,256]{1,0:T(8,128)(2,1)} %refs_4_.2) | copy-start | bytes 1572868
  44.1 20.1 %collective-permute-start.7 = (bf16[256,256]{1,0:T(8,128)(2,1)S(1)}, bf16[256,256]{1,0:T(8,128)(2,1)S(1)}, u32[]{:S(2)}, u32[]{:S(2)}) collective-permute-start(bf16[256,256]{1,0:T(8,128)(2,1)S(1)} %mlp.6), channel_id=1, source_target_pairs={{0,8},{4,12},{8,0},{12,4},{1,9},{5,13},{9,1},{13,5},{2,10},{6,14},... | collective-permute-start | bytes 393224 | tf_op jit(solution)/shard_map/ppermute | solution.py:360
  54.3 18.6 %collective-permute-start.11 = (bf16[480,256]{1,0:T(8,128)(2,1)S(1)}, bf16[480,256]{1,0:T(8,128)(2,1)S(1)}, u32[]{:S(2)}, u32[]{:S(2)}) collective-permute-start(bf16[480,256]{1,0:T(8,128)(2,1)S(1)} %mlp.10), channel_id=1, source_target_pairs={{0,4},{4,0},{8,12},{12,8},{1,5},{5,1},{9,13},{13,9},{2,6},{6,2},{1... | collective-permute-start | bytes 737288 | tf_op jit(solution)/shard_map/ppermute | solution.py:360
  55.5 11.2 %collective-permute-start.8 = (bf16[256,256]{1,0:T(8,128)(2,1)S(1)}, bf16[256,256]{1,0:T(8,128)(2,1)S(1)}, u32[]{:S(2)}, u32[]{:S(2)}) collective-permute-start(bf16[256,256]{1,0:T(8,128)(2,1)S(1)} %mlp.7), channel_id=1, source_target_pairs={{0,12},{4,8},{8,4},{12,0},{1,13},{5,9},{9,5},{13,1},{2,14},{6,10},... | collective-permute-start | bytes 393224 | tf_op jit(solution)/shard_map/ppermute | solution.py:360
  58.6 14.2 %collective-permute-start.9 = (bf16[224,256]{1,0:T(8,128)(2,1)S(1)}, bf16[224,256]{1,0:T(8,128)(2,1)S(1)}, u32[]{:S(2)}, u32[]{:S(2)}) collective-permute-start(bf16[224,256]{1,0:T(8,128)(2,1)S(1)} %mlp.8), channel_id=1, source_target_pairs={{0,8},{4,12},{8,0},{12,4},{1,9},{5,13},{9,1},{13,5},{2,10},{6,14},... | collective-permute-start | bytes 344072 | tf_op jit(solution)/shard_map/ppermute | solution.py:360
  60.3 12.6 %collective-permute-start.10 = (bf16[224,256]{1,0:T(8,128)(2,1)S(1)}, bf16[224,256]{1,0:T(8,128)(2,1)S(1)}, u32[]{:S(2)}, u32[]{:S(2)}) collective-permute-start(bf16[224,256]{1,0:T(8,128)(2,1)S(1)} %mlp.9), channel_id=1, source_target_pairs={{0,12},{4,8},{8,4},{12,0},{1,13},{5,9},{9,5},{13,1},{2,14},{6,10},... | collective-permute-start | bytes 344072 | tf_op jit(solution)/shard_map/ppermute | solution.py:360
  72.9 0.9 %copy-start.7 = (bf16[1,1,4,480,256]{4,3,2,1,0:T(8,128)(2,1)}, bf16[1,1,4,480,256]{4,3,2,1,0:T(8,128)(2,1)S(1)}, u32[]{:S(2)}) copy-start(bf16[1,1,4,480,256]{4,3,2,1,0:T(8,128)(2,1)S(1)} %bitcast_dynamic-update-slice_fusion.4) | copy-start | bytes 2949124

commit v3 on v2

--- a/solution.py
+++ b/solution.py
@@ -151,18 +151,26 @@
     head_dim = channels // HEADS
     lane = lax.broadcasted_iota(jnp.int32, (1, LANES), 1)
     ones = jnp.ones((16, length), jnp.bfloat16)
-    for head in range(HEADS):
+
+    def head_scores(head):
         tile = head * head_dim // LANES
         low = head * head_dim - tile * LANES
         held = (lane >= low) & (lane < low + head_dim)
         columns = slice(tile * LANES, (tile + 1) * LANES)
-        here = slice(head * head_dim, (head + 1) * head_dim)
         key_part = jnp.where(held, keys[:, columns], jnp.zeros((), jnp.bfloat16))
-        scores = dot_dims(key_part, queries[:, columns], 1, 1)
+        return dot_dims(key_part, queries[:, columns], 1, 1)
+
+    ahead = head_scores(0)
+    for head in range(HEADS):
+        scores = ahead
+        if head + 1 < HEADS:
+            ahead = head_scores(head + 1)
         top = jnp.max(scores, axis=0, keepdims=True)
         expo = jnp.exp2((scores - top) * (head_dim**-0.5 * LOG2E)).astype(jnp.bfloat16)
+        here = slice(head * head_dim, (head + 1) * head_dim)
         mixed = dot(jnp.concatenate([values[here, :], ones], axis=0), expo)
-        mix_ref[here, :] = (mixed[:head_dim] / mixed[head_dim : head_dim + 1]).astype(jnp.bfloat16)
+        over = 1.0 / mixed[head_dim : head_dim + 1]
+        mix_ref[here, :] = (mixed[:head_dim] * over).astype(jnp.bfloat16)
 
 
 def after_cross(own, mix_ref, gains_ref, out_ref, time_ref):
@@ -353,6 +361,22 @@
         ),
         name="mlp",
     )(*pieces, norm_gains, mlp_in, mlp_out)
+
+
+def copy_kernel(after_ref, value_ref, result_ref):
+    result_ref[...] = value_ref[...]
+
+
+def copied_after(after, value):
+    return pl.pallas_call(
+        copy_kernel,
+        out_shape=jax.ShapeDtypeStruct(value.shape, value.dtype),
+        in_specs=[pl.BlockSpec(memory_space=pl.ANY), pl.BlockSpec(memory_space=pltpu.VMEM)],
+        out_specs=pl.BlockSpec(memory_space=pltpu.VMEM),
+        compiler_params=PARAMS,
+        cost_estimate=pl.CostEstimate(flops=0, bytes_accessed=0, transcendentals=0),
+        name="copied_after",
+    )(after, value)
 
 
 def frame_swapped(value, distance):
@@ -379,6 +403,8 @@
         if d == order[-1]:
             break
         stream, proj = attend_row(own, other, *weights)
+        if d == 0:
+            weights = (copied_after(stream, norm_gains),) + weights[1:]
         streams.append(stream)
         projs.append(proj)
     count = min(row_width, 2 * LANES)
@@ -387,12 +413,16 @@
     far = order[1:]
     result = jnp.zeros(rows.shape, jnp.bfloat16)
     arrived = []
-    for pieces, first in ((early, 0), (late, count)):
-        for d in far:
-            done = mlp([pieces[d]], norm_gains, mlp_in, mlp_out)
-            arrived.append((here ^ d, first, frame_swapped(done, d)))
-    near = mlp([early[1], late[1]], norm_gains, mlp_in, mlp_out)
-    arrived.append((here ^ 1, 0, frame_swapped(near, 1)))
+
+    def send(pieces, d, first):
+        done = mlp(pieces, norm_gains, mlp_in, mlp_out)
+        arrived.append((here ^ d, first, frame_swapped(done, d)))
+
+    for d in far:
+        send([early[d]], d, 0)
+    for d in far:
+        send([late[d]], d, count)
+    send([early[1], late[1]], 1, 0)
     own_result = mlp([early[0], late[0]], norm_gains, mlp_in, mlp_out)
     arrived.insert(0, (here, 0, own_result))
     for row, first, value in arrived:

time: 74.7 us -> 73.2 us (0.980)
  Pallas kernels: 30.1 us -> 24.4 us
  waiting for transfers between devices: 20 us -> 24.2 us
    ppermute x8, waiting for transfers between devices: 18.4 us -> 22.7 us  [frame_swapped(): lax.ppermute(value, 'frame', [(i, i ^ distance) for i in range(count)])]
    pallas_call x3, Pallas kernels: 15.2 us -> 11 us  [attend_row(): pl.pallas_call(row_kernel, out_shape=(array(length, channels), array(3 *...]
    pallas_call x1, Pallas kernels: 5.16 us -> 4.32 us  [finish_rest(): pl.pallas_call(functools.partial(finish_rest_kernel, frames), out_shape=[...]
  transfers between devices with their start and end apart: 12 -> 12, of which waited for: 6 -> 6; matrix products, arithmetic and copies ran while one was open for 2% -> 2% of each run, Pallas kernels for 32% -> 26%
where the time goes in v3:
time: 73.2 us; the launch traced here: 73 us
  Pallas kernels  24.4 us (33%)
  waiting for transfers between devices  24.2 us (33%)
  starting transfers between devices  19.9 us (27%)
  local copies, waits for them, and re-layouts  4.41 us (6%)
    ppermute x8, waiting for transfers between devices, frame_swapped(): lax.ppermute(value, 'frame', [(i, i ^ distance) for i in range(count)])  22.7 us
    ppermute x8, starting transfers between devices, frame_swapped(): lax.ppermute(value, 'frame', [(i, i ^ distance) for i in range(count)])  19.3 us
    pallas_call x3, Pallas kernels, attend_row(): pl.pallas_call(row_kernel, out_shape=(array(length, channels), array(3 *...  11 us
    pallas_call x1, Pallas kernels, finish_head(): pl.pallas_call(functools.partial(finish_head_kernel, frames), out_shape=[...  4.94 us
    pallas_call x1, Pallas kernels, finish_rest(): pl.pallas_call(functools.partial(finish_rest_kernel, frames), out_shape=[...  4.32 us
    pallas_call x5, Pallas kernels, mlp(): pl.pallas_call(functools.partial(mlp_kernel, len(pieces)), out_shape=arra...  4.17 us
    ppermute x4, waiting for transfers between devices, swapped(): lax.ppermute(value, axis, [(i, i ^ 1 << bit) for i in range(lax.axis_size...  1.52 us
  transfers between devices with their start and end apart: 12, of which 6 were waited for; matrix products, arithmetic and copies ran while one was open for 2% of the time, Pallas kernels for 26%

profile of v3, /device:TPU:0, one launch (start us, length us, event | category | flops | bytes accessed | tf_op | source)
XLA Modules:
  0.0 73.0 jit_solution(18161315876714196982)
XLA Ops:
  0.0 0.0 copy-start.2
  0.0 0.0 copy-start.3
  0.0 0.0 copy-start.5
  0.0 0.0 copy-start.6
  0.0 1.4 %dynamic-slice_bitcast_fusion = (bf16[480,256]{1,0:T(8,128)(2,1)S(1)}, bf16[480,256]{1,0:T(8,128)(2,1)S(1)}, bf16[480,256]{1,0:T(8,128)(2,1)S(1)}, bf16[480,256]{1,0:T(8,128)(2,1)S(1)}) fusion(bf16[1,1,4,480,256]{4,3,2,1,0:T(8,128)(2,1)} %param.8, s32[]{:T(128)S(6)} %select_n.22, s32[]{:T(128)S(6)} %select_n.20, s32[]{:T(128)S(6)} %select_n.19, s32[]{:T(128)S(6)} %select_n.21), kind=kLoop, calls=%fused_computation.2 | loop fusion | bytes 1966096 | tf_op jit(solution)/shard_map/jit(dynamic_index_in_dim)/squeeze | solution.py:393
  1.5 0.6 collective-permute-start.3
  2.0 2.6 %collective-permute-start.2 = (bf16[480,256]{1,0:T(8,128)(2,1)S(1)}, bf16[480,256]{1,0:T(8,128)(2,1)S(1)}, u32[]{:S(2)}, u32[]{:S(2)}) collective-permute-start(bf16[480,256]{1,0:T(8,128)(2,1)S(1)} %get-tuple-element.54), channel_id=1, source_target_pairs={{0,4},{4,0},{8,12},{12,8},{1,5},{5,1},{9,13},{13,9},{2,6},{6,2},{1... | collective-permute-start | bytes 737288 | tf_op jit(solution)/shard_map/ppermute | solution.py:384
  4.7 0.0 collective-permute-done.3.other_ref
  4.7 0.0 copy-done.2
  4.7 0.0 copy-done.3
  4.7 0.0 copy-done.5
  4.7 0.0 copy-done.6
  4.7 3.7 %attend_row.3 = (bf16[480,256]{1,0:T(8,128)(2,1)S(1)}, bf16[768,480]{1,0:T(8,128)(2,1)S(1)}) custom-call(bf16[480,256]{1,0:T(8,128)(2,1)S(1)} %get-tuple-element.51.own_ref, bf16[480,256]{1,0:T(8,128)(2,1)S(1)} %collective-permute-done.3.other_ref, f32[3,256]{1,0:T(4,128)S(1)} %copy-done.6, bf16[256,768]{1,0:T(8,128)(2,1)S(1)} %copy-done.5, ...), custom_call_target="tpu_custom_call" | custom-call | flops 2327838720 | bytes 2392064 | tf_op jit(solution)/shard_map/attend_row/pallas_call | solution.py:289
  8.4 2.9 %collective-permute-done.2.own_ref = bf16[480,256]{1,0:T(8,128)(2,1)S(1)} collective-permute-done((bf16[480,256]{1,0:T(8,128)(2,1)S(1)}, bf16[480,256]{1,0:T(8,128)(2,1)S(1)}, u32[]{:S(2)}, u32[]{:S(2)}) %collective-permute-start.2) | collective-permute-done | bytes 245792 | tf_op jit(solution)/shard_map/ppermute | solution.py:384
  11.2 0.0 collective-permute-start.4
  11.2 2.8 %collective-permute-start.1 = (bf16[480,256]{1,0:T(8,128)(2,1)S(1)}, bf16[480,256]{1,0:T(8,128)(2,1)S(1)}, u32[]{:S(2)}, u32[]{:S(2)}) collective-permute-start(bf16[480,256]{1,0:T(8,128)(2,1)S(1)} %get-tuple-element.52), channel_id=1, source_target_pairs={{0,8},{4,12},{8,0},{12,4},{1,9},{5,13},{9,1},{13,5},{2,10},{6,14},... | collective-permute-start | bytes 737288 | tf_op jit(solution)/shard_map/ppermute | solution.py:384
  14.0 0.0 collective-permute-done.4.other_ref
  14.0 3.7 %attend_row.4 = (bf16[480,256]{1,0:T(8,128)(2,1)S(1)}, bf16[768,480]{1,0:T(8,128)(2,1)S(1)}) custom-call(bf16[480,256]{1,0:T(8,128)(2,1)S(1)} %collective-permute-done.2.own_ref, bf16[480,256]{1,0:T(8,128)(2,1)S(1)} %collective-permute-done.4.other_ref, f32[3,256]{1,0:T(4,128)S(1)} %copied_after.1.gains_ref, bf16[256,768]{1,0:T(8,128)(2,1)S(1)} %copy-done.5, ...), custom_call_target="tpu_custom_call" | custom-call | flops 2327838720 | bytes 2392064 | tf_op jit(solution)/shard_map/attend_row/pallas_call | solution.py:289
  17.6 8.2 %collective-permute-done.1.own_ref = bf16[480,256]{1,0:T(8,128)(2,1)S(1)} collective-permute-done((bf16[480,256]{1,0:T(8,128)(2,1)S(1)}, bf16[480,256]{1,0:T(8,128)(2,1)S(1)}, u32[]{:S(2)}, u32[]{:S(2)}) %collective-permute-start.1) | collective-permute-done | bytes 245792 | tf_op jit(solution)/shard_map/ppermute | solution.py:384
  25.9 0.0 collective-permute-start.5
  25.9 0.0 copy-start.4
  25.9 3.6 %collective-permute-start = (bf16[480,256]{1,0:T(8,128)(2,1)S(1)}, bf16[480,256]{1,0:T(8,128)(2,1)S(1)}, u32[]{:S(2)}, u32[]{:S(2)}) collective-permute-start(bf16[480,256]{1,0:T(8,128)(2,1)S(1)} %get-tuple-element.53), channel_id=1, source_target_pairs={{0,12},{4,8},{8,4},{12,0},{1,13},{5,9},{9,5},{13,1},{2,14},{6,10},... | collective-permute-start | bytes 737288 | tf_op jit(solution)/shard_map/ppermute | solution.py:384
  29.5 0.0 collective-permute-done.5.other_ref
  29.5 3.7 %attend_row.5 = (bf16[480,256]{1,0:T(8,128)(2,1)S(1)}, bf16[768,480]{1,0:T(8,128)(2,1)S(1)}) custom-call(bf16[480,256]{1,0:T(8,128)(2,1)S(1)} %collective-permute-done.1.own_ref, bf16[480,256]{1,0:T(8,128)(2,1)S(1)} %collective-permute-done.5.other_ref, f32[3,256]{1,0:T(4,128)S(1)} %copied_after.1.gains_ref, bf16[256,768]{1,0:T(8,128)(2,1)S(1)} %copy-done.5, ...), custom_call_target="tpu_custom_call" | custom-call | flops 2327838720 | bytes 2392064 | tf_op jit(solution)/shard_map/attend_row/pallas_call | solution.py:289
  33.1 3.0 %collective-permute-done.own_ref = bf16[480,256]{1,0:T(8,128)(2,1)S(1)} collective-permute-done((bf16[480,256]{1,0:T(8,128)(2,1)S(1)}, bf16[480,256]{1,0:T(8,128)(2,1)S(1)}, u32[]{:S(2)}, u32[]{:S(2)}) %collective-permute-start) | collective-permute-done | bytes 245792 | tf_op jit(solution)/shard_map/ppermute | solution.py:384
  36.1 0.0 collective-permute-start.6
  36.1 1.5 %collective-permute-done.6.other_ref = bf16[480,256]{1,0:T(8,128)(2,1)S(1)} collective-permute-done((bf16[480,256]{1,0:T(8,128)(2,1)S(1)}, bf16[480,256]{1,0:T(8,128)(2,1)S(1)}, u32[]{:S(2)}, u32[]{:S(2)}) %collective-permute-start.6) | collective-permute-done | bytes 245792 | tf_op jit(solution)/shard_map/ppermute | solution.py:18
  37.7 0.0 copy-done.4
  37.7 0.0 copy-start
  37.7 0.0 copy-start.1
  37.7 4.9 %finish_head.1 = (bf16[256,256]{1,0:T(8,128)(2,1)S(1)}, bf16[256,256]{1,0:T(8,128)(2,1)S(1)}, bf16[256,256]{1,0:T(8,128)(2,1)S(1)}, bf16[256,256]{1,0:T(8,128)(2...) custom-call(bf16[480,256]{1,0:T(8,128)(2,1)S(1)} %collective-permute-done.own_ref,, ...), custom_call_target="tpu_custom_call" | custom-call | flops 1195376640 | bytes 5242880 | tf_op jit(solution)/shard_map/finish_head/pallas_call | solution.py:323
  42.6 0.0 copy-done
  42.6 0.0 copy-done.1
  42.6 0.8 %mlp.6 = bf16[256,256]{1,0:T(8,128)(2,1)S(1)} custom-call(bf16[256,256]{1,0:T(8,128)(2,1)S(1)} %get-tuple-element.45.refs_0_, f32[3,256]{1,0:T(4,128)S(1)} %copy-done.6, bf16[256,1024]{1,0:T(8,128)(2,1)S(1)} %copy-done, bf16[1024,256]{1,0:T(8,128)(2,1)S(1)} %copy-done.1), custom_call_target="tpu_custom_call" | custom-call | flops 268435456 | bytes 1310720 | tf_op jit(solution)/shard_map/mlp/pallas_call | solution.py:353
  43.4 3.9 %collective-permute-start.7 = (bf16[256,256]{1,0:T(8,128)(2,1)S(1)}, bf16[256,256]{1,0:T(8,128)(2,1)S(1)}, u32[]{:S(2)}, u32[]{:S(2)}) collective-permute-start(bf16[256,256]{1,0:T(8,128)(2,1)S(1)} %mlp.6), channel_id=1, source_target_pairs={{0,8},{4,12},{8,0},{12,4},{1,9},{5,13},{9,1},{13,5},{2,10},{6,14},... | collective-permute-start | bytes 393224 | tf_op jit(solution)/shard_map/ppermute | solution.py:384
  47.3 4.3 %finish_rest.1 = (bf16[224,256]{1,0:T(8,128)(2,1)S(1)}, bf16[224,256]{1,0:T(8,128)(2,1)S(1)}, bf16[224,256]{1,0:T(8,128)(2,1)S(1)}, bf16[224,256]{1,0:T(8,128)(2,1)S(1)}) custom-call(bf16[480,256]{1,0:T(8,128)(2,1)S(1)} %collective-permute-done.own_ref, bf16[224,256]{1,0:T(8,128)(2,1)S(1)} %get-tuple-element.41.queries_ref, ...), custom_call_target="tpu_custom_call" | custom-call | flops 1069547520 | bytes 4718592 | tf_op jit(solution)/shard_map/finish_rest/pallas_call | solution.py:340
  51.6 1.2 %mlp.10 = bf16[480,256]{1,0:T(8,128)(2,1)S(1)} custom-call(bf16[256,256]{1,0:T(8,128)(2,1)S(1)} %get-tuple-element.49.refs_0_, bf16[224,256]{1,0:T(8,128)(2,1)S(1)} %get-tuple-element.50.refs_1_, f32[3,256]{1,0:T(4,128)S(1)} %copy-done.6, bf16[256,1024]{1,0:T(8,128)(2,1)S(1)} %copy-done, bf16[1024,256]{1,0:T(8,128)(2,1)S(1)} %copy-done.1), custom_call_target="tpu_custom_call" | custom-call | flops 503316480 | bytes 1540096 | tf_op jit(solution)/shard_map/mlp/pallas_call | solution.py:353
  52.8 0.4 collective-permute-start.11
  53.2 0.8 %mlp.7 = bf16[256,256]{1,0:T(8,128)(2,1)S(1)} custom-call(bf16[256,256]{1,0:T(8,128)(2,1)S(1)} %get-tuple-element.46.refs_0_, f32[3,256]{1,0:T(4,128)S(1)} %copy-done.6, bf16[256,1024]{1,0:T(8,128)(2,1)S(1)} %copy-done, bf16[1024,256]{1,0:T(8,128)(2,1)S(1)} %copy-done.1), custom_call_target="tpu_custom_call" | custom-call | flops 268435456 | bytes 1310720 | tf_op jit(solution)/shard_map/mlp/pallas_call | solution.py:353
  54.0 2.4 %collective-permute-start.8 = (bf16[256,256]{1,0:T(8,128)(2,1)S(1)}, bf16[256,256]{1,0:T(8,128)(2,1)S(1)}, u32[]{:S(2)}, u32[]{:S(2)}) collective-permute-start(bf16[256,256]{1,0:T(8,128)(2,1)S(1)} %mlp.7), channel_id=1, source_target_pairs={{0,12},{4,8},{8,4},{12,0},{1,13},{5,9},{9,5},{13,1},{2,14},{6,10},... | collective-permute-start | bytes 393224 | tf_op jit(solution)/shard_map/ppermute | solution.py:384
  56.4 0.7 %mlp.8 = bf16[224,256]{1,0:T(8,128)(2,1)S(1)} custom-call(bf16[224,256]{1,0:T(8,128)(2,1)S(1)} %get-tuple-element.47.refs_0_, f32[3,256]{1,0:T(4,128)S(1)} %copy-done.6, bf16[256,1024]{1,0:T(8,128)(2,1)S(1)} %copy-done, bf16[1024,256]{1,0:T(8,128)(2,1)S(1)} %copy-done.1), custom_call_target="tpu_custom_call" | custom-call | flops 234881024 | bytes 1277952 | tf_op jit(solution)/shard_map/mlp/pallas_call | solution.py:353
  57.1 0.9 %collective-permute-start.9 = (bf16[224,256]{1,0:T(8,128)(2,1)S(1)}, bf16[224,256]{1,0:T(8,128)(2,1)S(1)}, u32[]{:S(2)}, u32[]{:S(2)}) collective-permute-start(bf16[224,256]{1,0:T(8,128)(2,1)S(1)} %mlp.8), channel_id=1, source_target_pairs={{0,8},{4,12},{8,0},{12,4},{1,9},{5,13},{9,1},{13,5},{2,10},{6,14},... | collective-permute-start | bytes 344072 | tf_op jit(solution)/shard_map/ppermute | solution.py:384
  58.0 0.7 %mlp.9 = bf16[224,256]{1,0:T(8,128)(2,1)S(1)} custom-call(bf16[224,256]{1,0:T(8,128)(2,1)S(1)} %get-tuple-element.48.refs_0_, f32[3,256]{1,0:T(4,128)S(1)} %copy-done.6, bf16[256,1024]{1,0:T(8,128)(2,1)S(1)} %copy-done, bf16[1024,256]{1,0:T(8,128)(2,1)S(1)} %copy-done.1), custom_call_target="tpu_custom_call" | custom-call | flops 234881024 | bytes 1277952 | tf_op jit(solution)/shard_map/mlp/pallas_call | solution.py:353
  58.7 2.7 %collective-permute-start.10 = (bf16[224,256]{1,0:T(8,128)(2,1)S(1)}, bf16[224,256]{1,0:T(8,128)(2,1)S(1)}, u32[]{:S(2)}, u32[]{:S(2)}) collective-permute-start(bf16[224,256]{1,0:T(8,128)(2,1)S(1)} %mlp.9), channel_id=1, source_target_pairs={{0,12},{4,8},{8,4},{12,0},{1,13},{5,9},{9,5},{13,1},{2,14},{6,10},... | collective-permute-start | bytes 344072 | tf_op jit(solution)/shard_map/ppermute | solution.py:384
  61.4 0.1 broadcast_in_dim.22
  61.5 1.2 %mlp.11 = bf16[1,1,4,480,256]{4,3,2,1,0:T(8,128)(2,1)S(1)} fusion(bf16[1,1,4,480,256]{4,3,2,1,0:T(8,128)(2,1)S(1)} %broadcast_in_dim.22, s32[]{:T(128)S(6)} %select_n.22, bf16[256,256]{1,0:T(8,128)(2,1)S(1)} %get-tuple-element.40, bf16[224,256]{1,0:T(8,128)(2,1)S(1)} %get-tuple-element.44, f32[3,256]{1,0:T(4,128)S(1)} %copy-done.6, ...), kind=kCustom, calls=%fused_computation.1 | custom fusion | bytes 1544196 | tf_op jit(solution)/shard_map/mlp/pallas_call | solution.py:353
  62.7 0.0 collective-permute-done.7
  62.7 2.4 %collective-permute-done.8 = bf16[256,256]{1,0:T(8,128)(2,1)S(1)} collective-permute-done((bf16[256,256]{1,0:T(8,128)(2,1)S(1)}, bf16[256,256]{1,0:T(8,128)(2,1)S(1)}, u32[]{:S(2)}, u32[]{:S(2)}) %collective-permute-start.8) | collective-permute-done | bytes 131104 | tf_op jit(solution)/shard_map/ppermute | solution.py:384
  65.1 6.2 %collective-permute-done.9 = bf16[224,256]{1,0:T(8,128)(2,1)S(1)} collective-permute-done((bf16[224,256]{1,0:T(8,128)(2,1)S(1)}, bf16[224,256]{1,0:T(8,128)(2,1)S(1)}, u32[]{:S(2)}, u32[]{:S(2)}) %collective-permute-start.9) | collective-permute-done | bytes 114720 | tf_op jit(solution)/shard_map/ppermute | solution.py:384
  71.3 0.0 collective-permute-done.10
  71.4 0.0 copy-start.7
  71.4 0.0 collective-permute-done.11
  71.4 0.9 %copy-done.7 = bf16[1,1,4,480,256]{4,3,2,1,0:T(8,128)(2,1)} copy-done((bf16[1,1,4,480,256]{4,3,2,1,0:T(8,128)(2,1)}, bf16[1,1,4,480,256]{4,3,2,1,0:T(8,128)(2,1)S(1)}, u32[]{:S(2)}) %copy-start.7) | copy-done | bytes 983064
  72.3 0.7 bitcast_dynamic-update-slice_fusion
  (5 shorter events, 0.1 us)
Async XLA Ops:
  0.0 4.7 %copy-start.2 = (bf16[256,768]{1,0:T(8,128)(2,1)S(1)}, bf16[256,768]{1,0:T(8,128)(2,1)}, u32[]{:S(2)}) copy-start(bf16[256,768]{1,0:T(8,128)(2,1)} %time_ref.9) | copy-start | bytes 1179652
  0.0 4.7 %copy-start.3 = (bf16[256,256]{1,0:T(8,128)(2,1)S(1)}, bf16[256,256]{1,0:T(8,128)(2,1)}, u32[]{:S(2)}) copy-start(bf16[256,256]{1,0:T(8,128)(2,1)} %out_ref.9) | copy-start | bytes 393220
  0.0 4.7 %copy-start.5 = (bf16[256,768]{1,0:T(8,128)(2,1)S(1)}, bf16[256,768]{1,0:T(8,128)(2,1)}, u32[]{:S(2)}) copy-start(bf16[256,768]{1,0:T(8,128)(2,1)} %qkv_ref.7) | copy-start | bytes 1179652
  0.0 4.7 %copy-start.6 = (f32[3,256]{1,0:T(4,128)S(1)}, f32[3,256]{1,0:T(4,128)}, u32[]{:S(2)}) copy-start(f32[3,256]{1,0:T(4,128)} %refs_2_.10) | copy-start | bytes 9220
  1.5 3.2 %collective-permute-start.3 = (bf16[480,256]{1,0:T(8,128)(2,1)S(1)}, bf16[480,256]{1,0:T(8,128)(2,1)S(1)}, u32[]{:S(2)}, u32[]{:S(2)}) collective-permute-start(bf16[480,256]{1,0:T(8,128)(2,1)S(1)} %get-tuple-element.51.own_ref), channel_id=1, source_target_pairs={{0,1},{1,0},{2,3},{3,2},{4,5},{5,4},{6,7},{7,6},{8,9},{9,8},{10,11... | collective-permute-start | bytes 737288 | tf_op jit(solution)/shard_map/ppermute | solution.py:18
  2.0 9.2 %collective-permute-start.2 = (bf16[480,256]{1,0:T(8,128)(2,1)S(1)}, bf16[480,256]{1,0:T(8,128)(2,1)S(1)}, u32[]{:S(2)}, u32[]{:S(2)}) collective-permute-start(bf16[480,256]{1,0:T(8,128)(2,1)S(1)} %get-tuple-element.54), channel_id=1, source_target_pairs={{0,4},{4,0},{8,12},{12,8},{1,5},{5,1},{9,13},{13,9},{2,6},{6,2},{1... | collective-permute-start | bytes 737288 | tf_op jit(solution)/shard_map/ppermute | solution.py:384
  11.2 2.8 %collective-permute-start.4 = (bf16[480,256]{1,0:T(8,128)(2,1)S(1)}, bf16[480,256]{1,0:T(8,128)(2,1)S(1)}, u32[]{:S(2)}, u32[]{:S(2)}) collective-permute-start(bf16[480,256]{1,0:T(8,128)(2,1)S(1)} %collective-permute-done.2.own_ref), channel_id=1, source_target_pairs={{0,1},{1,0},{2,3},{3,2},{4,5},{5,4},{6,7},{7,6},{8,9},{9,8},{10,11... | collective-permute-start | bytes 737288 | tf_op jit(solution)/shard_map/ppermute | solution.py:18
  11.2 14.6 %collective-permute-start.1 = (bf16[480,256]{1,0:T(8,128)(2,1)S(1)}, bf16[480,256]{1,0:T(8,128)(2,1)S(1)}, u32[]{:S(2)}, u32[]{:S(2)}) collective-permute-start(bf16[480,256]{1,0:T(8,128)(2,1)S(1)} %get-tuple-element.52), channel_id=1, source_target_pairs={{0,8},{4,12},{8,0},{12,4},{1,9},{5,13},{9,1},{13,5},{2,10},{6,14},... | collective-permute-start | bytes 737288 | tf_op jit(solution)/shard_map/ppermute | solution.py:384
  25.9 3.6 %collective-permute-start.5 = (bf16[480,256]{1,0:T(8,128)(2,1)S(1)}, bf16[480,256]{1,0:T(8,128)(2,1)S(1)}, u32[]{:S(2)}, u32[]{:S(2)}) collective-permute-start(bf16[480,256]{1,0:T(8,128)(2,1)S(1)} %collective-permute-done.1.own_ref), channel_id=1, source_target_pairs={{0,1},{1,0},{2,3},{3,2},{4,5},{5,4},{6,7},{7,6},{8,9},{9,8},{10,11... | collective-permute-start | bytes 737288 | tf_op jit(solution)/shard_map/ppermute | solution.py:18
  25.9 11.8 %copy-start.4 = (bf16[256,256]{1,0:T(8,128)(2,1)S(1)}, bf16[256,256]{1,0:T(8,128)(2,1)}, u32[]{:S(2)}) copy-start(bf16[256,256]{1,0:T(8,128)(2,1)} %time_out_ref.3) | copy-start | bytes 393220
  25.9 10.3 %collective-permute-start = (bf16[480,256]{1,0:T(8,128)(2,1)S(1)}, bf16[480,256]{1,0:T(8,128)(2,1)S(1)}, u32[]{:S(2)}, u32[]{:S(2)}) collective-permute-start(bf16[480,256]{1,0:T(8,128)(2,1)S(1)} %get-tuple-element.53), channel_id=1, source_target_pairs={{0,12},{4,8},{8,4},{12,0},{1,13},{5,9},{9,5},{13,1},{2,14},{6,10},... | collective-permute-start | bytes 737288 | tf_op jit(solution)/shard_map/ppermute | solution.py:384
  36.1 1.5 %collective-permute-start.6 = (bf16[480,256]{1,0:T(8,128)(2,1)S(1)}, bf16[480,256]{1,0:T(8,128)(2,1)S(1)}, u32[]{:S(2)}, u32[]{:S(2)}) collective-permute-start(bf16[480,256]{1,0:T(8,128)(2,1)S(1)} %collective-permute-done.own_ref), channel_id=1, source_target_pairs={{0,1},{1,0},{2,3},{3,2},{4,5},{5,4},{6,7},{7,6},{8,9},{9,8},{10,11... | collective-permute-start | bytes 737288 | tf_op jit(solution)/shard_map/ppermute | solution.py:18
  37.7 5.0 %copy-start = (bf16[256,1024]{1,0:T(8,128)(2,1)S(1)}, bf16[256,1024]{1,0:T(8,128)(2,1)}, u32[]{:S(2)}) copy-start(bf16[256,1024]{1,0:T(8,128)(2,1)} %refs_3_.10) | copy-start | bytes 1572868
  37.7 5.0 %copy-start.1 = (bf16[1024,256]{1,0:T(8,128)(2,1)S(1)}, bf16[1024,256]{1,0:T(8,128)(2,1)}, u32[]{:S(2)}) copy-start(bf16[1024,256]{1,0:T(8,128)(2,1)} %refs_4_.2) | copy-start | bytes 1572868
  43.4 19.3 %collective-permute-start.7 = (bf16[256,256]{1,0:T(8,128)(2,1)S(1)}, bf16[256,256]{1,0:T(8,128)(2,1)S(1)}, u32[]{:S(2)}, u32[]{:S(2)}) collective-permute-start(bf16[256,256]{1,0:T(8,128)(2,1)S(1)} %mlp.6), channel_id=1, source_target_pairs={{0,8},{4,12},{8,0},{12,4},{1,9},{5,13},{9,1},{13,5},{2,10},{6,14},... | collective-permute-start | bytes 393224 | tf_op jit(solution)/shard_map/ppermute | solution.py:384
  52.8 18.6 %collective-permute-start.11 = (bf16[480,256]{1,0:T(8,128)(2,1)S(1)}, bf16[480,256]{1,0:T(8,128)(2,1)S(1)}, u32[]{:S(2)}, u32[]{:S(2)}) collective-permute-start(bf16[480,256]{1,0:T(8,128)(2,1)S(1)} %mlp.10), channel_id=1, source_target_pairs={{0,4},{4,0},{8,12},{12,8},{1,5},{5,1},{9,13},{13,9},{2,6},{6,2},{1... | collective-permute-start | bytes 737288 | tf_op jit(solution)/shard_map/ppermute | solution.py:384
  54.0 11.2 %collective-permute-start.8 = (bf16[256,256]{1,0:T(8,128)(2,1)S(1)}, bf16[256,256]{1,0:T(8,128)(2,1)S(1)}, u32[]{:S(2)}, u32[]{:S(2)}) collective-permute-start(bf16[256,256]{1,0:T(8,128)(2,1)S(1)} %mlp.7), channel_id=1, source_target_pairs={{0,12},{4,8},{8,4},{12,0},{1,13},{5,9},{9,5},{13,1},{2,14},{6,10},... | collective-permute-start | bytes 393224 | tf_op jit(solution)/shard_map/ppermute | solution.py:384
  57.1 14.2 %collective-permute-start.9 = (bf16[224,256]{1,0:T(8,128)(2,1)S(1)}, bf16[224,256]{1,0:T(8,128)(2,1)S(1)}, u32[]{:S(2)}, u32[]{:S(2)}) collective-permute-start(bf16[224,256]{1,0:T(8,128)(2,1)S(1)} %mlp.8), channel_id=1, source_target_pairs={{0,8},{4,12},{8,0},{12,4},{1,9},{5,13},{9,1},{13,5},{2,10},{6,14},... | collective-permute-start | bytes 344072 | tf_op jit(solution)/shard_map/ppermute | solution.py:384
  58.7 12.6 %collective-permute-start.10 = (bf16[224,256]{1,0:T(8,128)(2,1)S(1)}, bf16[224,256]{1,0:T(8,128)(2,1)S(1)}, u32[]{:S(2)}, u32[]{:S(2)}) collective-permute-start(bf16[224,256]{1,0:T(8,128)(2,1)S(1)} %mlp.9), channel_id=1, source_target_pairs={{0,12},{4,8},{8,4},{12,0},{1,13},{5,9},{9,5},{13,1},{2,14},{6,10},... | collective-permute-start | bytes 344072 | tf_op jit(solution)/shard_map/ppermute | solution.py:384
  71.4 0.9 %copy-start.7 = (bf16[1,1,4,480,256]{4,3,2,1,0:T(8,128)(2,1)}, bf16[1,1,4,480,256]{4,3,2,1,0:T(8,128)(2,1)S(1)}, u32[]{:S(2)}) copy-start(bf16[1,1,4,480,256]{4,3,2,1,0:T(8,128)(2,1)S(1)} %bitcast_dynamic-update-slice_fusion.4) | copy-start | bytes 2949124

commit v4 on v3

--- a/solution.py
+++ b/solution.py
@@ -395,18 +395,23 @@
         piece = lax.dynamic_index_in_dim(rows, here ^ d, 0, keepdims=False)
         own_rows[d] = frame_swapped(piece, d)
     streams, projs = [], []
-    for d in [0] + order:
-        own = own_rows[d]
-        if d:
-            own, streams[-1] = lax.optimization_barrier((own, streams[-1]))
-        other = swapped(own, "view", 0)
-        if d == order[-1]:
-            break
-        stream, proj = attend_row(own, other, *weights)
+
+    def other_view(d):
+        return swapped(own_rows[d], "view", 0)
+
+    others = {0: other_view(0)}
+    for d in range(len(order)):
+        stream, proj = attend_row(own_rows[d], others[d], *weights)
         if d == 0:
             weights = (copied_after(stream, norm_gains),) + weights[1:]
+        soon = order[:-1] if d == 0 else order[-1:] if d + 1 == len(order) else []
+        if soon:
+            *held, stream = lax.optimization_barrier((*(own_rows[e] for e in soon), stream))
+            own_rows.update(zip(soon, held))
+            others.update((e, other_view(e)) for e in soon)
         streams.append(stream)
         projs.append(proj)
+    own, other = own_rows[order[-1]], others[order[-1]]
     count = min(row_width, 2 * LANES)
     early, kept = finish_head(count, own, other, weights, time_out, projs, streams)
     late = finish_rest(own, kept, weights, time_out, projs, streams)

time: 73.2 us -> 68.5 us (0.936)
  waiting for transfers between devices: 24.2 us -> 20.8 us
  starting transfers between devices: 19.9 us -> 18.5 us
    ppermute x8, waiting for transfers between devices: 22.7 us -> 20.8 us  [frame_swapped(): lax.ppermute(value, 'frame', [(i, i ^ distance) for i in range(count)])]
    ppermute x8, starting transfers between devices: 19.3 us -> 17.7 us  [frame_swapped(): lax.ppermute(value, 'frame', [(i, i ^ distance) for i in range(count)])]
    ppermute x4, waiting for transfers between devices: 1.52 us -> 0.01 us  [swapped(): lax.ppermute(value, axis, [(i, i ^ 1 << bit) for i in range(lax.axis_size...]
  transfers between devices with their start and end apart: 12 -> 12, of which waited for: 6 -> 5; matrix products, arithmetic and copies ran while one was open for 2% -> 2% of each run, Pallas kernels for 26% -> 27%
where the time goes in v4:
time: 68.5 us; the launch traced here: 68.4 us
  Pallas kernels  24.4 us (36%)
  waiting for transfers between devices  20.8 us (30%)
  starting transfers between devices  18.5 us (27%)
  local copies, waits for them, and re-layouts  4.42 us (6%)
    ppermute x8, waiting for transfers between devices, frame_swapped(): lax.ppermute(value, 'frame', [(i, i ^ distance) for i in range(count)])  20.8 us
    ppermute x8, starting transfers between devices, frame_swapped(): lax.ppermute(value, 'frame', [(i, i ^ distance) for i in range(count)])  17.7 us
    pallas_call x3, Pallas kernels, attend_row(): pl.pallas_call(row_kernel, out_shape=(array(length, channels), array(3 *...  11 us
    pallas_call x1, Pallas kernels, finish_head(): pl.pallas_call(functools.partial(finish_head_kernel, frames), out_shape=[...  4.95 us
    pallas_call x1, Pallas kernels, finish_rest(): pl.pallas_call(functools.partial(finish_rest_kernel, frames), out_shape=[...  4.32 us
    pallas_call x5, Pallas kernels, mlp(): pl.pallas_call(functools.partial(mlp_kernel, len(pieces)), out_shape=arra...  4.17 us
    squeeze x1, local copies, waits for them, and re-layouts, local_rows(): own_rows = {0: lax.dynamic_index_in_dim(rows, here, 0, keepdims=False)}  1.44 us
  transfers between devices with their start and end apart: 12, of which 5 were waited for; matrix products, arithmetic and copies ran while one was open for 2% of the time, Pallas kernels for 27%

profile of v4, /device:TPU:0, one launch (start us, length us, event | category | flops | bytes accessed | tf_op | source)
XLA Modules:
  0.0 68.4 jit_solution(11240170537675348502)
XLA Ops:
  0.0 0.0 copy-start.2
  0.0 0.0 copy-start.3
  0.0 0.0 copy-start.5
  0.0 1.4 %dynamic-slice_bitcast_fusion = (bf16[480,256]{1,0:T(8,128)(2,1)S(1)}, bf16[480,256]{1,0:T(8,128)(2,1)S(1)}, bf16[480,256]{1,0:T(8,128)(2,1)S(1)}, bf16[480,256]{1,0:T(8,128)(2,1)S(1)}) fusion(bf16[1,1,4,480,256]{4,3,2,1,0:T(8,128)(2,1)} %param.8, s32[]{:T(128)S(6)} %select_n.22, s32[]{:T(128)S(6)} %select_n.20, s32[]{:T(128)S(6)} %select_n.19, s32[]{:T(128)S(6)} %select_n.21), kind=kLoop, calls=%fused_computation.2 | loop fusion | bytes 1966096 | tf_op jit(solution)/shard_map/jit(dynamic_index_in_dim)/squeeze | solution.py:393
  1.5 0.0 copy-start.6
  1.5 0.6 collective-permute-start.3
  2.0 2.6 %collective-permute-start.1 = (bf16[480,256]{1,0:T(8,128)(2,1)S(1)}, bf16[480,256]{1,0:T(8,128)(2,1)S(1)}, u32[]{:S(2)}, u32[]{:S(2)}) collective-permute-start(bf16[480,256]{1,0:T(8,128)(2,1)S(1)} %get-tuple-element.50), channel_id=1, source_target_pairs={{0,4},{4,0},{8,12},{12,8},{1,5},{5,1},{9,13},{13,9},{2,6},{6,2},{1... | collective-permute-start | bytes 737288 | tf_op jit(solution)/shard_map/ppermute | solution.py:384
  4.7 2.6 %collective-permute-start.2 = (bf16[480,256]{1,0:T(8,128)(2,1)S(1)}, bf16[480,256]{1,0:T(8,128)(2,1)S(1)}, u32[]{:S(2)}, u32[]{:S(2)}) collective-permute-start(bf16[480,256]{1,0:T(8,128)(2,1)S(1)} %get-tuple-element.52), channel_id=1, source_target_pairs={{0,8},{4,12},{8,0},{12,4},{1,9},{5,13},{9,1},{13,5},{2,10},{6,14},... | collective-permute-start | bytes 737288 | tf_op jit(solution)/shard_map/ppermute | solution.py:384
  7.3 0.0 collective-permute-done.3.other_ref
  7.3 0.0 copy-done.2
  7.3 0.0 copy-done.3
  7.3 0.0 copy-done.5
  7.3 0.0 copy-done.6
  7.3 3.7 %attend_row.3 = (bf16[480,256]{1,0:T(8,128)(2,1)S(1)}, bf16[768,480]{1,0:T(8,128)(2,1)S(1)}) custom-call(bf16[480,256]{1,0:T(8,128)(2,1)S(1)} %get-tuple-element.49.own_ref, bf16[480,256]{1,0:T(8,128)(2,1)S(1)} %collective-permute-done.3.other_ref, f32[3,256]{1,0:T(4,128)S(1)} %copy-done.6, bf16[256,768]{1,0:T(8,128)(2,1)S(1)} %copy-done.5, ...), custom_call_target="tpu_custom_call" | custom-call | flops 2327838720 | bytes 2392064 | tf_op jit(solution)/shard_map/attend_row/pallas_call | solution.py:289
  11.0 5.4 %collective-permute-done.1.own_ref = bf16[480,256]{1,0:T(8,128)(2,1)S(1)} collective-permute-done((bf16[480,256]{1,0:T(8,128)(2,1)S(1)}, bf16[480,256]{1,0:T(8,128)(2,1)S(1)}, u32[]{:S(2)}, u32[]{:S(2)}) %collective-permute-start.1) | collective-permute-done | bytes 245792 | tf_op jit(solution)/shard_map/ppermute | solution.py:384
  16.4 2.5 %collective-permute-done.2.own_ref = bf16[480,256]{1,0:T(8,128)(2,1)S(1)} collective-permute-done((bf16[480,256]{1,0:T(8,128)(2,1)S(1)}, bf16[480,256]{1,0:T(8,128)(2,1)S(1)}, u32[]{:S(2)}, u32[]{:S(2)}) %collective-permute-start.2) | collective-permute-done | bytes 245792 | tf_op jit(solution)/shard_map/ppermute | solution.py:384
  18.9 0.0 collective-permute-start.4
  18.9 2.5 %collective-permute-start = (bf16[480,256]{1,0:T(8,128)(2,1)S(1)}, bf16[480,256]{1,0:T(8,128)(2,1)S(1)}, u32[]{:S(2)}, u32[]{:S(2)}) collective-permute-start(bf16[480,256]{1,0:T(8,128)(2,1)S(1)} %get-tuple-element.51), channel_id=1, source_target_pairs={{0,12},{4,8},{8,4},{12,0},{1,13},{5,9},{9,5},{13,1},{2,14},{6,10},... | collective-permute-start | bytes 737288 | tf_op jit(solution)/shard_map/ppermute | solution.py:384
  21.4 0.2 collective-permute-start.6
  21.6 0.0 collective-permute-done.4.other_ref
  21.6 3.7 %attend_row.4 = (bf16[480,256]{1,0:T(8,128)(2,1)S(1)}, bf16[768,480]{1,0:T(8,128)(2,1)S(1)}) custom-call(bf16[480,256]{1,0:T(8,128)(2,1)S(1)} %collective-permute-done.2.own_ref, bf16[480,256]{1,0:T(8,128)(2,1)S(1)} %collective-permute-done.4.other_ref, f32[3,256]{1,0:T(4,128)S(1)} %copied_after.1.gains_ref, bf16[256,768]{1,0:T(8,128)(2,1)S(1)} %copy-done.5, ...), custom_call_target="tpu_custom_call" | custom-call | flops 2327838720 | bytes 2392064 | tf_op jit(solution)/shard_map/attend_row/pallas_call | solution.py:289
  25.3 3.9 %collective-permute-done.own_ref = bf16[480,256]{1,0:T(8,128)(2,1)S(1)} collective-permute-done((bf16[480,256]{1,0:T(8,128)(2,1)S(1)}, bf16[480,256]{1,0:T(8,128)(2,1)S(1)}, u32[]{:S(2)}, u32[]{:S(2)}) %collective-permute-start) | collective-permute-done | bytes 245792 | tf_op jit(solution)/shard_map/ppermute | solution.py:384
  29.2 0.0 copy-start.4
  29.2 0.0 collective-permute-start.5
  29.2 0.0 collective-permute-done.6.other_ref
  29.2 3.7 %attend_row.5 = (bf16[480,256]{1,0:T(8,128)(2,1)S(1)}, bf16[768,480]{1,0:T(8,128)(2,1)S(1)}) custom-call(bf16[480,256]{1,0:T(8,128)(2,1)S(1)} %collective-permute-done.1.own_ref, bf16[480,256]{1,0:T(8,128)(2,1)S(1)} %collective-permute-done.6.other_ref, f32[3,256]{1,0:T(4,128)S(1)} %copied_after.1.gains_ref, bf16[256,768]{1,0:T(8,128)(2,1)S(1)} %copy-done.5, ...), custom_call_target="tpu_custom_call" | custom-call | flops 2327838720 | bytes 2392064 | tf_op jit(solution)/shard_map/attend_row/pallas_call | solution.py:289
  32.8 0.0 collective-permute-done.5.other_ref
  32.9 0.0 copy-done.4
  32.9 0.0 copy-start
  32.9 0.0 copy-start.1
  32.9 4.9 %finish_head.1 = (bf16[256,256]{1,0:T(8,128)(2,1)S(1)}, bf16[256,256]{1,0:T(8,128)(2,1)S(1)}, bf16[256,256]{1,0:T(8,128)(2,1)S(1)}, bf16[256,256]{1,0:T(8,128)(2...) custom-call(bf16[480,256]{1,0:T(8,128)(2,1)S(1)} %collective-permute-done.own_ref,, ...), custom_call_target="tpu_custom_call" | custom-call | flops 1195376640 | bytes 5242880 | tf_op jit(solution)/shard_map/finish_head/pallas_call | solution.py:323
  37.8 0.0 copy-done
  37.9 0.0 copy-done.1
  37.9 0.8 %mlp.6 = bf16[256,256]{1,0:T(8,128)(2,1)S(1)} custom-call(bf16[256,256]{1,0:T(8,128)(2,1)S(1)} %get-tuple-element.43.refs_0_, f32[3,256]{1,0:T(4,128)S(1)} %copy-done.6, bf16[256,1024]{1,0:T(8,128)(2,1)S(1)} %copy-done, bf16[1024,256]{1,0:T(8,128)(2,1)S(1)} %copy-done.1), custom_call_target="tpu_custom_call" | custom-call | flops 268435456 | bytes 1310720 | tf_op jit(solution)/shard_map/mlp/pallas_call | solution.py:353
  38.6 3.8 %collective-permute-start.7 = (bf16[256,256]{1,0:T(8,128)(2,1)S(1)}, bf16[256,256]{1,0:T(8,128)(2,1)S(1)}, u32[]{:S(2)}, u32[]{:S(2)}) collective-permute-start(bf16[256,256]{1,0:T(8,128)(2,1)S(1)} %mlp.6), channel_id=1, source_target_pairs={{0,8},{4,12},{8,0},{12,4},{1,9},{5,13},{9,1},{13,5},{2,10},{6,14},... | collective-permute-start | bytes 393224 | tf_op jit(solution)/shard_map/ppermute | solution.py:384
  42.4 4.3 %finish_rest.1 = (bf16[224,256]{1,0:T(8,128)(2,1)S(1)}, bf16[224,256]{1,0:T(8,128)(2,1)S(1)}, bf16[224,256]{1,0:T(8,128)(2,1)S(1)}, bf16[224,256]{1,0:T(8,128)(2,1)S(1)}) custom-call(bf16[480,256]{1,0:T(8,128)(2,1)S(1)} %collective-permute-done.own_ref, bf16[224,256]{1,0:T(8,128)(2,1)S(1)} %get-tuple-element.39.queries_ref, ...), custom_call_target="tpu_custom_call" | custom-call | flops 1069547520 | bytes 4718592 | tf_op jit(solution)/shard_map/finish_rest/pallas_call | solution.py:340
  46.7 1.2 %mlp.10 = bf16[480,256]{1,0:T(8,128)(2,1)S(1)} custom-call(bf16[256,256]{1,0:T(8,128)(2,1)S(1)} %get-tuple-element.47.refs_0_, bf16[224,256]{1,0:T(8,128)(2,1)S(1)} %get-tuple-element.48.refs_1_, f32[3,256]{1,0:T(4,128)S(1)} %copy-done.6, bf16[256,1024]{1,0:T(8,128)(2,1)S(1)} %copy-done, bf16[1024,256]{1,0:T(8,128)(2,1)S(1)} %copy-done.1), custom_call_target="tpu_custom_call" | custom-call | flops 503316480 | bytes 1540096 | tf_op jit(solution)/shard_map/mlp/pallas_call | solution.py:353
  47.9 0.2 collective-permute-start.11
  48.1 0.8 %mlp.7 = bf16[256,256]{1,0:T(8,128)(2,1)S(1)} custom-call(bf16[256,256]{1,0:T(8,128)(2,1)S(1)} %get-tuple-element.44.refs_0_, f32[3,256]{1,0:T(4,128)S(1)} %copy-done.6, bf16[256,1024]{1,0:T(8,128)(2,1)S(1)} %copy-done, bf16[1024,256]{1,0:T(8,128)(2,1)S(1)} %copy-done.1), custom_call_target="tpu_custom_call" | custom-call | flops 268435456 | bytes 1310720 | tf_op jit(solution)/shard_map/mlp/pallas_call | solution.py:353
  48.9 2.4 %collective-permute-start.8 = (bf16[256,256]{1,0:T(8,128)(2,1)S(1)}, bf16[256,256]{1,0:T(8,128)(2,1)S(1)}, u32[]{:S(2)}, u32[]{:S(2)}) collective-permute-start(bf16[256,256]{1,0:T(8,128)(2,1)S(1)} %mlp.7), channel_id=1, source_target_pairs={{0,12},{4,8},{8,4},{12,0},{1,13},{5,9},{9,5},{13,1},{2,14},{6,10},... | collective-permute-start | bytes 393224 | tf_op jit(solution)/shard_map/ppermute | solution.py:384
  51.3 0.7 %mlp.8 = bf16[224,256]{1,0:T(8,128)(2,1)S(1)} custom-call(bf16[224,256]{1,0:T(8,128)(2,1)S(1)} %get-tuple-element.45.refs_0_, f32[3,256]{1,0:T(4,128)S(1)} %copy-done.6, bf16[256,1024]{1,0:T(8,128)(2,1)S(1)} %copy-done, bf16[1024,256]{1,0:T(8,128)(2,1)S(1)} %copy-done.1), custom_call_target="tpu_custom_call" | custom-call | flops 234881024 | bytes 1277952 | tf_op jit(solution)/shard_map/mlp/pallas_call | solution.py:353
  52.1 1.0 %collective-permute-start.9 = (bf16[224,256]{1,0:T(8,128)(2,1)S(1)}, bf16[224,256]{1,0:T(8,128)(2,1)S(1)}, u32[]{:S(2)}, u32[]{:S(2)}) collective-permute-start(bf16[224,256]{1,0:T(8,128)(2,1)S(1)} %mlp.8), channel_id=1, source_target_pairs={{0,8},{4,12},{8,0},{12,4},{1,9},{5,13},{9,1},{13,5},{2,10},{6,14},... | collective-permute-start | bytes 344072 | tf_op jit(solution)/shard_map/ppermute | solution.py:384
  53.1 0.7 %mlp.9 = bf16[224,256]{1,0:T(8,128)(2,1)S(1)} custom-call(bf16[224,256]{1,0:T(8,128)(2,1)S(1)} %get-tuple-element.46.refs_0_, f32[3,256]{1,0:T(4,128)S(1)} %copy-done.6, bf16[256,1024]{1,0:T(8,128)(2,1)S(1)} %copy-done, bf16[1024,256]{1,0:T(8,128)(2,1)S(1)} %copy-done.1), custom_call_target="tpu_custom_call" | custom-call | flops 234881024 | bytes 1277952 | tf_op jit(solution)/shard_map/mlp/pallas_call | solution.py:353
  53.8 2.6 %collective-permute-start.10 = (bf16[224,256]{1,0:T(8,128)(2,1)S(1)}, bf16[224,256]{1,0:T(8,128)(2,1)S(1)}, u32[]{:S(2)}, u32[]{:S(2)}) collective-permute-start(bf16[224,256]{1,0:T(8,128)(2,1)S(1)} %mlp.9), channel_id=1, source_target_pairs={{0,12},{4,8},{8,4},{12,0},{1,13},{5,9},{9,5},{13,1},{2,14},{6,10},... | collective-permute-start | bytes 344072 | tf_op jit(solution)/shard_map/ppermute | solution.py:384
  56.4 0.1 broadcast_in_dim.22
  56.5 1.2 %mlp.11 = bf16[1,1,4,480,256]{4,3,2,1,0:T(8,128)(2,1)S(1)} fusion(bf16[1,1,4,480,256]{4,3,2,1,0:T(8,128)(2,1)S(1)} %broadcast_in_dim.22, s32[]{:T(128)S(6)} %select_n.22, bf16[256,256]{1,0:T(8,128)(2,1)S(1)} %get-tuple-element.38, bf16[224,256]{1,0:T(8,128)(2,1)S(1)} %get-tuple-element.42, f32[3,256]{1,0:T(4,128)S(1)} %copy-done.6, ...), kind=kCustom, calls=%fused_computation.1 | custom fusion | bytes 1544196 | tf_op jit(solution)/shard_map/mlp/pallas_call | solution.py:353
  57.7 0.0 collective-permute-done.7
  57.7 2.4 %collective-permute-done.8 = bf16[256,256]{1,0:T(8,128)(2,1)S(1)} collective-permute-done((bf16[256,256]{1,0:T(8,128)(2,1)S(1)}, bf16[256,256]{1,0:T(8,128)(2,1)S(1)}, u32[]{:S(2)}, u32[]{:S(2)}) %collective-permute-start.8) | collective-permute-done | bytes 131104 | tf_op jit(solution)/shard_map/ppermute | solution.py:384
  60.1 6.6 %collective-permute-done.9 = bf16[224,256]{1,0:T(8,128)(2,1)S(1)} collective-permute-done((bf16[224,256]{1,0:T(8,128)(2,1)S(1)}, bf16[224,256]{1,0:T(8,128)(2,1)S(1)}, u32[]{:S(2)}, u32[]{:S(2)}) %collective-permute-start.9) | collective-permute-done | bytes 114720 | tf_op jit(solution)/shard_map/ppermute | solution.py:384
  66.7 0.0 collective-permute-done.10
  66.7 0.0 copy-start.7
  66.8 0.0 collective-permute-done.11
  66.8 0.9 %copy-done.7 = bf16[1,1,4,480,256]{4,3,2,1,0:T(8,128)(2,1)} copy-done((bf16[1,1,4,480,256]{4,3,2,1,0:T(8,128)(2,1)}, bf16[1,1,4,480,256]{4,3,2,1,0:T(8,128)(2,1)S(1)}, u32[]{:S(2)}) %copy-start.7) | copy-done | bytes 983064
  67.7 0.7 %bitcast_dynamic-update-slice_fusion = bf16[1,1,4,480,256]{4,3,2,1,0:T(8,128)(2,1)} fusion(bf16[1,1,4,480,256]{4,3,2,1,0:T(8,128)(2,1)} %copy-done.7, s32[]{:T(128)S(6)} %select_n.20, bf16[480,256]{1,0:T(8,128)(2,1)S(1)} %collective-permute-done.11), kind=kLoop, calls=%fused_computation | loop fusion | bytes 491524 | tf_op jit(solution)/shard_map/dynamic_update_slice | solution.py:434
  (5 shorter events, 0.1 us)
Async XLA Ops:
  0.0 7.3 %copy-start.2 = (bf16[256,768]{1,0:T(8,128)(2,1)S(1)}, bf16[256,768]{1,0:T(8,128)(2,1)}, u32[]{:S(2)}) copy-start(bf16[256,768]{1,0:T(8,128)(2,1)} %time_ref.9) | copy-start | bytes 1179652
  0.0 7.3 %copy-start.3 = (bf16[256,256]{1,0:T(8,128)(2,1)S(1)}, bf16[256,256]{1,0:T(8,128)(2,1)}, u32[]{:S(2)}) copy-start(bf16[256,256]{1,0:T(8,128)(2,1)} %out_ref.9) | copy-start | bytes 393220
  0.0 7.3 %copy-start.5 = (bf16[256,768]{1,0:T(8,128)(2,1)S(1)}, bf16[256,768]{1,0:T(8,128)(2,1)}, u32[]{:S(2)}) copy-start(bf16[256,768]{1,0:T(8,128)(2,1)} %qkv_ref.7) | copy-start | bytes 1179652
  1.5 5.8 %copy-start.6 = (f32[3,256]{1,0:T(4,128)S(1)}, f32[3,256]{1,0:T(4,128)}, u32[]{:S(2)}) copy-start(f32[3,256]{1,0:T(4,128)} %refs_2_.10) | copy-start | bytes 9220
  1.5 5.8 %collective-permute-start.3 = (bf16[480,256]{1,0:T(8,128)(2,1)S(1)}, bf16[480,256]{1,0:T(8,128)(2,1)S(1)}, u32[]{:S(2)}, u32[]{:S(2)}) collective-permute-start(bf16[480,256]{1,0:T(8,128)(2,1)S(1)} %get-tuple-element.49.own_ref), channel_id=1, source_target_pairs={{0,1},{1,0},{2,3},{3,2},{4,5},{5,4},{6,7},{7,6},{8,9},{9,8},{10,11... | collective-permute-start | bytes 737288 | tf_op jit(solution)/shard_map/ppermute | solution.py:18
  2.0 14.3 %collective-permute-start.1 = (bf16[480,256]{1,0:T(8,128)(2,1)S(1)}, bf16[480,256]{1,0:T(8,128)(2,1)S(1)}, u32[]{:S(2)}, u32[]{:S(2)}) collective-permute-start(bf16[480,256]{1,0:T(8,128)(2,1)S(1)} %get-tuple-element.50), channel_id=1, source_target_pairs={{0,4},{4,0},{8,12},{12,8},{1,5},{5,1},{9,13},{13,9},{2,6},{6,2},{1... | collective-permute-start | bytes 737288 | tf_op jit(solution)/shard_map/ppermute | solution.py:384
  4.7 14.2 %collective-permute-start.2 = (bf16[480,256]{1,0:T(8,128)(2,1)S(1)}, bf16[480,256]{1,0:T(8,128)(2,1)S(1)}, u32[]{:S(2)}, u32[]{:S(2)}) collective-permute-start(bf16[480,256]{1,0:T(8,128)(2,1)S(1)} %get-tuple-element.52), channel_id=1, source_target_pairs={{0,8},{4,12},{8,0},{12,4},{1,9},{5,13},{9,1},{13,5},{2,10},{6,14},... | collective-permute-start | bytes 737288 | tf_op jit(solution)/shard_map/ppermute | solution.py:384
  18.9 2.7 %collective-permute-start.4 = (bf16[480,256]{1,0:T(8,128)(2,1)S(1)}, bf16[480,256]{1,0:T(8,128)(2,1)S(1)}, u32[]{:S(2)}, u32[]{:S(2)}) collective-permute-start(bf16[480,256]{1,0:T(8,128)(2,1)S(1)} %collective-permute-done.2.own_ref), channel_id=1, source_target_pairs={{0,1},{1,0},{2,3},{3,2},{4,5},{5,4},{6,7},{7,6},{8,9},{9,8},{10,11... | collective-permute-start | bytes 737288 | tf_op jit(solution)/shard_map/ppermute | solution.py:18
  18.9 10.3 %collective-permute-start = (bf16[480,256]{1,0:T(8,128)(2,1)S(1)}, bf16[480,256]{1,0:T(8,128)(2,1)S(1)}, u32[]{:S(2)}, u32[]{:S(2)}) collective-permute-start(bf16[480,256]{1,0:T(8,128)(2,1)S(1)} %get-tuple-element.51), channel_id=1, source_target_pairs={{0,12},{4,8},{8,4},{12,0},{1,13},{5,9},{9,5},{13,1},{2,14},{6,10},... | collective-permute-start | bytes 737288 | tf_op jit(solution)/shard_map/ppermute | solution.py:384
  21.4 7.8 %collective-permute-start.6 = (bf16[480,256]{1,0:T(8,128)(2,1)S(1)}, bf16[480,256]{1,0:T(8,128)(2,1)S(1)}, u32[]{:S(2)}, u32[]{:S(2)}) collective-permute-start(bf16[480,256]{1,0:T(8,128)(2,1)S(1)} %collective-permute-done.1.own_ref), channel_id=1, source_target_pairs={{0,1},{1,0},{2,3},{3,2},{4,5},{5,4},{6,7},{7,6},{8,9},{9,8},{10,11... | collective-permute-start | bytes 737288 | tf_op jit(solution)/shard_map/ppermute | solution.py:18
  29.2 3.7 %copy-start.4 = (bf16[256,256]{1,0:T(8,128)(2,1)S(1)}, bf16[256,256]{1,0:T(8,128)(2,1)}, u32[]{:S(2)}) copy-start(bf16[256,256]{1,0:T(8,128)(2,1)} %time_out_ref.3) | copy-start | bytes 393220
  29.2 3.7 %collective-permute-start.5 = (bf16[480,256]{1,0:T(8,128)(2,1)S(1)}, bf16[480,256]{1,0:T(8,128)(2,1)S(1)}, u32[]{:S(2)}, u32[]{:S(2)}) collective-permute-start(bf16[480,256]{1,0:T(8,128)(2,1)S(1)} %collective-permute-done.own_ref), channel_id=1, source_target_pairs={{0,1},{1,0},{2,3},{3,2},{4,5},{5,4},{6,7},{7,6},{8,9},{9,8},{10,11... | collective-permute-start | bytes 737288 | tf_op jit(solution)/shard_map/ppermute | solution.py:18
  32.9 5.0 %copy-start = (bf16[256,1024]{1,0:T(8,128)(2,1)S(1)}, bf16[256,1024]{1,0:T(8,128)(2,1)}, u32[]{:S(2)}) copy-start(bf16[256,1024]{1,0:T(8,128)(2,1)} %refs_3_.10) | copy-start | bytes 1572868
  32.9 5.0 %copy-start.1 = (bf16[1024,256]{1,0:T(8,128)(2,1)S(1)}, bf16[1024,256]{1,0:T(8,128)(2,1)}, u32[]{:S(2)}) copy-start(bf16[1024,256]{1,0:T(8,128)(2,1)} %refs_4_.2) | copy-start | bytes 1572868
  38.6 19.0 %collective-permute-start.7 = (bf16[256,256]{1,0:T(8,128)(2,1)S(1)}, bf16[256,256]{1,0:T(8,128)(2,1)S(1)}, u32[]{:S(2)}, u32[]{:S(2)}) collective-permute-start(bf16[256,256]{1,0:T(8,128)(2,1)S(1)} %mlp.6), channel_id=1, source_target_pairs={{0,8},{4,12},{8,0},{12,4},{1,9},{5,13},{9,1},{13,5},{2,10},{6,14},... | collective-permute-start | bytes 393224 | tf_op jit(solution)/shard_map/ppermute | solution.py:384
  47.9 18.9 %collective-permute-start.11 = (bf16[480,256]{1,0:T(8,128)(2,1)S(1)}, bf16[480,256]{1,0:T(8,128)(2,1)S(1)}, u32[]{:S(2)}, u32[]{:S(2)}) collective-permute-start(bf16[480,256]{1,0:T(8,128)(2,1)S(1)} %mlp.10), channel_id=1, source_target_pairs={{0,4},{4,0},{8,12},{12,8},{1,5},{5,1},{9,13},{13,9},{2,6},{6,2},{1... | collective-permute-start | bytes 737288 | tf_op jit(solution)/shard_map/ppermute | solution.py:384
  48.9 11.2 %collective-permute-start.8 = (bf16[256,256]{1,0:T(8,128)(2,1)S(1)}, bf16[256,256]{1,0:T(8,128)(2,1)S(1)}, u32[]{:S(2)}, u32[]{:S(2)}) collective-permute-start(bf16[256,256]{1,0:T(8,128)(2,1)S(1)} %mlp.7), channel_id=1, source_target_pairs={{0,12},{4,8},{8,4},{12,0},{1,13},{5,9},{9,5},{13,1},{2,14},{6,10},... | collective-permute-start | bytes 393224 | tf_op jit(solution)/shard_map/ppermute | solution.py:384
  52.1 14.6 %collective-permute-start.9 = (bf16[224,256]{1,0:T(8,128)(2,1)S(1)}, bf16[224,256]{1,0:T(8,128)(2,1)S(1)}, u32[]{:S(2)}, u32[]{:S(2)}) collective-permute-start(bf16[224,256]{1,0:T(8,128)(2,1)S(1)} %mlp.8), channel_id=1, source_target_pairs={{0,8},{4,12},{8,0},{12,4},{1,9},{5,13},{9,1},{13,5},{2,10},{6,14},... | collective-permute-start | bytes 344072 | tf_op jit(solution)/shard_map/ppermute | solution.py:384
  53.8 12.9 %collective-permute-start.10 = (bf16[224,256]{1,0:T(8,128)(2,1)S(1)}, bf16[224,256]{1,0:T(8,128)(2,1)S(1)}, u32[]{:S(2)}, u32[]{:S(2)}) collective-permute-start(bf16[224,256]{1,0:T(8,128)(2,1)S(1)} %mlp.9), channel_id=1, source_target_pairs={{0,12},{4,8},{8,4},{12,0},{1,13},{5,9},{9,5},{13,1},{2,14},{6,10},... | collective-permute-start | bytes 344072 | tf_op jit(solution)/shard_map/ppermute | solution.py:384
  66.7 0.9 %copy-start.7 = (bf16[1,1,4,480,256]{4,3,2,1,0:T(8,128)(2,1)}, bf16[1,1,4,480,256]{4,3,2,1,0:T(8,128)(2,1)S(1)}, u32[]{:S(2)}) copy-start(bf16[1,1,4,480,256]{4,3,2,1,0:T(8,128)(2,1)S(1)} %bitcast_dynamic-update-slice_fusion.4) | copy-start | bytes 2949124

commit v5 on v4

--- a/solution.py
+++ b/solution.py
@@ -189,7 +189,7 @@
     )
 
 
-def time_heads(projs, pixels, mixes):
+def time_heads(projs, asked, mixes):
     frames = len(projs)
     channels = mixes[0].shape[0]
     head_dim = channels // HEADS
@@ -197,11 +197,11 @@
     def one_head(head, _):
         def rows(ref, part):
             start = pl.multiple_of(part * channels + head * head_dim, head_dim)
-            return ref[pl.ds(start, head_dim), pixels].astype(jnp.float32)
+            return ref[pl.ds(start, head_dim), :].astype(jnp.float32)
 
         keys = [rows(ref, 1) for ref in projs]
         values = [rows(ref, 2) for ref in projs]
-        for f in range(frames):
+        for mix, f in zip(mixes, asked):
             query = rows(projs[f], 0)
             scores = [jnp.sum(query * key, axis=0, keepdims=True) for key in keys]
             top = functools.reduce(jnp.maximum, scores)
@@ -213,57 +213,71 @@
                 part = share * values[g]
                 mixed = part if mixed is None else mixed + part
             start = pl.multiple_of(head * head_dim, head_dim)
-            mixes[f][pl.ds(start, head_dim), :] = mixed.astype(jnp.bfloat16)
+            mix[pl.ds(start, head_dim), :] = mixed.astype(jnp.bfloat16)
         return 0
 
     lax.fori_loop(0, HEADS, one_head, 0)
 
 
-def finish_tail(
-    own, mix_ref, first, gains_ref, out_ref, time_ref, time_out_ref, projs, streams, proj_ref, mixes, results
+def time_part(projs, asked, streams, mixes, time_out_ref, results):
+    time_heads(projs, asked, mixes)
+    for mix, stream, result in zip(mixes, streams, results):
+        result[...] = (
+            stream.astype(jnp.float32) + dot_dims(mix[...], time_out_ref[...], 0, 0)
+        ).astype(jnp.bfloat16)
+
+
+def queries_kernel(own_ref, gains_ref, qkv_ref, queries_ref):
+    queries_ref[...] = row_queries(own_ref, gains_ref, qkv_ref)
+
+
+def finish_head_kernel(
+    frames, own_ref, other_ref, queries_ref, gains_ref, qkv_ref, out_ref, time_ref, time_out_ref, *refs
 ):
-    count = own.shape[0]
-    stream, proj_ref[...] = after_cross(own, mix_ref, gains_ref, out_ref, time_ref)
-    time_heads(
-        [ref.at[:, first : first + count] for ref in projs] + [proj_ref], slice(None), mixes
-    )
-    before = [ref[first : first + count, :] for ref in streams] + [stream]
-    for f, result in enumerate(results):
-        result[...] = (
-            before[f].astype(jnp.float32) + dot_dims(mixes[f][...], time_out_ref[...], 0, 0)
-        ).astype(jnp.bfloat16)
-
-
-def finish_head_kernel(frames, own_ref, other_ref, gains_ref, qkv_ref, out_ref, time_ref, time_out_ref, *refs):
-    projs, streams = refs[: frames - 1], refs[frames - 1 : 2 * frames - 2]
-    refs = refs[2 * frames - 2 :]
-    results, refs = refs[:frames], refs[frames:]
-    queries_ref, keys_ref, values_ref, mix_ref, proj_ref = refs[:5]
+    projs, streams, refs = refs[: frames - 1], refs[frames - 1 : 2 * frames - 2], refs[2 * frames - 2 :]
+    results, refs = refs[: frames - 2], refs[frames - 2 :]
+    keys_ref, values_ref, proj_ref, mix_ref = refs[:4]
     count = results[0].shape[0]
-    queries = row_queries(own_ref, gains_ref, qkv_ref)
     keys, values = row_keys_values(other_ref, gains_ref, qkv_ref)
-    queries_ref[...] = queries[count:]
     keys_ref[...] = keys
     values_ref[...] = values
-    cross_heads(queries[:count], keys, values, mix_ref)
-    finish_tail(
-        own_ref[:count, :], mix_ref, 0, gains_ref, out_ref, time_ref, time_out_ref,
-        projs, streams, proj_ref, refs[5:], results,
+    cross_heads(queries_ref[:count, :], keys, values, mix_ref)
+    stream, proj_ref[...] = after_cross(own_ref[:count, :], mix_ref, gains_ref, out_ref, time_ref)
+    time_part(
+        [ref.at[:, :count] for ref in projs] + [proj_ref],
+        range(2, frames),
+        [ref[:count, :] for ref in streams[2:]] + [stream],
+        refs[4:],
+        time_out_ref,
+        results,
     )
 
 
 def finish_rest_kernel(
-    frames, own_ref, queries_ref, keys_ref, values_ref, gains_ref, out_ref, time_ref, time_out_ref, *refs
+    frames, own_ref, queries_ref, keys_ref, values_ref, head_ref, gains_ref, out_ref, time_ref, time_out_ref, *refs
 ):
-    projs, streams = refs[: frames - 1], refs[frames - 1 : 2 * frames - 2]
-    refs = refs[2 * frames - 2 :]
-    results, refs = refs[:frames], refs[frames:]
-    count = results[0].shape[0]
-    first = own_ref.shape[0] - count
-    cross_heads(queries_ref[...], keys_ref[...], values_ref[...], refs[0])
-    finish_tail(
-        own_ref[first:, :], refs[0], first, gains_ref, out_ref, time_ref, time_out_ref,
-        projs, streams, refs[1], refs[2:], results,
+    projs, streams, refs = refs[: frames - 1], refs[frames - 1 : 2 * frames - 2], refs[2 * frames - 2 :]
+    results, near, refs = refs[:frames], refs[frames : frames + 2], refs[frames + 2 :]
+    mix_ref, proj_ref, refs = refs[0], refs[1], refs[2:]
+    mixes, near_mixes = refs[:frames], refs[frames:]
+    first = near[0].shape[0]
+    cross_heads(queries_ref[first:, :], keys_ref[...], values_ref[...], mix_ref)
+    stream, proj_ref[...] = after_cross(own_ref[first:, :], mix_ref, gains_ref, out_ref, time_ref)
+    time_part(
+        [ref.at[:, first:] for ref in projs] + [proj_ref],
+        range(frames),
+        [ref[first:, :] for ref in streams] + [stream],
+        mixes,
+        time_out_ref,
+        results,
+    )
+    time_part(
+        [ref.at[:, :first] for ref in projs] + [head_ref],
+        range(2),
+        [ref[:first, :] for ref in streams[:2]],
+        near_mixes,
+        time_out_ref,
+        near,
     )
 
 
@@ -308,43 +322,112 @@
     )
 
 
-def finish_scratch(count, channels, frames):
-    return (
-        [pltpu.VMEM((channels, count), jnp.bfloat16)]
-        + [pltpu.VMEM((3 * channels, count), jnp.bfloat16)]
-        + [pltpu.VMEM((channels, count), jnp.bfloat16)] * frames
-    )
-
-
-def finish_head(count, own, other, weights, time_out, projs, streams):
-    norm_gains, cross_qkv, cross_out, time_qkv = weights
+def scratch(*shape):
+    return pltpu.VMEM(shape, jnp.bfloat16)
+
+
+def row_queries_call(own, norm_gains, cross_qkv):
+    length, channels = own.shape
+    return pl.pallas_call(
+        queries_kernel,
+        out_shape=array(length, channels),
+        compiler_params=PARAMS,
+        cost_estimate=pl.CostEstimate(
+            flops=2 * length * channels * channels,
+            bytes_accessed=4 * length * channels + 6 * channels * channels,
+            transcendentals=length,
+        ),
+        name="row_queries",
+    )(own, norm_gains, cross_qkv)
+
+
+def finish_head(count, own, other, queries, weights, time_out, projs, streams):
     length, channels = own.shape
     frames = len(projs) + 1
     out = pl.pallas_call(
         functools.partial(finish_head_kernel, frames),
-        out_shape=[array(count, channels)] * frames
-        + [array(length - count, channels), array(length, channels), array(channels, length)],
-        scratch_shapes=finish_scratch(count, channels, frames),
+        out_shape=[array(count, channels)] * (frames - 2)
+        + [array(length, channels), array(channels, length), array(3 * channels, count)],
+        scratch_shapes=[scratch(channels, count)] * (frames - 1),
         compiler_params=PARAMS,
         cost_estimate=finish_cost(length, count, channels, frames),
         name="finish_head",
-    )(own, other, norm_gains, cross_qkv, cross_out, time_qkv, time_out, *projs, *streams)
-    return out[:frames], out[frames:]
-
-
-def finish_rest(own, kept, weights, time_out, projs, streams):
+    )(own, other, queries, *weights, time_out, *projs, *streams)
+    return out[: frames - 2], out[frames - 2 :]
+
+
+def finish_rest(own, queries, kept, weights, time_out, projs, streams):
     norm_gains, _, cross_out, time_qkv = weights
     length, channels = own.shape
     frames = len(projs) + 1
-    count = kept[0].shape[0]
-    return pl.pallas_call(
+    first = kept[2].shape[1]
+    count = length - first
+    out = pl.pallas_call(
         functools.partial(finish_rest_kernel, frames),
-        out_shape=[array(count, channels)] * frames,
-        scratch_shapes=finish_scratch(count, channels, frames),
+        out_shape=[array(count, channels)] * frames + [array(first, channels)] * 2,
+        scratch_shapes=[scratch(channels, count), scratch(3 * channels, count)]
+        + [scratch(channels, count)] * frames
+        + [scratch(channels, first)] * 2,
         compiler_params=PARAMS,
         cost_estimate=finish_cost(length, count, channels, frames),
         name="finish_rest",
-    )(own, *kept, norm_gains, cross_out, time_qkv, time_out, *projs, *streams)
+    )(own, queries, *kept, norm_gains, cross_out, time_qkv, time_out, *projs, *streams)
+    return out[:frames], out[frames:]
+
+
+def take_kernel(distances, here_ref, rows_ref, *refs):
+    taken, sems = refs[:-1], refs[-1]
+    copies = [
+        pltpu.make_async_copy(rows_ref.at[here_ref[0] ^ d], ref, sems.at[i])
+        for i, (d, ref) in enumerate(zip(distances, taken))
+    ]
+    for copy in copies:
+        copy.start()
+    for copy in copies:
+        copy.wait()
+
+
+def take_rows(here, rows, distances):
+    count = len(distances)
+    return pl.pallas_call(
+        functools.partial(take_kernel, distances),
+        out_shape=[array(*rows.shape[1:])] * count,
+        in_specs=[pl.BlockSpec(memory_space=pltpu.SMEM), pl.BlockSpec(memory_space=pltpu.HBM)],
+        out_specs=[pl.BlockSpec(memory_space=pltpu.VMEM)] * count,
+        scratch_shapes=[pltpu.SemaphoreType.DMA((count,))],
+        compiler_params=PARAMS,
+        name="take_rows",
+    )(here, pltpu.with_memory_space_constraint(rows, pltpu.HBM))
+
+
+def place_kernel(places, here_ref, *refs):
+    pieces = refs[: len(places)]
+    result_ref, sems = refs[-2:]
+    copies = [
+        pltpu.make_async_copy(
+            ref, result_ref.at[here_ref[0] ^ d, pl.ds(first, ref.shape[0]), :], sems.at[i]
+        )
+        for i, ((d, first), ref) in enumerate(zip(places, pieces))
+    ]
+    for copy in copies:
+        copy.start()
+    for copy in copies:
+        copy.wait()
+
+
+def place_rows(here, pieces, places, shape, result=None):
+    held = [] if result is None else [result]
+    anywhere = pl.BlockSpec(memory_space=pl.ANY)
+    return pl.pallas_call(
+        functools.partial(place_kernel, places),
+        out_shape=array(*shape),
+        in_specs=[pl.BlockSpec(memory_space=pltpu.SMEM)] + [anywhere] * (len(pieces) + len(held)),
+        out_specs=anywhere,
+        scratch_shapes=[pltpu.SemaphoreType.DMA((len(pieces),))],
+        input_output_aliases={1 + len(pieces): 0} if held else {},
+        compiler_params=PARAMS,
+        name="place_rows",
+    )(here, *pieces, *held)
 
 
 def mlp(pieces, norm_gains, mlp_in, mlp_out):
@@ -363,22 +446,6 @@
     )(*pieces, norm_gains, mlp_in, mlp_out)
 
 
-def copy_kernel(after_ref, value_ref, result_ref):
-    result_ref[...] = value_ref[...]
-
-
-def copied_after(after, value):
-    return pl.pallas_call(
-        copy_kernel,
-        out_shape=jax.ShapeDtypeStruct(value.shape, value.dtype),
-        in_specs=[pl.BlockSpec(memory_space=pl.ANY), pl.BlockSpec(memory_space=pltpu.VMEM)],
-        out_specs=pl.BlockSpec(memory_space=pltpu.VMEM),
-        compiler_params=PARAMS,
-        cost_estimate=pl.CostEstimate(flops=0, bytes_accessed=0, transcendentals=0),
-        name="copied_after",
-    )(after, value)
-
-
 def frame_swapped(value, distance):
     count = lax.axis_size("frame")
     return lax.ppermute(value, "frame", [(i, i ^ distance) for i in range(count)])
@@ -386,14 +453,13 @@
 
 def local_rows(feats, norm_gains, cross_qkv, cross_out, time_qkv, time_out, mlp_in, mlp_out):
     rows_here, row_width, _ = feats.shape[2:]
-    here = lax.axis_index("frame")
+    here = lax.axis_index("frame").astype(jnp.int32).reshape(1)
     rows = feats[0, 0]
     weights = (norm_gains, cross_qkv, cross_out, time_qkv)
     order = list(range(1, rows_here))
-    own_rows = {0: lax.dynamic_index_in_dim(rows, here, 0, keepdims=False)}
+    own_rows = dict(enumerate(take_rows(here, rows, [0] + order)))
     for d in order:
-        piece = lax.dynamic_index_in_dim(rows, here ^ d, 0, keepdims=False)
-        own_rows[d] = frame_swapped(piece, d)
+        own_rows[d] = frame_swapped(own_rows[d], d)
     streams, projs = [], []
 
     def other_view(d):
@@ -402,36 +468,32 @@
     others = {0: other_view(0)}
     for d in range(len(order)):
         stream, proj = attend_row(own_rows[d], others[d], *weights)
-        if d == 0:
-            weights = (copied_after(stream, norm_gains),) + weights[1:]
-        soon = order[:-1] if d == 0 else order[-1:] if d + 1 == len(order) else []
-        if soon:
-            *held, stream = lax.optimization_barrier((*(own_rows[e] for e in soon), stream))
-            own_rows.update(zip(soon, held))
-            others.update((e, other_view(e)) for e in soon)
+        after = order[d]
+        own_rows[after], stream = lax.optimization_barrier((own_rows[after], stream))
+        others[after] = other_view(after)
         streams.append(stream)
         projs.append(proj)
     own, other = own_rows[order[-1]], others[order[-1]]
     count = min(row_width, 2 * LANES)
-    early, kept = finish_head(count, own, other, weights, time_out, projs, streams)
-    late = finish_rest(own, kept, weights, time_out, projs, streams)
+    queries = row_queries_call(own, norm_gains, cross_qkv)
+    early, kept = finish_head(count, own, other, queries, weights, time_out, projs, streams)
+    late, near = finish_rest(own, queries, kept, weights, time_out, projs, streams)
+
+    def send(pieces, d):
+        done = mlp(pieces, norm_gains, mlp_in, mlp_out)
+        return frame_swapped(done, d)
+
     far = order[1:]
-    result = jnp.zeros(rows.shape, jnp.bfloat16)
-    arrived = []
-
-    def send(pieces, d, first):
-        done = mlp(pieces, norm_gains, mlp_in, mlp_out)
-        arrived.append((here ^ d, first, frame_swapped(done, d)))
-
-    for d in far:
-        send([early[d]], d, 0)
-    for d in far:
-        send([late[d]], d, count)
-    send([early[1], late[1]], 1, 0)
-    own_result = mlp([early[0], late[0]], norm_gains, mlp_in, mlp_out)
-    arrived.insert(0, (here, 0, own_result))
-    for row, first, value in arrived:
-        result = lax.dynamic_update_slice(result, value[None], (row, first, 0))
+    sooner = [send([piece], d) for d, piece in zip(far, early)]
+    later = [send([late[d]], d) for d in far]
+    later.append(send([near[1], late[1]], 1))
+    own_result = mlp([near[0], late[0]], norm_gains, mlp_in, mlp_out)
+    result = place_rows(
+        here, [own_result] + sooner, [(0, 0)] + [(d, 0) for d in far], rows.shape
+    )
+    result = place_rows(
+        here, later, [(d, count) for d in far] + [(1, 0)], rows.shape, result
+    )
     return result[None, None]
 
 

time: 68.5 us -> 77.8 us (1.14)
  waiting for transfers between devices: 20.8 us -> 28.4 us
  Pallas kernels: 24.4 us -> 29.2 us
  local copies, waits for them, and re-layouts: 4.42 us -> 0.03 us
  starting transfers between devices: 18.5 us -> 19.8 us
    ppermute x8, waiting for transfers between devices: 20.8 us -> 27.2 us  [frame_swapped(): lax.ppermute(value, 'frame', [(i, i ^ distance) for i in range(count)])]
    pallas_call x1 -> x4, Pallas kernels: 0.01 us -> 3.38 us  [the longest x2 1.6 us: place_rows(): pl.pallas_call(functools.partial(place_kernel, places), out_shape=array(*...]
    ppermute x8, starting transfers between devices: 17.7 us -> 19.2 us  [frame_swapped(): lax.ppermute(value, 'frame', [(i, i ^ distance) for i in range(count)])]
    squeeze x1 -> x0, local copies, waits for them, and re-layouts: 1.44 us -> none  [local_rows(): own_rows = {0: lax.dynamic_index_in_dim(rows, here, 0, keepdims=False)}]
    pallas_call x1 -> x0, local copies, waits for them, and re-layouts: 1.18 us -> none  [mlp(): pl.pallas_call(functools.partial(mlp_kernel, len(pieces)), out_shape=arra...]
    pallas_call x5 -> x6, Pallas kernels: 4.17 us -> 5.34 us  [mlp(): pl.pallas_call(functools.partial(mlp_kernel, len(pieces)), out_shape=arra...]
    ppermute x4, waiting for transfers between devices: 0.01 us -> 1.14 us  [swapped(): lax.ppermute(value, axis, [(i, i ^ 1 << bit) for i in range(lax.axis_size...]
    pallas_call x1, Pallas kernels: 4.32 us -> 5.26 us  [finish_rest(): pl.pallas_call(functools.partial(finish_rest_kernel, frames), out_shape=[...]
  transfers between devices with their start and end apart: 12 -> 12, of which waited for: 5 -> 7; matrix products, arithmetic and copies ran while one was open for 2% -> 0% of each run, Pallas kernels for 27% -> 21%
where the time goes in v5:
time: 77.8 us; the launch traced here: 77.7 us
  Pallas kernels  29.2 us (38%)
  waiting for transfers between devices  28.4 us (37%)
  starting transfers between devices  19.8 us (25%)
    ppermute x8, waiting for transfers between devices, frame_swapped(): lax.ppermute(value, 'frame', [(i, i ^ distance) for i in range(count)])  27.2 us
    ppermute x8, starting transfers between devices, frame_swapped(): lax.ppermute(value, 'frame', [(i, i ^ distance) for i in range(count)])  19.2 us
    pallas_call x3, Pallas kernels, attend_row(): pl.pallas_call(row_kernel, out_shape=(array(length, channels), array(3 *...  11 us
    pallas_call x6, Pallas kernels, mlp(): pl.pallas_call(functools.partial(mlp_kernel, len(pieces)), out_shape=arra...  5.34 us
    pallas_call x1, Pallas kernels, finish_rest(): pl.pallas_call(functools.partial(finish_rest_kernel, frames), out_shape=[...  5.26 us
    pallas_call x1, Pallas kernels, finish_head(): pl.pallas_call(functools.partial(finish_head_kernel, frames), out_shape=[...  4.19 us
    pallas_call x2, Pallas kernels, place_rows(): pl.pallas_call(functools.partial(place_kernel, places), out_shape=array(*...  1.6 us
  transfers between devices with their start and end apart: 12, of which 7 were waited for; matrix products, arithmetic and copies ran while one was open for 0% of the time, Pallas kernels for 21%

profile of v5, /device:TPU:0, one launch (start us, length us, event | category | flops | bytes accessed | tf_op | source)
XLA Modules:
  0.0 77.7 jit_solution(6186327684223319510)
XLA Ops:
  0.0 0.0 copy-start.2
  0.0 0.0 copy-start.3
  0.0 0.0 copy-start.4
  0.0 0.0 copy-start.6
  0.0 1.4 %take_rows.1 = (bf16[480,256]{1,0:T(8,128)(2,1)S(1)}, bf16[480,256]{1,0:T(8,128)(2,1)S(1)}, bf16[480,256]{1,0:T(8,128)(2,1)S(1)}, bf16[480,256]{1,0:T(8,128)(2,1)S(1)}) custom-call(s32[1]{0:T(128)} %bitcast.here_ref, bf16[4,480,256]{2,1,0:T(8,128)(2,1)} %bitcast.3), custom_call_target="tpu_custom_call" | custom-call | tf_op jit(solution)/shard_map/take_rows/pallas_call | solution.py:392
  1.4 0.6 collective-permute-start.3
  2.0 2.6 %collective-permute-start.2 = (bf16[480,256]{1,0:T(8,128)(2,1)S(1)}, bf16[480,256]{1,0:T(8,128)(2,1)S(1)}, u32[]{:S(2)}, u32[]{:S(2)}) collective-permute-start(bf16[480,256]{1,0:T(8,128)(2,1)S(1)} %get-tuple-element.34), channel_id=1, source_target_pairs={{0,4},{4,0},{8,12},{12,8},{1,5},{5,1},{9,13},{13,9},{2,6},{6,2},{1... | collective-permute-start | bytes 737288 | tf_op jit(solution)/shard_map/ppermute | solution.py:451
  4.6 0.0 collective-permute-done.3.other_ref
  4.6 0.0 copy-done.2
  4.6 0.0 copy-done.3
  4.6 0.0 copy-done.4
  4.7 0.0 copy-done.6
  4.7 3.7 %attend_row.3 = (bf16[480,256]{1,0:T(8,128)(2,1)S(1)}, bf16[768,480]{1,0:T(8,128)(2,1)S(1)}) custom-call(bf16[480,256]{1,0:T(8,128)(2,1)S(1)} %get-tuple-element.35.own_ref, bf16[480,256]{1,0:T(8,128)(2,1)S(1)} %collective-permute-done.3.other_ref, f32[3,256]{1,0:T(4,128)S(1)} %copy-done.6, bf16[256,768]{1,0:T(8,128)(2,1)S(1)} %copy-done.2, ...), custom_call_target="tpu_custom_call" | custom-call | flops 2327838720 | bytes 2392064 | tf_op jit(solution)/shard_map/attend_row/pallas_call | solution.py:303
  8.3 2.8 %collective-permute-done.2.own_ref = bf16[480,256]{1,0:T(8,128)(2,1)S(1)} collective-permute-done((bf16[480,256]{1,0:T(8,128)(2,1)S(1)}, bf16[480,256]{1,0:T(8,128)(2,1)S(1)}, u32[]{:S(2)}, u32[]{:S(2)}) %collective-permute-start.2) | collective-permute-done | bytes 245792 | tf_op jit(solution)/shard_map/ppermute | solution.py:451
  11.2 0.0 collective-permute-start.4
  11.2 2.8 %collective-permute-start.1 = (bf16[480,256]{1,0:T(8,128)(2,1)S(1)}, bf16[480,256]{1,0:T(8,128)(2,1)S(1)}, u32[]{:S(2)}, u32[]{:S(2)}) collective-permute-start(bf16[480,256]{1,0:T(8,128)(2,1)S(1)} %get-tuple-element.33), channel_id=1, source_target_pairs={{0,8},{4,12},{8,0},{12,4},{1,9},{5,13},{9,1},{13,5},{2,10},{6,14},... | collective-permute-start | bytes 737288 | tf_op jit(solution)/shard_map/ppermute | solution.py:451
  13.9 0.0 collective-permute-done.4.other_ref
  13.9 3.7 %attend_row.4 = (bf16[480,256]{1,0:T(8,128)(2,1)S(1)}, bf16[768,480]{1,0:T(8,128)(2,1)S(1)}) custom-call(bf16[480,256]{1,0:T(8,128)(2,1)S(1)} %collective-permute-done.2.own_ref, bf16[480,256]{1,0:T(8,128)(2,1)S(1)} %collective-permute-done.4.other_ref, f32[3,256]{1,0:T(4,128)S(1)} %copy-done.6, bf16[256,768]{1,0:T(8,128)(2,1)S(1)} %copy-done.2, ...), custom_call_target="tpu_custom_call" | custom-call | flops 2327838720 | bytes 2392064 | tf_op jit(solution)/shard_map/attend_row/pallas_call | solution.py:303
  17.6 8.2 %collective-permute-done.1.own_ref = bf16[480,256]{1,0:T(8,128)(2,1)S(1)} collective-permute-done((bf16[480,256]{1,0:T(8,128)(2,1)S(1)}, bf16[480,256]{1,0:T(8,128)(2,1)S(1)}, u32[]{:S(2)}, u32[]{:S(2)}) %collective-permute-start.1) | collective-permute-done | bytes 245792 | tf_op jit(solution)/shard_map/ppermute | solution.py:451
  25.8 0.0 collective-permute-start.5
  25.8 3.6 %collective-permute-start = (bf16[480,256]{1,0:T(8,128)(2,1)S(1)}, bf16[480,256]{1,0:T(8,128)(2,1)S(1)}, u32[]{:S(2)}, u32[]{:S(2)}) collective-permute-start(bf16[480,256]{1,0:T(8,128)(2,1)S(1)} %get-tuple-element.32), channel_id=1, source_target_pairs={{0,12},{4,8},{8,4},{12,0},{1,13},{5,9},{9,5},{13,1},{2,14},{6,10},... | collective-permute-start | bytes 737288 | tf_op jit(solution)/shard_map/ppermute | solution.py:451
  29.4 0.0 collective-permute-done.5.other_ref
  29.5 3.7 %attend_row.5 = (bf16[480,256]{1,0:T(8,128)(2,1)S(1)}, bf16[768,480]{1,0:T(8,128)(2,1)S(1)}) custom-call(bf16[480,256]{1,0:T(8,128)(2,1)S(1)} %collective-permute-done.1.own_ref, bf16[480,256]{1,0:T(8,128)(2,1)S(1)} %collective-permute-done.5.other_ref, f32[3,256]{1,0:T(4,128)S(1)} %copy-done.6, bf16[256,768]{1,0:T(8,128)(2,1)S(1)} %copy-done.2, ...), custom_call_target="tpu_custom_call" | custom-call | flops 2327838720 | bytes 2392064 | tf_op jit(solution)/shard_map/attend_row/pallas_call | solution.py:303
  33.1 3.0 %collective-permute-done.own_ref = bf16[480,256]{1,0:T(8,128)(2,1)S(1)} collective-permute-done((bf16[480,256]{1,0:T(8,128)(2,1)S(1)}, bf16[480,256]{1,0:T(8,128)(2,1)S(1)}, u32[]{:S(2)}, u32[]{:S(2)}) %collective-permute-start) | collective-permute-done | bytes 245792 | tf_op jit(solution)/shard_map/ppermute | solution.py:451
  36.1 0.0 copy-start.5
  36.1 0.0 collective-permute-start.6
  36.1 0.4 row_queries.1.queries_ref
  36.5 1.1 %collective-permute-done.6.other_ref = bf16[480,256]{1,0:T(8,128)(2,1)S(1)} collective-permute-done((bf16[480,256]{1,0:T(8,128)(2,1)S(1)}, bf16[480,256]{1,0:T(8,128)(2,1)S(1)}, u32[]{:S(2)}, u32[]{:S(2)}) %collective-permute-start.6) | collective-permute-done | bytes 245792 | tf_op jit(solution)/shard_map/ppermute | solution.py:18
  37.6 0.0 copy-done.5
  37.6 4.2 %finish_head.1 = (bf16[256,256]{1,0:T(8,128)(2,1)S(1)}, bf16[256,256]{1,0:T(8,128)(2,1)S(1)}, bf16[480,256]{1,0:T(8,128)(2,1)S(1)}, bf16[256,480]{1,0:T(8,128)(2,1)S(1)}, bf16[768,256]{1,0:T(8,128)(2,1)S(1)}) custom-call(bf16[480,256]{1,0:T(8,128)(2,1)S(1)} %collective-permute-done.own_ref, bf16[480,256]{1,0:T(8,128)(2,1)S(1)} %collective-permute-done.6.other_ref, ...), custom_call_target="tpu_custom_call" | custom-call | flops 1195376640 | bytes 5242880 | tf_op jit(solution)/shard_map/finish_head/pallas_call | solution.py:347
  41.8 0.0 copy-start
  41.8 0.0 copy-start.1
  41.8 5.3 %finish_rest.1 = (bf16[224,256]{1,0:T(8,128)(2,1)S(1)}, bf16[224,256]{1,0:T(8,128)(2,1)S(1)}, bf16[224,256]{1,0:T(8,128)(2,1)S(1)}, bf16[224,256]{1,0:T(8,128)(2...) custom-call(bf16[480,256]{1,0:T(8,128)(2,1)S(1)} %collective-permute-done.own_ref, ...), custom_call_target="tpu_custom_call" | custom-call | flops 1069547520 | bytes 4718592 | tf_op jit(solution)/shard_map/finish_rest/pallas_call | solution.py:365
  47.1 0.0 copy-done
  47.1 0.0 copy-done.1
  47.1 1.2 %mlp.8 = bf16[480,256]{1,0:T(8,128)(2,1)S(1)} custom-call(bf16[256,256]{1,0:T(8,128)(2,1)S(1)} %get-tuple-element.53.refs_0_, bf16[224,256]{1,0:T(8,128)(2,1)S(1)} %get-tuple-element.54.refs_1_, f32[3,256]{1,0:T(4,128)S(1)} %copy-done.6, bf16[256,1024]{1,0:T(8,128)(2,1)S(1)} %copy-done, bf16[1024,256]{1,0:T(8,128)(2,1)S(1)} %copy-done.1), custom_call_target="tpu_custom_call" | custom-call | flops 503316480 | bytes 1540096 | tf_op jit(solution)/shard_map/mlp/pallas_call | solution.py:436
  48.3 4.2 %collective-permute-start.9 = (bf16[480,256]{1,0:T(8,128)(2,1)S(1)}, bf16[480,256]{1,0:T(8,128)(2,1)S(1)}, u32[]{:S(2)}, u32[]{:S(2)}) collective-permute-start(bf16[480,256]{1,0:T(8,128)(2,1)S(1)} %mlp.8), channel_id=1, source_target_pairs={{0,4},{4,0},{8,12},{12,8},{1,5},{5,1},{9,13},{13,9},{2,6},{6,2},{1... | collective-permute-start | bytes 737288 | tf_op jit(solution)/shard_map/ppermute | solution.py:451
  52.5 0.8 mlp.11
  53.3 1.3 %collective-permute-start.11 = (bf16[256,256]{1,0:T(8,128)(2,1)S(1)}, bf16[256,256]{1,0:T(8,128)(2,1)S(1)}, u32[]{:S(2)}, u32[]{:S(2)}) collective-permute-start(bf16[256,256]{1,0:T(8,128)(2,1)S(1)} %mlp.11), channel_id=1, source_target_pairs={{0,12},{4,8},{8,4},{12,0},{1,13},{5,9},{9,5},{13,1},{2,14},{6,10},... | collective-permute-start | bytes 393224 | tf_op jit(solution)/shard_map/ppermute | solution.py:451
  54.5 0.8 mlp.10
  55.3 0.4 collective-permute-start.10
  55.6 0.7 mlp.6
  56.4 0.7 mlp.7
  57.1 2.4 %collective-permute-start.8 = (bf16[224,256]{1,0:T(8,128)(2,1)S(1)}, bf16[224,256]{1,0:T(8,128)(2,1)S(1)}, u32[]{:S(2)}, u32[]{:S(2)}) collective-permute-start(bf16[224,256]{1,0:T(8,128)(2,1)S(1)} %mlp.7), channel_id=1, source_target_pairs={{0,12},{4,8},{8,4},{12,0},{1,13},{5,9},{9,5},{13,1},{2,14},{6,10},... | collective-permute-start | bytes 344072 | tf_op jit(solution)/shard_map/ppermute | solution.py:451
  59.5 2.0 %collective-permute-start.7 = (bf16[224,256]{1,0:T(8,128)(2,1)S(1)}, bf16[224,256]{1,0:T(8,128)(2,1)S(1)}, u32[]{:S(2)}, u32[]{:S(2)}) collective-permute-start(bf16[224,256]{1,0:T(8,128)(2,1)S(1)} %mlp.6), channel_id=1, source_target_pairs={{0,8},{4,12},{8,0},{12,4},{1,9},{5,13},{9,1},{13,5},{2,10},{6,14},... | collective-permute-start | bytes 344072 | tf_op jit(solution)/shard_map/ppermute | solution.py:451
  61.6 1.2 %mlp.9.refs_0_ = bf16[480,256]{1,0:T(8,128)(2,1)S(1)} custom-call(bf16[256,256]{1,0:T(8,128)(2,1)S(1)} %get-tuple-element.55.refs_0_, bf16[224,256]{1,0:T(8,128)(2,1)S(1)} %get-tuple-element.56.refs_1_, f32[3,256]{1,0:T(4,128)S(1)} %copy-done.6, bf16[256,1024]{1,0:T(8,128)(2,1)S(1)} %copy-done, bf16[1024,256]{1,0:T(8,128)(2,1)S(1)} %copy-done.1), custom_call_target="tpu_custom_call" | custom-call | flops 503316480 | bytes 1540096 | tf_op jit(solution)/shard_map/mlp/pallas_call | solution.py:436
  62.7 0.5 collective-permute-done.11.refs_2_
  63.3 9.4 %collective-permute-done.10.refs_1_ = bf16[256,256]{1,0:T(8,128)(2,1)S(1)} collective-permute-done((bf16[256,256]{1,0:T(8,128)(2,1)S(1)}, bf16[256,256]{1,0:T(8,128)(2,1)S(1)}, u32[]{:S(2)}, u32[]{:S(2)}) %collective-permute-start.10) | collective-permute-done | bytes 131104 | tf_op jit(solution)/shard_map/ppermute | solution.py:451
  72.6 0.8 %place_rows.2.refs_3_ = bf16[4,480,256]{2,1,0:T(8,128)(2,1)} custom-call(s32[1]{0:T(128)} %bitcast.here_ref, bf16[480,256]{1,0:T(8,128)(2,1)S(1)} %mlp.9.refs_0_, bf16[256,256]{1,0:T(8,128)(2,1)S(1)} %collective-permute-done.10.refs_1_, bf16[256,256]{1,0:T(8,128)(2,1)S(1)} %collective-permute-done.11.refs_2_), custom_call_target="tpu_custom_call" | custom-call | tf_op jit(solution)/shard_map/place_rows/pallas_call | solution.py:421
  73.5 0.0 collective-permute-done.8.refs_1_
  73.5 3.3 %collective-permute-done.7.refs_0_ = bf16[224,256]{1,0:T(8,128)(2,1)S(1)} collective-permute-done((bf16[224,256]{1,0:T(8,128)(2,1)S(1)}, bf16[224,256]{1,0:T(8,128)(2,1)S(1)}, u32[]{:S(2)}, u32[]{:S(2)}) %collective-permute-start.7) | collective-permute-done | bytes 114720 | tf_op jit(solution)/shard_map/ppermute | solution.py:451
  76.7 0.0 collective-permute-done.9.refs_2_
  76.7 0.8 %place_rows.3 = bf16[4,480,256]{2,1,0:T(8,128)(2,1)} custom-call(s32[1]{0:T(128)} %bitcast.here_ref, bf16[224,256]{1,0:T(8,128)(2,1)S(1)} %collective-permute-done.7.refs_0_, bf16[224,256]{1,0:T(8,128)(2,1)S(1)} %collective-permute-done.8.refs_1_, bf16[480,256]{1,0:T(8,128)(2,1)S(1)} %collective-permute-done.9.refs_2_, ...), custom_call_target="tpu_custom_call", output_to_operand_aliasing={{}: (4, {})} | custom-call | tf_op jit(solution)/shard_map/place_rows/pallas_call | solution.py:421
Async XLA Ops:
  0.0 4.6 %copy-start.2 = (bf16[256,768]{1,0:T(8,128)(2,1)S(1)}, bf16[256,768]{1,0:T(8,128)(2,1)}, u32[]{:S(2)}) copy-start(bf16[256,768]{1,0:T(8,128)(2,1)} %qkv_ref.9) | copy-start | bytes 1179652
  0.0 4.6 %copy-start.3 = (bf16[256,768]{1,0:T(8,128)(2,1)S(1)}, bf16[256,768]{1,0:T(8,128)(2,1)}, u32[]{:S(2)}) copy-start(bf16[256,768]{1,0:T(8,128)(2,1)} %time_ref.9) | copy-start | bytes 1179652
  0.0 4.6 %copy-start.4 = (bf16[256,256]{1,0:T(8,128)(2,1)S(1)}, bf16[256,256]{1,0:T(8,128)(2,1)}, u32[]{:S(2)}) copy-start(bf16[256,256]{1,0:T(8,128)(2,1)} %out_ref.9) | copy-start | bytes 393220
  0.0 4.7 %copy-start.6 = (f32[3,256]{1,0:T(4,128)S(1)}, f32[3,256]{1,0:T(4,128)}, u32[]{:S(2)}) copy-start(f32[3,256]{1,0:T(4,128)} %refs_1_.7) | copy-start | bytes 9220
  1.4 3.2 %collective-permute-start.3 = (bf16[480,256]{1,0:T(8,128)(2,1)S(1)}, bf16[480,256]{1,0:T(8,128)(2,1)S(1)}, u32[]{:S(2)}, u32[]{:S(2)}) collective-permute-start(bf16[480,256]{1,0:T(8,128)(2,1)S(1)} %get-tuple-element.35.own_ref), channel_id=1, source_target_pairs={{0,1},{1,0},{2,3},{3,2},{4,5},{5,4},{6,7},{7,6},{8,9},{9,8},{10,11... | collective-permute-start | bytes 737288 | tf_op jit(solution)/shard_map/ppermute | solution.py:18
  2.0 9.2 %collective-permute-start.2 = (bf16[480,256]{1,0:T(8,128)(2,1)S(1)}, bf16[480,256]{1,0:T(8,128)(2,1)S(1)}, u32[]{:S(2)}, u32[]{:S(2)}) collective-permute-start(bf16[480,256]{1,0:T(8,128)(2,1)S(1)} %get-tuple-element.34), channel_id=1, source_target_pairs={{0,4},{4,0},{8,12},{12,8},{1,5},{5,1},{9,13},{13,9},{2,6},{6,2},{1... | collective-permute-start | bytes 737288 | tf_op jit(solution)/shard_map/ppermute | solution.py:451
  11.2 2.8 %collective-permute-start.4 = (bf16[480,256]{1,0:T(8,128)(2,1)S(1)}, bf16[480,256]{1,0:T(8,128)(2,1)S(1)}, u32[]{:S(2)}, u32[]{:S(2)}) collective-permute-start(bf16[480,256]{1,0:T(8,128)(2,1)S(1)} %collective-permute-done.2.own_ref), channel_id=1, source_target_pairs={{0,1},{1,0},{2,3},{3,2},{4,5},{5,4},{6,7},{7,6},{8,9},{9,8},{10,11... | collective-permute-start | bytes 737288 | tf_op jit(solution)/shard_map/ppermute | solution.py:18
  11.2 14.6 %collective-permute-start.1 = (bf16[480,256]{1,0:T(8,128)(2,1)S(1)}, bf16[480,256]{1,0:T(8,128)(2,1)S(1)}, u32[]{:S(2)}, u32[]{:S(2)}) collective-permute-start(bf16[480,256]{1,0:T(8,128)(2,1)S(1)} %get-tuple-element.33), channel_id=1, source_target_pairs={{0,8},{4,12},{8,0},{12,4},{1,9},{5,13},{9,1},{13,5},{2,10},{6,14},... | collective-permute-start | bytes 737288 | tf_op jit(solution)/shard_map/ppermute | solution.py:451
  25.8 3.6 %collective-permute-start.5 = (bf16[480,256]{1,0:T(8,128)(2,1)S(1)}, bf16[480,256]{1,0:T(8,128)(2,1)S(1)}, u32[]{:S(2)}, u32[]{:S(2)}) collective-permute-start(bf16[480,256]{1,0:T(8,128)(2,1)S(1)} %collective-permute-done.1.own_ref), channel_id=1, source_target_pairs={{0,1},{1,0},{2,3},{3,2},{4,5},{5,4},{6,7},{7,6},{8,9},{9,8},{10,11... | collective-permute-start | bytes 737288 | tf_op jit(solution)/shard_map/ppermute | solution.py:18
  25.8 10.3 %collective-permute-start = (bf16[480,256]{1,0:T(8,128)(2,1)S(1)}, bf16[480,256]{1,0:T(8,128)(2,1)S(1)}, u32[]{:S(2)}, u32[]{:S(2)}) collective-permute-start(bf16[480,256]{1,0:T(8,128)(2,1)S(1)} %get-tuple-element.32), channel_id=1, source_target_pairs={{0,12},{4,8},{8,4},{12,0},{1,13},{5,9},{9,5},{13,1},{2,14},{6,10},... | collective-permute-start | bytes 737288 | tf_op jit(solution)/shard_map/ppermute | solution.py:451
  36.1 1.5 %copy-start.5 = (bf16[256,256]{1,0:T(8,128)(2,1)S(1)}, bf16[256,256]{1,0:T(8,128)(2,1)}, u32[]{:S(2)}) copy-start(bf16[256,256]{1,0:T(8,128)(2,1)} %time_out_ref.3) | copy-start | bytes 393220
  36.1 1.5 %collective-permute-start.6 = (bf16[480,256]{1,0:T(8,128)(2,1)S(1)}, bf16[480,256]{1,0:T(8,128)(2,1)S(1)}, u32[]{:S(2)}, u32[]{:S(2)}) collective-permute-start(bf16[480,256]{1,0:T(8,128)(2,1)S(1)} %collective-permute-done.own_ref), channel_id=1, source_target_pairs={{0,1},{1,0},{2,3},{3,2},{4,5},{5,4},{6,7},{7,6},{8,9},{9,8},{10,11... | collective-permute-start | bytes 737288 | tf_op jit(solution)/shard_map/ppermute | solution.py:18
  41.8 5.3 %copy-start = (bf16[256,1024]{1,0:T(8,128)(2,1)S(1)}, bf16[256,1024]{1,0:T(8,128)(2,1)}, u32[]{:S(2)}) copy-start(bf16[256,1024]{1,0:T(8,128)(2,1)} %refs_2_.11) | copy-start | bytes 1572868
  41.8 5.3 %copy-start.1 = (bf16[1024,256]{1,0:T(8,128)(2,1)S(1)}, bf16[1024,256]{1,0:T(8,128)(2,1)}, u32[]{:S(2)}) copy-start(bf16[1024,256]{1,0:T(8,128)(2,1)} %refs_3_.11) | copy-start | bytes 1572868
  48.3 28.4 %collective-permute-start.9 = (bf16[480,256]{1,0:T(8,128)(2,1)S(1)}, bf16[480,256]{1,0:T(8,128)(2,1)S(1)}, u32[]{:S(2)}, u32[]{:S(2)}) collective-permute-start(bf16[480,256]{1,0:T(8,128)(2,1)S(1)} %mlp.8), channel_id=1, source_target_pairs={{0,4},{4,0},{8,12},{12,8},{1,5},{5,1},{9,13},{13,9},{2,6},{6,2},{1... | collective-permute-start | bytes 737288 | tf_op jit(solution)/shard_map/ppermute | solution.py:451
  53.3 10.0 %collective-permute-start.11 = (bf16[256,256]{1,0:T(8,128)(2,1)S(1)}, bf16[256,256]{1,0:T(8,128)(2,1)S(1)}, u32[]{:S(2)}, u32[]{:S(2)}) collective-permute-start(bf16[256,256]{1,0:T(8,128)(2,1)S(1)} %mlp.11), channel_id=1, source_target_pairs={{0,12},{4,8},{8,4},{12,0},{1,13},{5,9},{9,5},{13,1},{2,14},{6,10},... | collective-permute-start | bytes 393224 | tf_op jit(solution)/shard_map/ppermute | solution.py:451
  55.3 17.4 %collective-permute-start.10 = (bf16[256,256]{1,0:T(8,128)(2,1)S(1)}, bf16[256,256]{1,0:T(8,128)(2,1)S(1)}, u32[]{:S(2)}, u32[]{:S(2)}) collective-permute-start(bf16[256,256]{1,0:T(8,128)(2,1)S(1)} %mlp.10), channel_id=1, source_target_pairs={{0,8},{4,12},{8,0},{12,4},{1,9},{5,13},{9,1},{13,5},{2,10},{6,14},... | collective-permute-start | bytes 393224 | tf_op jit(solution)/shard_map/ppermute | solution.py:451
  57.1 16.3 %collective-permute-start.8 = (bf16[224,256]{1,0:T(8,128)(2,1)S(1)}, bf16[224,256]{1,0:T(8,128)(2,1)S(1)}, u32[]{:S(2)}, u32[]{:S(2)}) collective-permute-start(bf16[224,256]{1,0:T(8,128)(2,1)S(1)} %mlp.7), channel_id=1, source_target_pairs={{0,12},{4,8},{8,4},{12,0},{1,13},{5,9},{9,5},{13,1},{2,14},{6,10},... | collective-permute-start | bytes 344072 | tf_op jit(solution)/shard_map/ppermute | solution.py:451
  59.5 17.2 %collective-permute-start.7 = (bf16[224,256]{1,0:T(8,128)(2,1)S(1)}, bf16[224,256]{1,0:T(8,128)(2,1)S(1)}, u32[]{:S(2)}, u32[]{:S(2)}) collective-permute-start(bf16[224,256]{1,0:T(8,128)(2,1)S(1)} %mlp.6), channel_id=1, source_target_pairs={{0,8},{4,12},{8,0},{12,4},{1,9},{5,13},{9,1},{13,5},{2,10},{6,14},... | collective-permute-start | bytes 344072 | tf_op jit(solution)/shard_map/ppermute | solution.py:451

commit v6 on v5

--- a/solution.py
+++ b/solution.py
@@ -180,8 +180,10 @@
     return stream, dot_dims(time_ref[...], normed, 0, 1).astype(jnp.bfloat16)
 
 
-def row_kernel(own_ref, other_ref, gains_ref, qkv_ref, out_ref, time_ref, stream_ref, proj_ref, mix_ref):
-    queries = row_queries(own_ref, gains_ref, qkv_ref)
+def row_kernel(
+    own_ref, other_ref, queries_ref, gains_ref, qkv_ref, out_ref, time_ref, stream_ref, proj_ref, mix_ref
+):
+    queries = queries_ref[...]
     keys, values = row_keys_values(other_ref, gains_ref, qkv_ref)
     cross_heads(queries, keys, values, mix_ref)
     stream_ref[...], proj_ref[...] = after_cross(
@@ -298,7 +300,7 @@
     return jax.ShapeDtypeStruct(shape, jnp.bfloat16)
 
 
-def attend_row(own, other, norm_gains, cross_qkv, cross_out, time_qkv):
+def attend_row(own, other, queries, norm_gains, cross_qkv, cross_out, time_qkv):
     length, channels = own.shape
     return pl.pallas_call(
         row_kernel,
@@ -311,7 +313,7 @@
             transcendentals=HEADS * length * length,
         ),
         name="attend_row",
-    )(own, other, norm_gains, cross_qkv, cross_out, time_qkv)
+    )(own, other, queries, norm_gains, cross_qkv, cross_out, time_qkv)
 
 
 def finish_cost(length, count, channels, frames):
@@ -457,7 +459,9 @@
     rows = feats[0, 0]
     weights = (norm_gains, cross_qkv, cross_out, time_qkv)
     order = list(range(1, rows_here))
-    own_rows = dict(enumerate(take_rows(here, rows, [0] + order)))
+    own_rows = {}
+    for taken in (order[:2], [0] + order[2:]):
+        own_rows.update(zip(taken, take_rows(here, rows, taken)))
     for d in order:
         own_rows[d] = frame_swapped(own_rows[d], d)
     streams, projs = [], []
@@ -467,7 +471,8 @@
 
     others = {0: other_view(0)}
     for d in range(len(order)):
-        stream, proj = attend_row(own_rows[d], others[d], *weights)
+        queries = row_queries_call(own_rows[d], norm_gains, cross_qkv)
+        stream, proj = attend_row(own_rows[d], others[d], queries, *weights)
         after = order[d]
         own_rows[after], stream = lax.optimization_barrier((own_rows[after], stream))
         others[after] = other_view(after)
@@ -483,8 +488,8 @@
         done = mlp(pieces, norm_gains, mlp_in, mlp_out)
         return frame_swapped(done, d)
 
-    far = order[1:]
-    sooner = [send([piece], d) for d, piece in zip(far, early)]
+    far = order[:0:-1]
+    sooner = [send([early[d - 2]], d) for d in far]
     later = [send([late[d]], d) for d in far]
     later.append(send([near[1], late[1]], 1))
     own_result = mlp([near[0], late[0]], norm_gains, mlp_in, mlp_out)
@@ -499,7 +504,7 @@
 
 def local(feats, *rest):
     rows_here = feats.shape[2]
-    whole = rows_here == lax.axis_size("frame") and rows_here & (rows_here - 1) == 0
+    whole = rows_here == lax.axis_size("frame") == 4
     return (local_rows if whole else local_pixels)(feats, *rest)
 
 

time: 77.8 us -> 78.4 us (level)
  Pallas kernels: 29.2 us -> 30.7 us
  waiting for transfers between devices: 28.4 us -> 27.2 us
    ppermute x8, waiting for transfers between devices: 27.2 us -> 26.1 us  [frame_swapped(): lax.ppermute(value, 'frame', [(i, i ^ distance) for i in range(count)])]
    pallas_call x1 -> x4, Pallas kernels: 0.37 us -> 1.47 us  [row_queries_call(): pl.pallas_call(queries_kernel, out_shape=array(length, channels), compile...]
    pallas_call x1 -> x2, Pallas kernels: 1.41 us -> 2.17 us  [take_rows(): pl.pallas_call(functools.partial(take_kernel, distances), out_shape=[arra...]
  transfers between devices with their start and end apart: 12 -> 12, of which waited for: 7 -> 6; matrix products, arithmetic and copies ran while one was open for 0% -> 0% of each run, Pallas kernels for 21% -> 23%
where the time goes in v6:
time: 78.4 us; the launch traced here: 78.2 us
  Pallas kernels  30.7 us (39%)
  waiting for transfers between devices  27.2 us (35%)
  starting transfers between devices  19.8 us (25%)
    ppermute x8, waiting for transfers between devices, frame_swapped(): lax.ppermute(value, 'frame', [(i, i ^ distance) for i in range(count)])  26.1 us
    ppermute x8, starting transfers between devices, frame_swapped(): lax.ppermute(value, 'frame', [(i, i ^ distance) for i in range(count)])  19.3 us
    pallas_call x3, Pallas kernels, attend_row(): pl.pallas_call(row_kernel, out_shape=(array(length, channels), array(3 *...  10.7 us
    pallas_call x6, Pallas kernels, mlp(): pl.pallas_call(functools.partial(mlp_kernel, len(pieces)), out_shape=arra...  5.34 us
    pallas_call x1, Pallas kernels, finish_rest(): pl.pallas_call(functools.partial(finish_rest_kernel, frames), out_shape=[...  5.26 us
    pallas_call x1, Pallas kernels, finish_head(): pl.pallas_call(functools.partial(finish_head_kernel, frames), out_shape=[...  4.19 us
    pallas_call x2, Pallas kernels, take_rows(): pl.pallas_call(functools.partial(take_kernel, distances), out_shape=[arra...  2.17 us
    pallas_call x2, Pallas kernels, place_rows(): pl.pallas_call(functools.partial(place_kernel, places), out_shape=array(*...  1.6 us
  transfers between devices with their start and end apart: 12, of which 6 were waited for; matrix products, arithmetic and copies ran while one was open for 0% of the time, Pallas kernels for 23%

profile of v6, /device:TPU:0, one launch (start us, length us, event | category | flops | bytes accessed | tf_op | source)
XLA Modules:
  0.0 78.2 jit_solution(18409246810977006622)
XLA Ops:
  0.0 1.1 %take_rows.2 = (bf16[480,256]{1,0:T(8,128)(2,1)S(1)}, bf16[480,256]{1,0:T(8,128)(2,1)S(1)}) custom-call(s32[1]{0:T(128)} %bitcast.here_ref, bf16[4,480,256]{2,1,0:T(8,128)(2,1)} %bitcast.3), custom_call_target="tpu_custom_call" | custom-call | tf_op jit(solution)/shard_map/take_rows/pallas_call | solution.py:394
  1.1 0.0 copy-start
  1.1 0.6 collective-permute-start.3
  1.7 0.0 copy-start.6
  1.7 1.1 %take_rows.3 = (bf16[480,256]{1,0:T(8,128)(2,1)S(1)}, bf16[480,256]{1,0:T(8,128)(2,1)S(1)}) custom-call(s32[1]{0:T(128)} %bitcast.here_ref, bf16[4,480,256]{2,1,0:T(8,128)(2,1)} %bitcast.4), custom_call_target="tpu_custom_call" | custom-call | tf_op jit(solution)/shard_map/take_rows/pallas_call | solution.py:394
  2.8 0.0 copy-start.3
  2.8 0.0 copy-start.4
  2.8 2.7 %collective-permute-start.2 = (bf16[480,256]{1,0:T(8,128)(2,1)S(1)}, bf16[480,256]{1,0:T(8,128)(2,1)S(1)}, u32[]{:S(2)}, u32[]{:S(2)}) collective-permute-start(bf16[480,256]{1,0:T(8,128)(2,1)S(1)} %get-tuple-element.34), channel_id=1, source_target_pairs={{0,4},{4,0},{8,12},{12,8},{1,5},{5,1},{9,13},{13,9},{2,6},{6,2},{1... | collective-permute-start | bytes 737288 | tf_op jit(solution)/shard_map/ppermute | solution.py:453
  5.5 0.0 copy-done
  5.5 0.0 copy-done.6
  5.5 0.4 row_queries.4.queries_ref
  5.8 0.0 collective-permute-done.3.other_ref
  5.8 0.0 copy-done.3
  5.9 0.0 copy-done.4
  5.9 3.6 %attend_row.3 = (bf16[480,256]{1,0:T(8,128)(2,1)S(1)}, bf16[768,480]{1,0:T(8,128)(2,1)S(1)}) custom-call(bf16[480,256]{1,0:T(8,128)(2,1)S(1)} %get-tuple-element.35.own_ref, bf16[480,256]{1,0:T(8,128)(2,1)S(1)} %collective-permute-done.3.other_ref, bf16[480,256]{1,0:T(8,128)(2,1)S(1)} %row_queries.4.queries_ref, f32[3,256]{1,0:T(4,128)S(1)} %copy-done.6, ...), custom_call_target="tpu_custom_call" | custom-call | flops 2327838720 | bytes 2392064 | tf_op jit(solution)/shard_map/attend_row/pallas_call | solution.py:305
  9.4 2.6 %collective-permute-done.2.own_ref = bf16[480,256]{1,0:T(8,128)(2,1)S(1)} collective-permute-done((bf16[480,256]{1,0:T(8,128)(2,1)S(1)}, bf16[480,256]{1,0:T(8,128)(2,1)S(1)}, u32[]{:S(2)}, u32[]{:S(2)}) %collective-permute-start.2) | collective-permute-done | bytes 245792 | tf_op jit(solution)/shard_map/ppermute | solution.py:453
  12.0 0.0 collective-permute-start.4
  12.0 2.8 %collective-permute-start.1 = (bf16[480,256]{1,0:T(8,128)(2,1)S(1)}, bf16[480,256]{1,0:T(8,128)(2,1)S(1)}, u32[]{:S(2)}, u32[]{:S(2)}) collective-permute-start(bf16[480,256]{1,0:T(8,128)(2,1)S(1)} %get-tuple-element.33), channel_id=1, source_target_pairs={{0,8},{4,12},{8,0},{12,4},{1,9},{5,13},{9,1},{13,5},{2,10},{6,14},... | collective-permute-start | bytes 737288 | tf_op jit(solution)/shard_map/ppermute | solution.py:453
  14.8 0.4 row_queries.5.queries_ref
  15.2 0.0 collective-permute-done.4.other_ref
  15.2 3.6 %attend_row.4 = (bf16[480,256]{1,0:T(8,128)(2,1)S(1)}, bf16[768,480]{1,0:T(8,128)(2,1)S(1)}) custom-call(bf16[480,256]{1,0:T(8,128)(2,1)S(1)} %collective-permute-done.2.own_ref, bf16[480,256]{1,0:T(8,128)(2,1)S(1)} %collective-permute-done.4.other_ref, bf16[480,256]{1,0:T(8,128)(2,1)S(1)} %row_queries.5.queries_ref, f32[3,256]{1,0:T(4,128)S(1)} %copy-done.6, ...), custom_call_target="tpu_custom_call" | custom-call | flops 2327838720 | bytes 2392064 | tf_op jit(solution)/shard_map/attend_row/pallas_call | solution.py:305
  18.8 7.9 %collective-permute-done.1.own_ref = bf16[480,256]{1,0:T(8,128)(2,1)S(1)} collective-permute-done((bf16[480,256]{1,0:T(8,128)(2,1)S(1)}, bf16[480,256]{1,0:T(8,128)(2,1)S(1)}, u32[]{:S(2)}, u32[]{:S(2)}) %collective-permute-start.1) | collective-permute-done | bytes 245792 | tf_op jit(solution)/shard_map/ppermute | solution.py:453
  26.7 0.0 collective-permute-start.5
  26.7 3.6 %collective-permute-start = (bf16[480,256]{1,0:T(8,128)(2,1)S(1)}, bf16[480,256]{1,0:T(8,128)(2,1)S(1)}, u32[]{:S(2)}, u32[]{:S(2)}) collective-permute-start(bf16[480,256]{1,0:T(8,128)(2,1)S(1)} %get-tuple-element.32), channel_id=1, source_target_pairs={{0,12},{4,8},{8,4},{12,0},{1,13},{5,9},{9,5},{13,1},{2,14},{6,10},... | collective-permute-start | bytes 737288 | tf_op jit(solution)/shard_map/ppermute | solution.py:453
  30.3 0.4 row_queries.6.queries_ref
  30.7 0.0 collective-permute-done.5.other_ref
  30.7 3.6 %attend_row.5 = (bf16[480,256]{1,0:T(8,128)(2,1)S(1)}, bf16[768,480]{1,0:T(8,128)(2,1)S(1)}) custom-call(bf16[480,256]{1,0:T(8,128)(2,1)S(1)} %collective-permute-done.1.own_ref, bf16[480,256]{1,0:T(8,128)(2,1)S(1)} %collective-permute-done.5.other_ref, bf16[480,256]{1,0:T(8,128)(2,1)S(1)} %row_queries.6.queries_ref, f32[3,256]{1,0:T(4,128)S(1)} %copy-done.6, ...), custom_call_target="tpu_custom_call" | custom-call | flops 2327838720 | bytes 2392064 | tf_op jit(solution)/shard_map/attend_row/pallas_call | solution.py:305
  34.3 2.7 %collective-permute-done.own_ref = bf16[480,256]{1,0:T(8,128)(2,1)S(1)} collective-permute-done((bf16[480,256]{1,0:T(8,128)(2,1)S(1)}, bf16[480,256]{1,0:T(8,128)(2,1)S(1)}, u32[]{:S(2)}, u32[]{:S(2)}) %collective-permute-start) | collective-permute-done | bytes 245792 | tf_op jit(solution)/shard_map/ppermute | solution.py:453
  37.0 0.0 copy-start.5
  37.0 0.0 collective-permute-start.6
  37.0 0.4 row_queries.7.queries_ref
  37.3 1.1 %collective-permute-done.6.other_ref = bf16[480,256]{1,0:T(8,128)(2,1)S(1)} collective-permute-done((bf16[480,256]{1,0:T(8,128)(2,1)S(1)}, bf16[480,256]{1,0:T(8,128)(2,1)S(1)}, u32[]{:S(2)}, u32[]{:S(2)}) %collective-permute-start.6) | collective-permute-done | bytes 245792 | tf_op jit(solution)/shard_map/ppermute | solution.py:18
  38.5 0.0 copy-done.5
  38.5 4.2 %finish_head.1 = (bf16[256,256]{1,0:T(8,128)(2,1)S(1)}, bf16[256,256]{1,0:T(8,128)(2,1)S(1)}, bf16[480,256]{1,0:T(8,128)(2,1)S(1)}, bf16[256,480]{1,0:T(8,128)(2,1)S(1)}, bf16[768,256]{1,0:T(8,128)(2,1)S(1)}) custom-call(bf16[480,256]{1,0:T(8,128)(2,1)S(1)} %collective-permute-done.own_ref, bf16[480,256]{1,0:T(8,128)(2,1)S(1)} %collective-permute-done.6.other_ref, ...), custom_call_target="tpu_custom_call" | custom-call | flops 1195376640 | bytes 5242880 | tf_op jit(solution)/shard_map/finish_head/pallas_call | solution.py:349
  42.7 0.0 copy-start.1
  42.7 0.0 copy-start.2
  42.7 5.3 %finish_rest.1 = (bf16[224,256]{1,0:T(8,128)(2,1)S(1)}, bf16[224,256]{1,0:T(8,128)(2,1)S(1)}, bf16[224,256]{1,0:T(8,128)(2,1)S(1)}, bf16[224,256]{1,0:T(8,128)(2...) custom-call(bf16[480,256]{1,0:T(8,128)(2,1)S(1)} %collective-permute-done.own_ref, ...), custom_call_target="tpu_custom_call" | custom-call | flops 1069547520 | bytes 4718592 | tf_op jit(solution)/shard_map/finish_rest/pallas_call | solution.py:367
  48.0 0.0 copy-done.1
  48.0 0.0 copy-done.2
  48.0 1.2 %mlp.8 = bf16[480,256]{1,0:T(8,128)(2,1)S(1)} custom-call(bf16[256,256]{1,0:T(8,128)(2,1)S(1)} %get-tuple-element.53.refs_0_, bf16[224,256]{1,0:T(8,128)(2,1)S(1)} %get-tuple-element.54.refs_1_, f32[3,256]{1,0:T(4,128)S(1)} %copy-done.6, bf16[256,1024]{1,0:T(8,128)(2,1)S(1)} %copy-done.1, bf16[1024,256]{1,0:T(8,128)(2,1)S(1)} %copy-done.2), custom_call_target="tpu_custom_call" | custom-call | flops 503316480 | bytes 1540096 | tf_op jit(solution)/shard_map/mlp/pallas_call | solution.py:438
  49.1 4.2 %collective-permute-start.9 = (bf16[480,256]{1,0:T(8,128)(2,1)S(1)}, bf16[480,256]{1,0:T(8,128)(2,1)S(1)}, u32[]{:S(2)}, u32[]{:S(2)}) collective-permute-start(bf16[480,256]{1,0:T(8,128)(2,1)S(1)} %mlp.8), channel_id=1, source_target_pairs={{0,4},{4,0},{8,12},{12,8},{1,5},{5,1},{9,13},{13,9},{2,6},{6,2},{1... | collective-permute-start | bytes 737288 | tf_op jit(solution)/shard_map/ppermute | solution.py:453
  53.3 0.8 mlp.11
  54.1 0.1 collective-permute-start.11
  54.2 0.8 mlp.10
  55.0 2.4 %collective-permute-start.10 = (bf16[256,256]{1,0:T(8,128)(2,1)S(1)}, bf16[256,256]{1,0:T(8,128)(2,1)S(1)}, u32[]{:S(2)}, u32[]{:S(2)}) collective-permute-start(bf16[256,256]{1,0:T(8,128)(2,1)S(1)} %mlp.10), channel_id=1, source_target_pairs={{0,12},{4,8},{8,4},{12,0},{1,13},{5,9},{9,5},{13,1},{2,14},{6,10},... | collective-permute-start | bytes 393224 | tf_op jit(solution)/shard_map/ppermute | solution.py:453
  57.4 0.7 mlp.6
  58.1 0.7 mlp.7
  58.9 0.9 %collective-permute-start.8 = (bf16[224,256]{1,0:T(8,128)(2,1)S(1)}, bf16[224,256]{1,0:T(8,128)(2,1)S(1)}, u32[]{:S(2)}, u32[]{:S(2)}) collective-permute-start(bf16[224,256]{1,0:T(8,128)(2,1)S(1)} %mlp.7), channel_id=1, source_target_pairs={{0,8},{4,12},{8,0},{12,4},{1,9},{5,13},{9,1},{13,5},{2,10},{6,14},... | collective-permute-start | bytes 344072 | tf_op jit(solution)/shard_map/ppermute | solution.py:453
  59.8 2.6 %collective-permute-start.7 = (bf16[224,256]{1,0:T(8,128)(2,1)S(1)}, bf16[224,256]{1,0:T(8,128)(2,1)S(1)}, u32[]{:S(2)}, u32[]{:S(2)}) collective-permute-start(bf16[224,256]{1,0:T(8,128)(2,1)S(1)} %mlp.6), channel_id=1, source_target_pairs={{0,12},{4,8},{8,4},{12,0},{1,13},{5,9},{9,5},{13,1},{2,14},{6,10},... | collective-permute-start | bytes 344072 | tf_op jit(solution)/shard_map/ppermute | solution.py:453
  62.4 1.2 %mlp.9.refs_0_ = bf16[480,256]{1,0:T(8,128)(2,1)S(1)} custom-call(bf16[256,256]{1,0:T(8,128)(2,1)S(1)} %get-tuple-element.55.refs_0_, bf16[224,256]{1,0:T(8,128)(2,1)S(1)} %get-tuple-element.56.refs_1_, f32[3,256]{1,0:T(4,128)S(1)} %copy-done.6, bf16[256,1024]{1,0:T(8,128)(2,1)S(1)} %copy-done.1, bf16[1024,256]{1,0:T(8,128)(2,1)S(1)} %copy-done.2), custom_call_target="tpu_custom_call" | custom-call | flops 503316480 | bytes 1540096 | tf_op jit(solution)/shard_map/mlp/pallas_call | solution.py:438
  63.6 8.4 %collective-permute-done.11.refs_2_ = bf16[256,256]{1,0:T(8,128)(2,1)S(1)} collective-permute-done((bf16[256,256]{1,0:T(8,128)(2,1)S(1)}, bf16[256,256]{1,0:T(8,128)(2,1)S(1)}, u32[]{:S(2)}, u32[]{:S(2)}) %collective-permute-start.11) | collective-permute-done | bytes 131104 | tf_op jit(solution)/shard_map/ppermute | solution.py:453
  72.0 0.0 collective-permute-done.10.refs_1_
  72.0 0.8 %place_rows.2.refs_3_ = bf16[4,480,256]{2,1,0:T(8,128)(2,1)} custom-call(s32[1]{0:T(128)} %bitcast.here_ref, bf16[480,256]{1,0:T(8,128)(2,1)S(1)} %mlp.9.refs_0_, bf16[256,256]{1,0:T(8,128)(2,1)S(1)} %collective-permute-done.10.refs_1_, bf16[256,256]{1,0:T(8,128)(2,1)S(1)} %collective-permute-done.11.refs_2_), custom_call_target="tpu_custom_call" | custom-call | tf_op jit(solution)/shard_map/place_rows/pallas_call | solution.py:423
  72.8 4.5 %collective-permute-done.8.refs_1_ = bf16[224,256]{1,0:T(8,128)(2,1)S(1)} collective-permute-done((bf16[224,256]{1,0:T(8,128)(2,1)S(1)}, bf16[224,256]{1,0:T(8,128)(2,1)S(1)}, u32[]{:S(2)}, u32[]{:S(2)}) %collective-permute-start.8) | collective-permute-done | bytes 114720 | tf_op jit(solution)/shard_map/ppermute | solution.py:453
  77.2 0.0 collective-permute-done.7.refs_0_
  77.2 0.0 collective-permute-done.9.refs_2_
  77.3 0.8 %place_rows.3 = bf16[4,480,256]{2,1,0:T(8,128)(2,1)} custom-call(s32[1]{0:T(128)} %bitcast.here_ref, bf16[224,256]{1,0:T(8,128)(2,1)S(1)} %collective-permute-done.7.refs_0_, bf16[224,256]{1,0:T(8,128)(2,1)S(1)} %collective-permute-done.8.refs_1_, bf16[480,256]{1,0:T(8,128)(2,1)S(1)} %collective-permute-done.9.refs_2_, ...), custom_call_target="tpu_custom_call", output_to_operand_aliasing={{}: (4, {})} | custom-call | tf_op jit(solution)/shard_map/place_rows/pallas_call | solution.py:423
Async XLA Ops:
  1.1 4.4 %copy-start = (bf16[256,768]{1,0:T(8,128)(2,1)S(1)}, bf16[256,768]{1,0:T(8,128)(2,1)}, u32[]{:S(2)}) copy-start(bf16[256,768]{1,0:T(8,128)(2,1)} %qkv_ref.15) | copy-start | bytes 1179652
  1.1 4.7 %collective-permute-start.3 = (bf16[480,256]{1,0:T(8,128)(2,1)S(1)}, bf16[480,256]{1,0:T(8,128)(2,1)S(1)}, u32[]{:S(2)}, u32[]{:S(2)}) collective-permute-start(bf16[480,256]{1,0:T(8,128)(2,1)S(1)} %get-tuple-element.35.own_ref), channel_id=1, source_target_pairs={{0,1},{1,0},{2,3},{3,2},{4,5},{5,4},{6,7},{7,6},{8,9},{9,8},{10,11... | collective-permute-start | bytes 737288 | tf_op jit(solution)/shard_map/ppermute | solution.py:18
  1.7 3.8 %copy-start.6 = (f32[3,256]{1,0:T(4,128)S(1)}, f32[3,256]{1,0:T(4,128)}, u32[]{:S(2)}) copy-start(f32[3,256]{1,0:T(4,128)} %refs_1_.7) | copy-start | bytes 9220
  2.8 3.1 %copy-start.3 = (bf16[256,768]{1,0:T(8,128)(2,1)S(1)}, bf16[256,768]{1,0:T(8,128)(2,1)}, u32[]{:S(2)}) copy-start(bf16[256,768]{1,0:T(8,128)(2,1)} %time_ref.9) | copy-start | bytes 1179652
  2.8 3.1 %copy-start.4 = (bf16[256,256]{1,0:T(8,128)(2,1)S(1)}, bf16[256,256]{1,0:T(8,128)(2,1)}, u32[]{:S(2)}) copy-start(bf16[256,256]{1,0:T(8,128)(2,1)} %out_ref.9) | copy-start | bytes 393220
  2.8 9.3 %collective-permute-start.2 = (bf16[480,256]{1,0:T(8,128)(2,1)S(1)}, bf16[480,256]{1,0:T(8,128)(2,1)S(1)}, u32[]{:S(2)}, u32[]{:S(2)}) collective-permute-start(bf16[480,256]{1,0:T(8,128)(2,1)S(1)} %get-tuple-element.34), channel_id=1, source_target_pairs={{0,4},{4,0},{8,12},{12,8},{1,5},{5,1},{9,13},{13,9},{2,6},{6,2},{1... | collective-permute-start | bytes 737288 | tf_op jit(solution)/shard_map/ppermute | solution.py:453
  12.0 3.1 %collective-permute-start.4 = (bf16[480,256]{1,0:T(8,128)(2,1)S(1)}, bf16[480,256]{1,0:T(8,128)(2,1)S(1)}, u32[]{:S(2)}, u32[]{:S(2)}) collective-permute-start(bf16[480,256]{1,0:T(8,128)(2,1)S(1)} %collective-permute-done.2.own_ref), channel_id=1, source_target_pairs={{0,1},{1,0},{2,3},{3,2},{4,5},{5,4},{6,7},{7,6},{8,9},{9,8},{10,11... | collective-permute-start | bytes 737288 | tf_op jit(solution)/shard_map/ppermute | solution.py:18
  12.0 14.6 %collective-permute-start.1 = (bf16[480,256]{1,0:T(8,128)(2,1)S(1)}, bf16[480,256]{1,0:T(8,128)(2,1)S(1)}, u32[]{:S(2)}, u32[]{:S(2)}) collective-permute-start(bf16[480,256]{1,0:T(8,128)(2,1)S(1)} %get-tuple-element.33), channel_id=1, source_target_pairs={{0,8},{4,12},{8,0},{12,4},{1,9},{5,13},{9,1},{13,5},{2,10},{6,14},... | collective-permute-start | bytes 737288 | tf_op jit(solution)/shard_map/ppermute | solution.py:453
  26.7 4.0 %collective-permute-start.5 = (bf16[480,256]{1,0:T(8,128)(2,1)S(1)}, bf16[480,256]{1,0:T(8,128)(2,1)S(1)}, u32[]{:S(2)}, u32[]{:S(2)}) collective-permute-start(bf16[480,256]{1,0:T(8,128)(2,1)S(1)} %collective-permute-done.1.own_ref), channel_id=1, source_target_pairs={{0,1},{1,0},{2,3},{3,2},{4,5},{5,4},{6,7},{7,6},{8,9},{9,8},{10,11... | collective-permute-start | bytes 737288 | tf_op jit(solution)/shard_map/ppermute | solution.py:18
  26.7 10.3 %collective-permute-start = (bf16[480,256]{1,0:T(8,128)(2,1)S(1)}, bf16[480,256]{1,0:T(8,128)(2,1)S(1)}, u32[]{:S(2)}, u32[]{:S(2)}) collective-permute-start(bf16[480,256]{1,0:T(8,128)(2,1)S(1)} %get-tuple-element.32), channel_id=1, source_target_pairs={{0,12},{4,8},{8,4},{12,0},{1,13},{5,9},{9,5},{13,1},{2,14},{6,10},... | collective-permute-start | bytes 737288 | tf_op jit(solution)/shard_map/ppermute | solution.py:453
  37.0 1.5 %copy-start.5 = (bf16[256,256]{1,0:T(8,128)(2,1)S(1)}, bf16[256,256]{1,0:T(8,128)(2,1)}, u32[]{:S(2)}) copy-start(bf16[256,256]{1,0:T(8,128)(2,1)} %time_out_ref.3) | copy-start | bytes 393220
  37.0 1.5 %collective-permute-start.6 = (bf16[480,256]{1,0:T(8,128)(2,1)S(1)}, bf16[480,256]{1,0:T(8,128)(2,1)S(1)}, u32[]{:S(2)}, u32[]{:S(2)}) collective-permute-start(bf16[480,256]{1,0:T(8,128)(2,1)S(1)} %collective-permute-done.own_ref), channel_id=1, source_target_pairs={{0,1},{1,0},{2,3},{3,2},{4,5},{5,4},{6,7},{7,6},{8,9},{9,8},{10,11... | collective-permute-start | bytes 737288 | tf_op jit(solution)/shard_map/ppermute | solution.py:18
  42.7 5.3 %copy-start.1 = (bf16[256,1024]{1,0:T(8,128)(2,1)S(1)}, bf16[256,1024]{1,0:T(8,128)(2,1)}, u32[]{:S(2)}) copy-start(bf16[256,1024]{1,0:T(8,128)(2,1)} %refs_2_.11) | copy-start | bytes 1572868
  42.7 5.3 %copy-start.2 = (bf16[1024,256]{1,0:T(8,128)(2,1)S(1)}, bf16[1024,256]{1,0:T(8,128)(2,1)}, u32[]{:S(2)}) copy-start(bf16[1024,256]{1,0:T(8,128)(2,1)} %refs_3_.11) | copy-start | bytes 1572868
  49.1 28.1 %collective-permute-start.9 = (bf16[480,256]{1,0:T(8,128)(2,1)S(1)}, bf16[480,256]{1,0:T(8,128)(2,1)S(1)}, u32[]{:S(2)}, u32[]{:S(2)}) collective-permute-start(bf16[480,256]{1,0:T(8,128)(2,1)S(1)} %mlp.8), channel_id=1, source_target_pairs={{0,4},{4,0},{8,12},{12,8},{1,5},{5,1},{9,13},{13,9},{2,6},{6,2},{1... | collective-permute-start | bytes 737288 | tf_op jit(solution)/shard_map/ppermute | solution.py:453
  54.1 17.9 %collective-permute-start.11 = (bf16[256,256]{1,0:T(8,128)(2,1)S(1)}, bf16[256,256]{1,0:T(8,128)(2,1)S(1)}, u32[]{:S(2)}, u32[]{:S(2)}) collective-permute-start(bf16[256,256]{1,0:T(8,128)(2,1)S(1)} %mlp.11), channel_id=1, source_target_pairs={{0,8},{4,12},{8,0},{12,4},{1,9},{5,13},{9,1},{13,5},{2,10},{6,14},... | collective-permute-start | bytes 393224 | tf_op jit(solution)/shard_map/ppermute | solution.py:453
  55.0 17.0 %collective-permute-start.10 = (bf16[256,256]{1,0:T(8,128)(2,1)S(1)}, bf16[256,256]{1,0:T(8,128)(2,1)S(1)}, u32[]{:S(2)}, u32[]{:S(2)}) collective-permute-start(bf16[256,256]{1,0:T(8,128)(2,1)S(1)} %mlp.10), channel_id=1, source_target_pairs={{0,12},{4,8},{8,4},{12,0},{1,13},{5,9},{9,5},{13,1},{2,14},{6,10},... | collective-permute-start | bytes 393224 | tf_op jit(solution)/shard_map/ppermute | solution.py:453
  58.9 18.4 %collective-permute-start.8 = (bf16[224,256]{1,0:T(8,128)(2,1)S(1)}, bf16[224,256]{1,0:T(8,128)(2,1)S(1)}, u32[]{:S(2)}, u32[]{:S(2)}) collective-permute-start(bf16[224,256]{1,0:T(8,128)(2,1)S(1)} %mlp.7), channel_id=1, source_target_pairs={{0,8},{4,12},{8,0},{12,4},{1,9},{5,13},{9,1},{13,5},{2,10},{6,14},... | collective-permute-start | bytes 344072 | tf_op jit(solution)/shard_map/ppermute | solution.py:453
  59.8 17.5 %collective-permute-start.7 = (bf16[224,256]{1,0:T(8,128)(2,1)S(1)}, bf16[224,256]{1,0:T(8,128)(2,1)S(1)}, u32[]{:S(2)}, u32[]{:S(2)}) collective-permute-start(bf16[224,256]{1,0:T(8,128)(2,1)S(1)} %mlp.6), channel_id=1, source_target_pairs={{0,12},{4,8},{8,4},{12,0},{1,13},{5,9},{9,5},{13,1},{2,14},{6,10},... | collective-permute-start | bytes 344072 | tf_op jit(solution)/shard_map/ppermute | solution.py:453

commit v7 on v6

--- a/solution.py
+++ b/solution.py
@@ -218,7 +218,7 @@
             mix[pl.ds(start, head_dim), :] = mixed.astype(jnp.bfloat16)
         return 0
 
-    lax.fori_loop(0, HEADS, one_head, 0)
+    lax.fori_loop(0, HEADS, one_head, 0, unroll=4)
 
 
 def time_part(projs, asked, streams, mixes, time_out_ref, results):
@@ -283,13 +283,19 @@
     )
 
 
+def gelu(x):
+    half = 0.5 * x
+    scale = (2 / 3.141592653589793) ** 0.5
+    return half + half * jnp.tanh(x * (scale + (scale * 0.044715) * (x * x)))
+
+
 def mlp_kernel(pieces, *refs):
     gains_ref, in_ref, out_ref, result_ref = refs[pieces:]
     first = 0
     for ref in refs[:pieces]:
         stream = ref[...]
         normed = layer_norm(stream, gains_ref[2:3, :])
-        inner = jax.nn.gelu(dot(normed, in_ref[...]), approximate=True).astype(jnp.bfloat16)
+        inner = gelu(dot(normed, in_ref[...])).astype(jnp.bfloat16)
         result_ref[first : first + stream.shape[0], :] = (
             stream.astype(jnp.float32) + dot(inner, out_ref[...])
         ).astype(jnp.bfloat16)

time: 78.4 us -> 78 us (level)
  no operation moved by 1% of the time
where the time goes in v7:
time: 78 us; the launch traced here: 77.9 us
  Pallas kernels  30.3 us (39%)
  waiting for transfers between devices  27.3 us (35%)
  starting transfers between devices  19.8 us (25%)
    ppermute x8, waiting for transfers between devices, frame_swapped(): lax.ppermute(value, 'frame', [(i, i ^ distance) for i in range(count)])  26.2 us
    ppermute x8, starting transfers between devices, frame_swapped(): lax.ppermute(value, 'frame', [(i, i ^ distance) for i in range(count)])  19.3 us
    pallas_call x3, Pallas kernels, attend_row(): pl.pallas_call(row_kernel, out_shape=(array(length, channels), array(3 *...  10.7 us
    pallas_call x6, Pallas kernels, mlp(): pl.pallas_call(functools.partial(mlp_kernel, len(pieces)), out_shape=arra...  5.18 us
    pallas_call x1, Pallas kernels, finish_rest(): pl.pallas_call(functools.partial(finish_rest_kernel, frames), out_shape=[...  5.06 us
    pallas_call x1, Pallas kernels, finish_head(): pl.pallas_call(functools.partial(finish_head_kernel, frames), out_shape=[...  4.1 us
    pallas_call x2, Pallas kernels, take_rows(): pl.pallas_call(functools.partial(take_kernel, distances), out_shape=[arra...  2.17 us
    pallas_call x2, Pallas kernels, place_rows(): pl.pallas_call(functools.partial(place_kernel, places), out_shape=array(*...  1.6 us
  transfers between devices with their start and end apart: 12, of which 6 were waited for; matrix products, arithmetic and copies ran while one was open for 0% of the time, Pallas kernels for 23%

profile of v7, /device:TPU:0, one launch (start us, length us, event | category | flops | bytes accessed | tf_op | source)
XLA Modules:
  0.0 77.9 jit_solution(2942424353496189834)
XLA Ops:
  0.0 1.1 %take_rows.2 = (bf16[480,256]{1,0:T(8,128)(2,1)S(1)}, bf16[480,256]{1,0:T(8,128)(2,1)S(1)}) custom-call(s32[1]{0:T(128)} %bitcast.here_ref, bf16[4,480,256]{2,1,0:T(8,128)(2,1)} %bitcast.3), custom_call_target="tpu_custom_call" | custom-call | tf_op jit(solution)/shard_map/take_rows/pallas_call | solution.py:400
  1.1 0.0 copy-start
  1.1 0.6 collective-permute-start.3
  1.7 0.0 copy-start.6
  1.7 1.1 %take_rows.3 = (bf16[480,256]{1,0:T(8,128)(2,1)S(1)}, bf16[480,256]{1,0:T(8,128)(2,1)S(1)}) custom-call(s32[1]{0:T(128)} %bitcast.here_ref, bf16[4,480,256]{2,1,0:T(8,128)(2,1)} %bitcast.4), custom_call_target="tpu_custom_call" | custom-call | tf_op jit(solution)/shard_map/take_rows/pallas_call | solution.py:400
  2.8 0.0 copy-start.3
  2.8 0.0 copy-start.4
  2.8 2.7 %collective-permute-start.2 = (bf16[480,256]{1,0:T(8,128)(2,1)S(1)}, bf16[480,256]{1,0:T(8,128)(2,1)S(1)}, u32[]{:S(2)}, u32[]{:S(2)}) collective-permute-start(bf16[480,256]{1,0:T(8,128)(2,1)S(1)} %get-tuple-element.34), channel_id=1, source_target_pairs={{0,4},{4,0},{8,12},{12,8},{1,5},{5,1},{9,13},{13,9},{2,6},{6,2},{1... | collective-permute-start | bytes 737288 | tf_op jit(solution)/shard_map/ppermute | solution.py:459
  5.5 0.0 copy-done
  5.5 0.0 copy-done.6
  5.5 0.4 row_queries.4.queries_ref
  5.8 0.0 collective-permute-done.3.other_ref
  5.8 0.0 copy-done.3
  5.9 0.0 copy-done.4
  5.9 3.6 %attend_row.3 = (bf16[480,256]{1,0:T(8,128)(2,1)S(1)}, bf16[768,480]{1,0:T(8,128)(2,1)S(1)}) custom-call(bf16[480,256]{1,0:T(8,128)(2,1)S(1)} %get-tuple-element.35.own_ref, bf16[480,256]{1,0:T(8,128)(2,1)S(1)} %collective-permute-done.3.other_ref, bf16[480,256]{1,0:T(8,128)(2,1)S(1)} %row_queries.4.queries_ref, f32[3,256]{1,0:T(4,128)S(1)} %copy-done.6, ...), custom_call_target="tpu_custom_call" | custom-call | flops 2327838720 | bytes 2392064 | tf_op jit(solution)/shard_map/attend_row/pallas_call | solution.py:311
  9.4 2.6 %collective-permute-done.2.own_ref = bf16[480,256]{1,0:T(8,128)(2,1)S(1)} collective-permute-done((bf16[480,256]{1,0:T(8,128)(2,1)S(1)}, bf16[480,256]{1,0:T(8,128)(2,1)S(1)}, u32[]{:S(2)}, u32[]{:S(2)}) %collective-permute-start.2) | collective-permute-done | bytes 245792 | tf_op jit(solution)/shard_map/ppermute | solution.py:459
  12.0 0.0 collective-permute-start.4
  12.0 2.8 %collective-permute-start.1 = (bf16[480,256]{1,0:T(8,128)(2,1)S(1)}, bf16[480,256]{1,0:T(8,128)(2,1)S(1)}, u32[]{:S(2)}, u32[]{:S(2)}) collective-permute-start(bf16[480,256]{1,0:T(8,128)(2,1)S(1)} %get-tuple-element.33), channel_id=1, source_target_pairs={{0,8},{4,12},{8,0},{12,4},{1,9},{5,13},{9,1},{13,5},{2,10},{6,14},... | collective-permute-start | bytes 737288 | tf_op jit(solution)/shard_map/ppermute | solution.py:459
  14.8 0.4 row_queries.5.queries_ref
  15.2 0.0 collective-permute-done.4.other_ref
  15.2 3.6 %attend_row.4 = (bf16[480,256]{1,0:T(8,128)(2,1)S(1)}, bf16[768,480]{1,0:T(8,128)(2,1)S(1)}) custom-call(bf16[480,256]{1,0:T(8,128)(2,1)S(1)} %collective-permute-done.2.own_ref, bf16[480,256]{1,0:T(8,128)(2,1)S(1)} %collective-permute-done.4.other_ref, bf16[480,256]{1,0:T(8,128)(2,1)S(1)} %row_queries.5.queries_ref, f32[3,256]{1,0:T(4,128)S(1)} %copy-done.6, ...), custom_call_target="tpu_custom_call" | custom-call | flops 2327838720 | bytes 2392064 | tf_op jit(solution)/shard_map/attend_row/pallas_call | solution.py:311
  18.8 7.9 %collective-permute-done.1.own_ref = bf16[480,256]{1,0:T(8,128)(2,1)S(1)} collective-permute-done((bf16[480,256]{1,0:T(8,128)(2,1)S(1)}, bf16[480,256]{1,0:T(8,128)(2,1)S(1)}, u32[]{:S(2)}, u32[]{:S(2)}) %collective-permute-start.1) | collective-permute-done | bytes 245792 | tf_op jit(solution)/shard_map/ppermute | solution.py:459
  26.7 0.0 collective-permute-start.5
  26.7 3.6 %collective-permute-start = (bf16[480,256]{1,0:T(8,128)(2,1)S(1)}, bf16[480,256]{1,0:T(8,128)(2,1)S(1)}, u32[]{:S(2)}, u32[]{:S(2)}) collective-permute-start(bf16[480,256]{1,0:T(8,128)(2,1)S(1)} %get-tuple-element.32), channel_id=1, source_target_pairs={{0,12},{4,8},{8,4},{12,0},{1,13},{5,9},{9,5},{13,1},{2,14},{6,10},... | collective-permute-start | bytes 737288 | tf_op jit(solution)/shard_map/ppermute | solution.py:459
  30.3 0.4 row_queries.6.queries_ref
  30.7 0.0 collective-permute-done.5.other_ref
  30.7 3.6 %attend_row.5 = (bf16[480,256]{1,0:T(8,128)(2,1)S(1)}, bf16[768,480]{1,0:T(8,128)(2,1)S(1)}) custom-call(bf16[480,256]{1,0:T(8,128)(2,1)S(1)} %collective-permute-done.1.own_ref, bf16[480,256]{1,0:T(8,128)(2,1)S(1)} %collective-permute-done.5.other_ref, bf16[480,256]{1,0:T(8,128)(2,1)S(1)} %row_queries.6.queries_ref, f32[3,256]{1,0:T(4,128)S(1)} %copy-done.6, ...), custom_call_target="tpu_custom_call" | custom-call | flops 2327838720 | bytes 2392064 | tf_op jit(solution)/shard_map/attend_row/pallas_call | solution.py:311
  34.3 2.7 %collective-permute-done.own_ref = bf16[480,256]{1,0:T(8,128)(2,1)S(1)} collective-permute-done((bf16[480,256]{1,0:T(8,128)(2,1)S(1)}, bf16[480,256]{1,0:T(8,128)(2,1)S(1)}, u32[]{:S(2)}, u32[]{:S(2)}) %collective-permute-start) | collective-permute-done | bytes 245792 | tf_op jit(solution)/shard_map/ppermute | solution.py:459
  37.0 0.0 copy-start.5
  37.0 0.0 collective-permute-start.6
  37.0 0.4 row_queries.7.queries_ref
  37.3 1.1 %collective-permute-done.6.other_ref = bf16[480,256]{1,0:T(8,128)(2,1)S(1)} collective-permute-done((bf16[480,256]{1,0:T(8,128)(2,1)S(1)}, bf16[480,256]{1,0:T(8,128)(2,1)S(1)}, u32[]{:S(2)}, u32[]{:S(2)}) %collective-permute-start.6) | collective-permute-done | bytes 245792 | tf_op jit(solution)/shard_map/ppermute | solution.py:18
  38.5 0.0 copy-done.5
  38.5 4.1 %finish_head.1 = (bf16[256,256]{1,0:T(8,128)(2,1)S(1)}, bf16[256,256]{1,0:T(8,128)(2,1)S(1)}, bf16[480,256]{1,0:T(8,128)(2,1)S(1)}, bf16[256,480]{1,0:T(8,128)(2,1)S(1)}, bf16[768,256]{1,0:T(8,128)(2,1)S(1)}) custom-call(bf16[480,256]{1,0:T(8,128)(2,1)S(1)} %collective-permute-done.own_ref, bf16[480,256]{1,0:T(8,128)(2,1)S(1)} %collective-permute-done.6.other_ref, ...), custom_call_target="tpu_custom_call" | custom-call | flops 1195376640 | bytes 5242880 | tf_op jit(solution)/shard_map/finish_head/pallas_call | solution.py:355
  42.6 0.0 copy-start.1
  42.6 0.0 copy-start.2
  42.6 5.1 %finish_rest.1 = (bf16[224,256]{1,0:T(8,128)(2,1)S(1)}, bf16[224,256]{1,0:T(8,128)(2,1)S(1)}, bf16[224,256]{1,0:T(8,128)(2,1)S(1)}, bf16[224,256]{1,0:T(8,128)(2...) custom-call(bf16[480,256]{1,0:T(8,128)(2,1)S(1)} %collective-permute-done.own_ref, ...), custom_call_target="tpu_custom_call" | custom-call | flops 1069547520 | bytes 4718592 | tf_op jit(solution)/shard_map/finish_rest/pallas_call | solution.py:373
  47.7 0.0 copy-done.1
  47.7 0.0 copy-done.2
  47.7 1.1 %mlp.8 = bf16[480,256]{1,0:T(8,128)(2,1)S(1)} custom-call(bf16[256,256]{1,0:T(8,128)(2,1)S(1)} %get-tuple-element.53.refs_0_, bf16[224,256]{1,0:T(8,128)(2,1)S(1)} %get-tuple-element.54.refs_1_, f32[3,256]{1,0:T(4,128)S(1)} %copy-done.6, bf16[256,1024]{1,0:T(8,128)(2,1)S(1)} %copy-done.1, bf16[1024,256]{1,0:T(8,128)(2,1)S(1)} %copy-done.2), custom_call_target="tpu_custom_call" | custom-call | flops 503316480 | bytes 1540096 | tf_op jit(solution)/shard_map/mlp/pallas_call | solution.py:444
  48.8 4.2 %collective-permute-start.9 = (bf16[480,256]{1,0:T(8,128)(2,1)S(1)}, bf16[480,256]{1,0:T(8,128)(2,1)S(1)}, u32[]{:S(2)}, u32[]{:S(2)}) collective-permute-start(bf16[480,256]{1,0:T(8,128)(2,1)S(1)} %mlp.8), channel_id=1, source_target_pairs={{0,4},{4,0},{8,12},{12,8},{1,5},{5,1},{9,13},{13,9},{2,6},{6,2},{1... | collective-permute-start | bytes 737288 | tf_op jit(solution)/shard_map/ppermute | solution.py:459
  53.0 0.7 mlp.11
  53.8 0.1 collective-permute-start.11
  53.8 0.7 mlp.10
  54.6 2.4 %collective-permute-start.10 = (bf16[256,256]{1,0:T(8,128)(2,1)S(1)}, bf16[256,256]{1,0:T(8,128)(2,1)S(1)}, u32[]{:S(2)}, u32[]{:S(2)}) collective-permute-start(bf16[256,256]{1,0:T(8,128)(2,1)S(1)} %mlp.10), channel_id=1, source_target_pairs={{0,12},{4,8},{8,4},{12,0},{1,13},{5,9},{9,5},{13,1},{2,14},{6,10},... | collective-permute-start | bytes 393224 | tf_op jit(solution)/shard_map/ppermute | solution.py:459
  57.0 0.7 mlp.6
  57.7 0.7 mlp.7
  58.4 0.9 %collective-permute-start.8 = (bf16[224,256]{1,0:T(8,128)(2,1)S(1)}, bf16[224,256]{1,0:T(8,128)(2,1)S(1)}, u32[]{:S(2)}, u32[]{:S(2)}) collective-permute-start(bf16[224,256]{1,0:T(8,128)(2,1)S(1)} %mlp.7), channel_id=1, source_target_pairs={{0,8},{4,12},{8,0},{12,4},{1,9},{5,13},{9,1},{13,5},{2,10},{6,14},... | collective-permute-start | bytes 344072 | tf_op jit(solution)/shard_map/ppermute | solution.py:459
  59.3 2.6 %collective-permute-start.7 = (bf16[224,256]{1,0:T(8,128)(2,1)S(1)}, bf16[224,256]{1,0:T(8,128)(2,1)S(1)}, u32[]{:S(2)}, u32[]{:S(2)}) collective-permute-start(bf16[224,256]{1,0:T(8,128)(2,1)S(1)} %mlp.6), channel_id=1, source_target_pairs={{0,12},{4,8},{8,4},{12,0},{1,13},{5,9},{9,5},{13,1},{2,14},{6,10},... | collective-permute-start | bytes 344072 | tf_op jit(solution)/shard_map/ppermute | solution.py:459
  62.0 1.1 %mlp.9.refs_0_ = bf16[480,256]{1,0:T(8,128)(2,1)S(1)} custom-call(bf16[256,256]{1,0:T(8,128)(2,1)S(1)} %get-tuple-element.55.refs_0_, bf16[224,256]{1,0:T(8,128)(2,1)S(1)} %get-tuple-element.56.refs_1_, f32[3,256]{1,0:T(4,128)S(1)} %copy-done.6, bf16[256,1024]{1,0:T(8,128)(2,1)S(1)} %copy-done.1, bf16[1024,256]{1,0:T(8,128)(2,1)S(1)} %copy-done.2), custom_call_target="tpu_custom_call" | custom-call | flops 503316480 | bytes 1540096 | tf_op jit(solution)/shard_map/mlp/pallas_call | solution.py:444
  63.1 8.5 %collective-permute-done.11.refs_2_ = bf16[256,256]{1,0:T(8,128)(2,1)S(1)} collective-permute-done((bf16[256,256]{1,0:T(8,128)(2,1)S(1)}, bf16[256,256]{1,0:T(8,128)(2,1)S(1)}, u32[]{:S(2)}, u32[]{:S(2)}) %collective-permute-start.11) | collective-permute-done | bytes 131104 | tf_op jit(solution)/shard_map/ppermute | solution.py:459
  71.6 0.0 collective-permute-done.10.refs_1_
  71.6 0.8 %place_rows.2.refs_3_ = bf16[4,480,256]{2,1,0:T(8,128)(2,1)} custom-call(s32[1]{0:T(128)} %bitcast.here_ref, bf16[480,256]{1,0:T(8,128)(2,1)S(1)} %mlp.9.refs_0_, bf16[256,256]{1,0:T(8,128)(2,1)S(1)} %collective-permute-done.10.refs_1_, bf16[256,256]{1,0:T(8,128)(2,1)S(1)} %collective-permute-done.11.refs_2_), custom_call_target="tpu_custom_call" | custom-call | tf_op jit(solution)/shard_map/place_rows/pallas_call | solution.py:429
  72.4 4.5 %collective-permute-done.8.refs_1_ = bf16[224,256]{1,0:T(8,128)(2,1)S(1)} collective-permute-done((bf16[224,256]{1,0:T(8,128)(2,1)S(1)}, bf16[224,256]{1,0:T(8,128)(2,1)S(1)}, u32[]{:S(2)}, u32[]{:S(2)}) %collective-permute-start.8) | collective-permute-done | bytes 114720 | tf_op jit(solution)/shard_map/ppermute | solution.py:459
  76.9 0.0 collective-permute-done.7.refs_0_
  76.9 0.0 collective-permute-done.9.refs_2_
  76.9 0.8 %place_rows.3 = bf16[4,480,256]{2,1,0:T(8,128)(2,1)} custom-call(s32[1]{0:T(128)} %bitcast.here_ref, bf16[224,256]{1,0:T(8,128)(2,1)S(1)} %collective-permute-done.7.refs_0_, bf16[224,256]{1,0:T(8,128)(2,1)S(1)} %collective-permute-done.8.refs_1_, bf16[480,256]{1,0:T(8,128)(2,1)S(1)} %collective-permute-done.9.refs_2_, ...), custom_call_target="tpu_custom_call", output_to_operand_aliasing={{}: (4, {})} | custom-call | tf_op jit(solution)/shard_map/place_rows/pallas_call | solution.py:429
Async XLA Ops:
  1.1 4.4 %copy-start = (bf16[256,768]{1,0:T(8,128)(2,1)S(1)}, bf16[256,768]{1,0:T(8,128)(2,1)}, u32[]{:S(2)}) copy-start(bf16[256,768]{1,0:T(8,128)(2,1)} %qkv_ref.15) | copy-start | bytes 1179652
  1.1 4.7 %collective-permute-start.3 = (bf16[480,256]{1,0:T(8,128)(2,1)S(1)}, bf16[480,256]{1,0:T(8,128)(2,1)S(1)}, u32[]{:S(2)}, u32[]{:S(2)}) collective-permute-start(bf16[480,256]{1,0:T(8,128)(2,1)S(1)} %get-tuple-element.35.own_ref), channel_id=1, source_target_pairs={{0,1},{1,0},{2,3},{3,2},{4,5},{5,4},{6,7},{7,6},{8,9},{9,8},{10,11... | collective-permute-start | bytes 737288 | tf_op jit(solution)/shard_map/ppermute | solution.py:18
  1.7 3.8 %copy-start.6 = (f32[3,256]{1,0:T(4,128)S(1)}, f32[3,256]{1,0:T(4,128)}, u32[]{:S(2)}) copy-start(f32[3,256]{1,0:T(4,128)} %refs_1_.7) | copy-start | bytes 9220
  2.8 3.1 %copy-start.3 = (bf16[256,768]{1,0:T(8,128)(2,1)S(1)}, bf16[256,768]{1,0:T(8,128)(2,1)}, u32[]{:S(2)}) copy-start(bf16[256,768]{1,0:T(8,128)(2,1)} %time_ref.9) | copy-start | bytes 1179652
  2.8 3.1 %copy-start.4 = (bf16[256,256]{1,0:T(8,128)(2,1)S(1)}, bf16[256,256]{1,0:T(8,128)(2,1)}, u32[]{:S(2)}) copy-start(bf16[256,256]{1,0:T(8,128)(2,1)} %out_ref.9) | copy-start | bytes 393220
  2.8 9.3 %collective-permute-start.2 = (bf16[480,256]{1,0:T(8,128)(2,1)S(1)}, bf16[480,256]{1,0:T(8,128)(2,1)S(1)}, u32[]{:S(2)}, u32[]{:S(2)}) collective-permute-start(bf16[480,256]{1,0:T(8,128)(2,1)S(1)} %get-tuple-element.34), channel_id=1, source_target_pairs={{0,4},{4,0},{8,12},{12,8},{1,5},{5,1},{9,13},{13,9},{2,6},{6,2},{1... | collective-permute-start | bytes 737288 | tf_op jit(solution)/shard_map/ppermute | solution.py:459
  12.0 3.1 %collective-permute-start.4 = (bf16[480,256]{1,0:T(8,128)(2,1)S(1)}, bf16[480,256]{1,0:T(8,128)(2,1)S(1)}, u32[]{:S(2)}, u32[]{:S(2)}) collective-permute-start(bf16[480,256]{1,0:T(8,128)(2,1)S(1)} %collective-permute-done.2.own_ref), channel_id=1, source_target_pairs={{0,1},{1,0},{2,3},{3,2},{4,5},{5,4},{6,7},{7,6},{8,9},{9,8},{10,11... | collective-permute-start | bytes 737288 | tf_op jit(solution)/shard_map/ppermute | solution.py:18
  12.0 14.6 %collective-permute-start.1 = (bf16[480,256]{1,0:T(8,128)(2,1)S(1)}, bf16[480,256]{1,0:T(8,128)(2,1)S(1)}, u32[]{:S(2)}, u32[]{:S(2)}) collective-permute-start(bf16[480,256]{1,0:T(8,128)(2,1)S(1)} %get-tuple-element.33), channel_id=1, source_target_pairs={{0,8},{4,12},{8,0},{12,4},{1,9},{5,13},{9,1},{13,5},{2,10},{6,14},... | collective-permute-start | bytes 737288 | tf_op jit(solution)/shard_map/ppermute | solution.py:459
  26.7 4.0 %collective-permute-start.5 = (bf16[480,256]{1,0:T(8,128)(2,1)S(1)}, bf16[480,256]{1,0:T(8,128)(2,1)S(1)}, u32[]{:S(2)}, u32[]{:S(2)}) collective-permute-start(bf16[480,256]{1,0:T(8,128)(2,1)S(1)} %collective-permute-done.1.own_ref), channel_id=1, source_target_pairs={{0,1},{1,0},{2,3},{3,2},{4,5},{5,4},{6,7},{7,6},{8,9},{9,8},{10,11... | collective-permute-start | bytes 737288 | tf_op jit(solution)/shard_map/ppermute | solution.py:18
  26.7 10.3 %collective-permute-start = (bf16[480,256]{1,0:T(8,128)(2,1)S(1)}, bf16[480,256]{1,0:T(8,128)(2,1)S(1)}, u32[]{:S(2)}, u32[]{:S(2)}) collective-permute-start(bf16[480,256]{1,0:T(8,128)(2,1)S(1)} %get-tuple-element.32), channel_id=1, source_target_pairs={{0,12},{4,8},{8,4},{12,0},{1,13},{5,9},{9,5},{13,1},{2,14},{6,10},... | collective-permute-start | bytes 737288 | tf_op jit(solution)/shard_map/ppermute | solution.py:459
  37.0 1.5 %copy-start.5 = (bf16[256,256]{1,0:T(8,128)(2,1)S(1)}, bf16[256,256]{1,0:T(8,128)(2,1)}, u32[]{:S(2)}) copy-start(bf16[256,256]{1,0:T(8,128)(2,1)} %time_out_ref.3) | copy-start | bytes 393220
  37.0 1.5 %collective-permute-start.6 = (bf16[480,256]{1,0:T(8,128)(2,1)S(1)}, bf16[480,256]{1,0:T(8,128)(2,1)S(1)}, u32[]{:S(2)}, u32[]{:S(2)}) collective-permute-start(bf16[480,256]{1,0:T(8,128)(2,1)S(1)} %collective-permute-done.own_ref), channel_id=1, source_target_pairs={{0,1},{1,0},{2,3},{3,2},{4,5},{5,4},{6,7},{7,6},{8,9},{9,8},{10,11... | collective-permute-start | bytes 737288 | tf_op jit(solution)/shard_map/ppermute | solution.py:18
  42.6 5.1 %copy-start.1 = (bf16[256,1024]{1,0:T(8,128)(2,1)S(1)}, bf16[256,1024]{1,0:T(8,128)(2,1)}, u32[]{:S(2)}) copy-start(bf16[256,1024]{1,0:T(8,128)(2,1)} %refs_2_.11) | copy-start | bytes 1572868
  42.6 5.1 %copy-start.2 = (bf16[1024,256]{1,0:T(8,128)(2,1)S(1)}, bf16[1024,256]{1,0:T(8,128)(2,1)}, u32[]{:S(2)}) copy-start(bf16[1024,256]{1,0:T(8,128)(2,1)} %refs_3_.11) | copy-start | bytes 1572868
  48.8 28.1 %collective-permute-start.9 = (bf16[480,256]{1,0:T(8,128)(2,1)S(1)}, bf16[480,256]{1,0:T(8,128)(2,1)S(1)}, u32[]{:S(2)}, u32[]{:S(2)}) collective-permute-start(bf16[480,256]{1,0:T(8,128)(2,1)S(1)} %mlp.8), channel_id=1, source_target_pairs={{0,4},{4,0},{8,12},{12,8},{1,5},{5,1},{9,13},{13,9},{2,6},{6,2},{1... | collective-permute-start | bytes 737288 | tf_op jit(solution)/shard_map/ppermute | solution.py:459
  53.8 17.9 %collective-permute-start.11 = (bf16[256,256]{1,0:T(8,128)(2,1)S(1)}, bf16[256,256]{1,0:T(8,128)(2,1)S(1)}, u32[]{:S(2)}, u32[]{:S(2)}) collective-permute-start(bf16[256,256]{1,0:T(8,128)(2,1)S(1)} %mlp.11), channel_id=1, source_target_pairs={{0,8},{4,12},{8,0},{12,4},{1,9},{5,13},{9,1},{13,5},{2,10},{6,14},... | collective-permute-start | bytes 393224 | tf_op jit(solution)/shard_map/ppermute | solution.py:459
  54.6 17.0 %collective-permute-start.10 = (bf16[256,256]{1,0:T(8,128)(2,1)S(1)}, bf16[256,256]{1,0:T(8,128)(2,1)S(1)}, u32[]{:S(2)}, u32[]{:S(2)}) collective-permute-start(bf16[256,256]{1,0:T(8,128)(2,1)S(1)} %mlp.10), channel_id=1, source_target_pairs={{0,12},{4,8},{8,4},{12,0},{1,13},{5,9},{9,5},{13,1},{2,14},{6,10},... | collective-permute-start | bytes 393224 | tf_op jit(solution)/shard_map/ppermute | solution.py:459
  58.4 18.5 %collective-permute-start.8 = (bf16[224,256]{1,0:T(8,128)(2,1)S(1)}, bf16[224,256]{1,0:T(8,128)(2,1)S(1)}, u32[]{:S(2)}, u32[]{:S(2)}) collective-permute-start(bf16[224,256]{1,0:T(8,128)(2,1)S(1)} %mlp.7), channel_id=1, source_target_pairs={{0,8},{4,12},{8,0},{12,4},{1,9},{5,13},{9,1},{13,5},{2,10},{6,14},... | collective-permute-start | bytes 344072 | tf_op jit(solution)/shard_map/ppermute | solution.py:459
  59.3 17.6 %collective-permute-start.7 = (bf16[224,256]{1,0:T(8,128)(2,1)S(1)}, bf16[224,256]{1,0:T(8,128)(2,1)S(1)}, u32[]{:S(2)}, u32[]{:S(2)}) collective-permute-start(bf16[224,256]{1,0:T(8,128)(2,1)S(1)} %mlp.6), channel_id=1, source_target_pairs={{0,12},{4,8},{8,4},{12,0},{1,13},{5,9},{9,5},{13,1},{2,14},{6,10},... | collective-permute-start | bytes 344072 | tf_op jit(solution)/shard_map/ppermute | solution.py:459
